TPU v7x, 32 devices: a whole 2x2x4 slice. The times are simulated.
32 devices in a mesh: dp: 8 (over y, x, core), tensor: 4 (over z).
Axes of the slice: x: 2, y: 2, z: 4, core: 2. Of those that a mesh axis runs over, the one named last changes fastest.
Arguments:
- inputs: bfloat16 [8, 1024, 2048], P('dp'), may hold values from -6 to 6
- segments: int32 [8, 1024], P('dp'), may hold values from 0 to 3, never falling along the last dimension, each value on 1 to 512 neighbouring positions
- cotangent: bfloat16 [8, 1024, 2048], P('dp'), may hold values from -6 to 6
- w_query: bfloat16 [2048, 2048], P(None, 'tensor'), may hold values from -0.046875 to 0.046875
- w_key: bfloat16 [2048, 2048], P(None, 'tensor'), may hold values from -0.046875 to 0.046875
- w_value: bfloat16 [2048, 2048], P(None, 'tensor'), may hold values from -0.125 to 0.125
- w_out: bfloat16 [2048, 2048], P('tensor'), may hold values from -0.5 to 0.5
- w_gate: bfloat16 [2048, 5120], P(None, 'tensor'), may hold values from -0.125 to 0.125
- w_up: bfloat16 [2048, 5120], P(None, 'tensor'), may hold values from -0.125 to 0.125
- w_down: bfloat16 [5120, 2048], P('tensor'), may hold values from -0.125 to 0.125
- gain_attn: float32 [2048], replicated, may hold values from 0.5 to 1.5
- gain_ffn: float32 [2048], replicated, may hold values from 0.5 to 1.5
- bias_table: float32 [32, 32], P(None, 'tensor'), may hold values from -4 to 4
Outputs:
- output: bfloat16 [8, 1024, 2048], P('dp', 'tensor')
- input_grad: bfloat16 [8, 1024, 2048], P('dp', 'tensor')
- query_grad: float32 [2048, 2048], P(None, 'tensor')
- key_grad: float32 [2048, 2048], P(None, 'tensor')
- value_grad: float32 [2048, 2048], P(None, 'tensor')
- out_grad: float32 [2048, 2048], P('tensor')
- gate_grad: float32 [2048, 5120], P(None, 'tensor')
- up_grad: float32 [2048, 5120], P(None, 'tensor')
- down_grad: float32 [5120, 2048], P('tensor')
- gain_attn_grad: float32 [2048], replicated
- gain_ffn_grad: float32 [2048], replicated
- table_grad: float32 [32, 32], P(None, 'tensor')
Inputs may be any that keep to these rules, and one draw needn't show every extreme that they name: `segments`: each row of 1024 tokens holds 4 documents one after another; document numbers never fall along a row; each document has 1 to 512 tokens and one in every row has exactly 512.
All inputs are finite; a program needn't handle non-finite values.
Results may differ from a plain program's by a relative error of at most 0.024.
Values may be sent and summed in bfloat16 or wider, within the bound.
A program may use at most 320 MiB of HBM per device.

v0:
```python
import jax
import jax.numpy as jnp
from jax import lax
from jax.sharding import PartitionSpec as P

thresholds = (12, 16, 23, 32, 46, 64, 91)
highest = lax.Precision.HIGHEST


def buckets_of(start_row, query_count, length):
    queries = start_row + jnp.arange(query_count, dtype=jnp.int32)
    targets = jnp.arange(length, dtype=jnp.int32)
    offset = targets[None, :] - queries[:, None]
    distance = jnp.abs(offset)
    far_bucket = jnp.full(distance.shape, 8, jnp.int32)
    for bound_value in thresholds:
        far_bucket = far_bucket + (distance >= bound_value).astype(jnp.int32)
    near_bucket = jnp.where(distance < 8, distance, far_bucket)
    return near_bucket + 16 * (offset > 0).astype(jnp.int32)


def bucket_onehot(start_row, query_count, length, bucket_count):
    bucket = buckets_of(start_row, query_count, length).reshape(1, query_count * length)
    labels = jnp.arange(bucket_count, dtype=jnp.int32)[:, None]
    return (bucket == labels).astype(jnp.float32)


def project(left_side, right_side):
    return jnp.dot(left_side, right_side, preferred_element_type=jnp.float32)


def project_back(left_side, right_side):
    return lax.dot_general(
        left_side, right_side, (((1,), (1,)), ((), ())), preferred_element_type=jnp.float32
    )


def weight_term(left_side, right_side):
    return lax.dot_general(
        left_side, right_side, (((0,), (0,)), ((), ())), preferred_element_type=jnp.float32
    )


def norm_scale(signal):
    return lax.rsqrt(jnp.mean(signal * signal, axis=-1, keepdims=True) + 1e-06)


def norm_back(signal, rms_scale, gain_vec, grad_normed):
    grad_hat = grad_normed * gain_vec
    inner_mean = jnp.mean(grad_hat * signal, axis=-1, keepdims=True)
    return rms_scale * (grad_hat - signal * rms_scale * rms_scale * inner_mean)


def gain_term(signal, rms_scale, grad_normed):
    return jnp.sum((grad_normed * signal * rms_scale).reshape(-1, signal.shape[-1]), axis=0)


def score_block(query_block, key_row, bias_block, same_doc):
    raw_scores = jnp.einsum(
        "qhd,khd->hqk", query_block, key_row, preferred_element_type=jnp.float32
    )
    return jnp.where(same_doc[None], raw_scores + bias_block, -1000000000.0)


def shards(
    inputs,
    segments,
    cotangent,
    w_query,
    w_key,
    w_value,
    w_out,
    w_gate,
    w_up,
    w_down,
    gain_attn,
    gain_ffn,
    bias_table,
):
    row_count, length, model_width = inputs.shape
    share_rows = length // lax.axis_size("tensor")
    first_row = lax.axis_index("tensor") * share_rows
    bucket_count, head_count = bias_table.shape
    local_width = w_query.shape[1]
    head_dim = local_width // head_count
    block_rows = min(512, length)
    block_count = length // block_rows
    token_count = row_count * length
    plane = (row_count, length, model_width)

    def take_share(signal):
        return lax.dynamic_slice_in_dim(signal, first_row, share_rows, 1)

    flat_inputs = inputs.reshape(token_count, model_width).astype(jnp.float32)
    scale_attn = norm_scale(flat_inputs)
    normed = (flat_inputs * scale_attn * gain_attn).astype(jnp.bfloat16)
    heads_shape = (row_count, length, head_count, head_dim)
    queries = project(normed, w_query).astype(jnp.bfloat16).reshape(heads_shape)
    key_proj = project(normed, w_key).astype(jnp.bfloat16).reshape(heads_shape)
    value_proj = project(normed, w_value).astype(jnp.bfloat16).reshape(heads_shape)
    table_heads = jnp.transpose(bias_table)
    bias_blocks = []
    for block_index in range(block_count):
        onehot = bucket_onehot(block_index * block_rows, block_rows, length, bucket_count)
        bias_flat = jnp.dot(table_heads, onehot, precision=highest)
        bias_blocks.append(bias_flat.reshape(head_count, block_rows, length))
    row_index = 0
    doc_row = segments[row_index]
    pieces = []
    totals_row = []
    for block_index in range(block_count):
        block_start = block_index * block_rows
        same_doc = doc_row[block_start : block_start + block_rows, None] == doc_row[None, :]
        query_block = queries[row_index, block_start : block_start + block_rows]
        scores = score_block(query_block, key_proj[row_index], bias_blocks[block_index], same_doc)
        row_max = jnp.max(scores, axis=-1, keepdims=True)
        weighted = jnp.exp(scores - row_max)
        row_total = jnp.sum(weighted, axis=-1, keepdims=True)
        softmaxed = (weighted / row_total).astype(jnp.bfloat16)
        totals_row.append(row_max + jnp.log(row_total))
        pieces.append(
            jnp.einsum(
                "hqk,khd->qhd", softmaxed, value_proj[row_index], preferred_element_type=jnp.float32
            ).astype(jnp.bfloat16)
        )
    log_totals = [totals_row]
    mixed_rows = [jnp.concatenate(pieces, axis=0)]
    mixed_heads = jnp.stack(mixed_rows).reshape(token_count, local_width)
    attn_part = project(mixed_heads, w_out)
    attn_total = lax.psum(attn_part.astype(jnp.bfloat16), "tensor").astype(jnp.float32)
    middle = flat_inputs + attn_total
    scale_ffn = norm_scale(middle)
    normed_ffn = (middle * scale_ffn * gain_ffn).astype(jnp.bfloat16)
    gate_pre = project(normed_ffn, w_gate)
    up_pre = project(normed_ffn, w_up)
    hidden = (jax.nn.gelu(gate_pre, approximate=True) * up_pre).astype(jnp.bfloat16)
    ffn_part = project(hidden, w_down)
    ffn_total = lax.psum(ffn_part.astype(jnp.bfloat16), "tensor").astype(jnp.float32)
    output = take_share((middle + ffn_total).reshape(plane)).astype(jnp.bfloat16)
    grad_out = cotangent.reshape(token_count, model_width)
    down_grad = weight_term(hidden, grad_out)
    grad_hidden = project_back(grad_out, w_down)
    normed_again = lax.optimization_barrier(normed_ffn)
    gate_back = project(normed_again, w_gate)
    up_back = project(normed_again, w_up)
    act_value, act_pull = jax.vjp(lambda signal: jax.nn.gelu(signal, approximate=True), gate_back)
    grad_gate = act_pull(grad_hidden * up_back)[0].astype(jnp.bfloat16)
    grad_up = (grad_hidden * act_value).astype(jnp.bfloat16)
    gate_grad = weight_term(normed_ffn, grad_gate)
    up_grad = weight_term(normed_ffn, grad_up)
    norm_ffn_part = project_back(grad_gate, w_gate) + project_back(grad_up, w_up)
    grad_normed_ffn = lax.psum(norm_ffn_part.astype(jnp.bfloat16), "tensor").astype(jnp.float32)
    grad_middle = grad_out.astype(jnp.float32) + norm_back(
        middle, scale_ffn, gain_ffn, grad_normed_ffn
    )
    gain_ffn_part = gain_term(
        take_share(middle.reshape(plane)),
        take_share(scale_ffn.reshape(row_count, length, 1)),
        take_share(grad_normed_ffn.reshape(plane)),
    )
    grad_branch = grad_middle.astype(jnp.bfloat16)
    out_grad = weight_term(mixed_heads, grad_branch)
    grad_mixed = project_back(grad_branch, w_out).astype(jnp.bfloat16).reshape(heads_shape)
    score_sums = [
        jnp.zeros((head_count, block_rows, length), jnp.float32)
        for block_index in range(block_count)
    ]
    row_index = 0
    doc_row = segments[row_index]
    key_row = key_proj[row_index]
    value_row = value_proj[row_index]
    key_sum = jnp.zeros((length, head_count, head_dim), jnp.float32)
    value_sum = jnp.zeros((length, head_count, head_dim), jnp.float32)
    query_pieces = []
    for block_index in range(block_count):
        block_start = block_index * block_rows
        same_doc = doc_row[block_start : block_start + block_rows, None] == doc_row[None, :]
        query_block = queries[row_index, block_start : block_start + block_rows]
        grad_block = grad_mixed[row_index, block_start : block_start + block_rows]
        scores = score_block(query_block, key_row, bias_blocks[block_index], same_doc)
        weights_back = jnp.exp(scores - log_totals[row_index][block_index])
        grad_weights = jnp.einsum(
            "qhd,khd->hqk", grad_block, value_row, preferred_element_type=jnp.float32
        )
        row_delta = jnp.sum(weights_back * grad_weights, axis=-1, keepdims=True)
        grad_scores = weights_back * (grad_weights - row_delta)
        score_sums[block_index] = grad_scores
        scores_low = grad_scores.astype(jnp.bfloat16)
        query_pieces.append(
            jnp.einsum(
                "hqk,khd->qhd", scores_low, key_row, preferred_element_type=jnp.float32
            ).astype(jnp.bfloat16)
        )
        key_sum = key_sum + jnp.einsum(
            "hqk,qhd->khd", scores_low, query_block, preferred_element_type=jnp.float32
        )
        value_sum = value_sum + jnp.einsum(
            "hqk,qhd->khd",
            weights_back.astype(jnp.bfloat16),
            grad_block,
            preferred_element_type=jnp.float32,
        )
    query_rows = [jnp.concatenate(query_pieces, axis=0)]
    key_rows = [key_sum.astype(jnp.bfloat16)]
    value_rows = [value_sum.astype(jnp.bfloat16)]
    grad_query = jnp.stack(query_rows).reshape(token_count, local_width)
    grad_key = jnp.stack(key_rows).reshape(token_count, local_width)
    grad_value = jnp.stack(value_rows).reshape(token_count, local_width)
    table_grad = jnp.zeros((bucket_count, head_count), jnp.float32)
    for block_index in range(block_count):
        onehot = bucket_onehot(block_index * block_rows, block_rows, length, bucket_count)
        table_grad = table_grad + lax.dot_general(
            onehot,
            score_sums[block_index].reshape(head_count, block_rows * length),
            (((1,), (1,)), ((), ())),
            precision=highest,
        )
    query_grad = weight_term(normed, grad_query)
    key_grad = weight_term(normed, grad_key)
    value_grad = weight_term(normed, grad_value)
    norm_attn_part = (
        project_back(grad_query, w_query)
        + project_back(grad_key, w_key)
        + project_back(grad_value, w_value)
    )
    grad_normed_attn = lax.psum(norm_attn_part.astype(jnp.bfloat16), "tensor").astype(jnp.float32)
    grad_input = grad_middle + norm_back(flat_inputs, scale_attn, gain_attn, grad_normed_attn)
    input_grad = take_share(grad_input.reshape(plane)).astype(jnp.bfloat16)
    gain_attn_part = gain_term(
        take_share(flat_inputs.reshape(plane)),
        take_share(scale_attn.reshape(row_count, length, 1)),
        take_share(grad_normed_attn.reshape(plane)),
    )
    gain_attn_grad, gain_ffn_grad = lax.psum((gain_attn_part, gain_ffn_part), ("dp", "tensor"))
    reduced = (
        lax.psum_scatter(
            query_grad.astype(jnp.bfloat16), "dp", scatter_dimension=0, tiled=True
        ).astype(jnp.float32),
        lax.psum_scatter(
            key_grad.astype(jnp.bfloat16), "dp", scatter_dimension=0, tiled=True
        ).astype(jnp.float32),
        lax.psum_scatter(
            value_grad.astype(jnp.bfloat16), "dp", scatter_dimension=0, tiled=True
        ).astype(jnp.float32),
        lax.psum_scatter(
            out_grad.astype(jnp.bfloat16), "dp", scatter_dimension=1, tiled=True
        ).astype(jnp.float32),
        lax.psum_scatter(
            gate_grad.astype(jnp.bfloat16), "dp", scatter_dimension=0, tiled=True
        ).astype(jnp.float32),
        lax.psum_scatter(
            up_grad.astype(jnp.bfloat16), "dp", scatter_dimension=0, tiled=True
        ).astype(jnp.float32),
        lax.psum_scatter(
            down_grad.astype(jnp.bfloat16), "dp", scatter_dimension=1, tiled=True
        ).astype(jnp.float32),
        lax.psum_scatter(
            table_grad.astype(jnp.bfloat16), "dp", scatter_dimension=0, tiled=True
        ).astype(jnp.float32),
    )
    gathered = (
        lax.all_gather(reduced[0].astype(jnp.bfloat16), "dp", axis=0, tiled=True).astype(
            jnp.float32
        ),
        lax.all_gather(reduced[1].astype(jnp.bfloat16), "dp", axis=0, tiled=True).astype(
            jnp.float32
        ),
        lax.all_gather(reduced[2].astype(jnp.bfloat16), "dp", axis=0, tiled=True).astype(
            jnp.float32
        ),
        lax.all_gather(reduced[3].astype(jnp.bfloat16), "dp", axis=1, tiled=True).astype(
            jnp.float32
        ),
        lax.all_gather(reduced[4].astype(jnp.bfloat16), "dp", axis=0, tiled=True).astype(
            jnp.float32
        ),
        lax.all_gather(reduced[5].astype(jnp.bfloat16), "dp", axis=0, tiled=True).astype(
            jnp.float32
        ),
        lax.all_gather(reduced[6].astype(jnp.bfloat16), "dp", axis=1, tiled=True).astype(
            jnp.float32
        ),
        lax.all_gather(reduced[7].astype(jnp.bfloat16), "dp", axis=0, tiled=True).astype(
            jnp.float32
        ),
    )
    return (
        output,
        input_grad,
        gathered[0],
        gathered[1],
        gathered[2],
        gathered[3],
        gathered[4],
        gathered[5],
        gathered[6],
        gain_attn_grad,
        gain_ffn_grad,
        gathered[7],
    )


def solution(mesh):
    return jax.shard_map(
        shards,
        mesh=mesh,
        in_specs=(
            P("dp", None, None),
            P("dp", None),
            P("dp", None, None),
            P(None, "tensor"),
            P(None, "tensor"),
            P(None, "tensor"),
            P("tensor", None),
            P(None, "tensor"),
            P(None, "tensor"),
            P("tensor", None),
            P(),
            P(),
            P(None, "tensor"),
        ),
        out_specs=(
            P("dp", "tensor", None),
            P("dp", "tensor", None),
            P(None, "tensor"),
            P(None, "tensor"),
            P(None, "tensor"),
            P("tensor", None),
            P(None, "tensor"),
            P(None, "tensor"),
            P("tensor", None),
            P(),
            P(),
            P(None, "tensor"),
        ),
        check_vma=False,
    )
```

profile of v0, /device:TPU:17, one launch (start us, length us, event | category | flops | bytes accessed | tf_op | source)
XLA Modules:
  0.0 1493.4 jit_solution(11549578221789818774)
XLA Ops:
  17.8 3.6 convolution_convert_fusion.11
  24.2 23.3 %fusion.1 = f32[524288,8]{0,1:T(8,128)} fusion(f32[32,8]{0,1:T(8,128)S(1)} %copy-done.45, s32[524288]{0:T(1024)S(1)} %fusion.51), kind=kOutput, calls=%fused_computation.2 | convolution fusion | flops 1627389952 | bytes 18875392 | tf_op jit(solution)/shard_map/dot_general | solution.py:105
  49.1 23.8 %fusion.3 = f32[524288,8]{0,1:T(8,128)} fusion(f32[32,8]{0,1:T(8,128)S(1)} %copy-done.45, s32[524288]{0:T(1024)S(1)} %fusion.50), kind=kOutput, calls=%fused_computation.5 | convolution fusion | flops 1627389952 | bytes 18875392 | tf_op jit(solution)/shard_map/dot_general | solution.py:105
  73.6 21.5 %fusion.84 = (f32[8,512]{1,0:T(8,128)S(1)}, f32[8,512,1024]{2,1,0:T(8,128)}) fusion(f32[1,8,512,1024]{3,1,2,0:T(8,128)} %bitcast.182, bf16[1024,8,64]{0,2,1:T(8,128)(2,1)S(1)} %bitcast.183, bf16[1,1024,8,64]{1,3,2,0:T(8,128)(2,1)S(1)} %bitcast.193, pred[512,1024]{1,0:T(8,128)(4,1)S(1)} %get-tuple-element.52), kind=kOutput, calls=%fused_computation.152 | convolution fusion | flops 549449728 | bytes 35667968 | tf_op jit(solution)/shard_map/qhd,khd->hqk/dot_general | solution.py:59
  95.1 7.8 fusion.11
  105.7 3.8 fusion.72
  109.6 21.5 %fusion.85 = (f32[8,512]{1,0:T(8,128)S(1)}, f32[8,512,1024]{2,1,0:T(8,128)}) fusion(f32[1,8,512,1024]{3,1,2,0:T(8,128)} %bitcast.181, bf16[1024,8,64]{0,2,1:T(8,128)(2,1)S(1)} %bitcast.184, bf16[1,1024,8,64]{1,3,2,0:T(8,128)(2,1)S(1)} %bitcast.194, pred[512,1024]{1,0:T(8,128)(4,1)S(1)} %get-tuple-element.51), kind=kOutput, calls=%fused_computation.153 | convolution fusion | flops 549449728 | bytes 35667968 | tf_op jit(solution)/shard_map/qhd,khd->hqk/dot_general | solution.py:59
  131.0 7.8 fusion.10
  141.7 3.8 fusion.71
  146.6 4.4 convolution_convert_fusion.4
  151.5 154.8 %all-reduce.7.cloned.1.call-done = bf16[1024,2048]{1,0:T(8,128)(2,1)} async-done(((bf16[1024,2048]{1,0:T(8,128)(2,1)}), bf16[1024,2048]{1,0:T(8,128)(2,1)}) %all-reduce.7.cloned.1.call-update) | async-done | bytes 4194320 | tf_op jit(solution)/shard_map/psum | solution.py:130
  306.3 5.0 multiply_reduce_fusion.3
  315.0 7.3 fusion.87
  322.3 11.4 multiply_convert_fusion.2
  333.8 13.3 fusion.32
  347.0 7.8 fusion.88
  354.9 11.2 add_convert_fusion.1
  366.2 154.1 %all-reduce.9.cloned.1.call-done = bf16[1024,2048]{1,0:T(8,128)(2,1)} async-done(((bf16[1024,2048]{1,0:T(8,128)(2,1)}), bf16[1024,2048]{1,0:T(8,128)(2,1)}) %all-reduce.9.cloned.1.call-update) | async-done | bytes 4194320 | tf_op jit(solution)/shard_map/psum | solution.py:152
  520.2 6.7 multiply_reduce_fusion.2
  528.5 10.1 multiply_add_fusion
  538.6 6.9 fusion.64
  545.5 13.4 multiply_reduce_fusion.1
  558.9 4.2 fusion.14
  563.1 8.8 add_convert_fusion.2
  572.9 4.4 convolution_convert_fusion.6
  577.4 19.0 %fusion.42 = (f32[1,8,512,1024]{3,2,1,0:T(8,128)}, bf16[8,512,1024]{2,1,0:T(8,128)(2,1)S(1)}) fusion(f32[8,512,1024]{2,1,0:T(8,128)} %get-tuple-element.68, f32[8,512]{1,0:T(8,128)S(1)} %get-tuple-element.67, f32[8,512,1024]{2,1,0:T(8,128)} %get-tuple-element.62, f32[8,512]{1,0:T(8,128)S(1)} %log_add_fusion.1), kind=kLoop, calls=%fused_computation.75 | loop fusion | flops 16777216 | bytes 58753024
  599.9 7.1 convolution_convert_fusion.5
  607.0 11.8 multiply_reduce_fusion
  618.8 19.2 %fusion.44 = (f32[1,8,512,1024]{3,2,1,0:T(8,128)}, bf16[8,512,1024]{2,1,0:T(8,128)(2,1)S(1)}) fusion(f32[8,512,1024]{2,1,0:T(8,128)} %get-tuple-element.66, f32[8,512]{1,0:T(8,128)S(1)} %get-tuple-element.65, f32[8,512,1024]{2,1,0:T(8,128)} %get-tuple-element.60, f32[8,512]{1,0:T(8,128)S(1)} %log_add_fusion), kind=kLoop, calls=%fused_computation.77 | loop fusion | flops 16777216 | bytes 58753024
  643.3 4.2 convolution_convert_fusion.7
  647.6 6.3 fusion.69
  656.7 4.2 convolution_convert_fusion.8
  661.0 10.0 convolution_convert_fusion.2
  671.0 9.9 convolution_convert_fusion.1
  681.1 9.0 fusion.86
  690.1 9.1 fusion.41
  700.7 7.5 convolution_convert_fusion
  710.2 43.0 %reduce-scatter.8.cloned.1.call-done = bf16[256,512]{1,0:T(8,128)(2,1)} async-done(((bf16[2048,512]{1,0:T(8,128)(2,1)}), bf16[256,512]{1,0:T(8,128)(2,1)}) %reduce-scatter.8.cloned.1.call-update) | async-done | bytes 262160 | tf_op jit(solution)/shard_map/reduce_scatter | solution.py:236
  753.3 10.4 convolution_convert_fusion.3
  768.5 6.3 add_convert_fusion
  774.9 38.9 %reduce-scatter.16.cloned.1.call-done = bf16[256,1280]{1,0:T(8,128)(2,1)} async-done(((bf16[2048,1280]{1,0:T(8,128)(2,1)}), bf16[256,1280]{1,0:T(8,128)(2,1)}) %reduce-scatter.16.cloned.1.call-update) | async-done | bytes 655376 | tf_op jit(solution)/shard_map/reduce_scatter | solution.py:248
  813.8 60.3 %reduce-scatter.18.cloned.1.call-done = bf16[256,1280]{1,0:T(8,128)(2,1)} async-done(((bf16[2048,1280]{1,0:T(8,128)(2,1)}), bf16[256,1280]{1,0:T(8,128)(2,1)}) %reduce-scatter.18.cloned.1.call-update) | async-done | bytes 655376 | tf_op jit(solution)/shard_map/reduce_scatter | solution.py:251
  874.2 59.9 %reduce-scatter.20.cloned.1.call-done = bf16[1280,256]{1,0:T(8,128)(2,1)} async-done(((bf16[1280,2048]{1,0:T(8,128)(2,1)}), bf16[1280,256]{1,0:T(8,128)(2,1)}) %reduce-scatter.20.cloned.1.call-update) | async-done | bytes 655376 | tf_op jit(solution)/shard_map/reduce_scatter | solution.py:254
  934.1 6.7 convert_element_type.351
  942.9 18.6 %copy.33 = f32[1,8,512,1024]{3,1,2,0:T(8,128)} copy(f32[1,8,512,1024]{3,2,1,0:T(8,128)} %get-tuple-element.40) | data formatting | bytes 33554432
  961.4 18.1 %copy.34 = f32[1,8,512,1024]{3,1,2,0:T(8,128)} copy(f32[1,8,512,1024]{3,2,1,0:T(8,128)} %get-tuple-element.42) | data formatting | bytes 33554432
  979.5 34.5 %fusion = f32[32,8]{1,0:T(8,128)S(1)} fusion(f32[8,524288]{1,0:T(8,128)} %bitcast.188, s32[524288]{0:T(1024)S(1)} %copy-done.21), kind=kOutput, calls=%fused_computation.1 | convolution fusion | flops 1627389952 | bytes 18875392 | tf_op jit(solution)/shard_map/dot_general | solution.py:212
  1014.1 34.9 %fusion.74 = bf16[32,8]{1,0:T(8,128)(2,1)S(1)} fusion(f32[32,8]{1,0:T(8,128)S(1)} %fusion, f32[8,524288]{1,0:T(8,128)} %bitcast.187, s32[524288]{0:T(1024)S(1)} %copy-done.23), kind=kOutput, calls=%fused_computation.129 | convolution fusion | flops 1627390464 | bytes 18875904 | tf_op jit(solution)/shard_map/dot_general | solution.py:212
  1048.9 12.1 all-reduce
  1061.0 10.4 all-gather
  1072.1 6.5 convert_element_type.389
  1078.6 4.2 convert_element_type.415
  1082.8 4.1 convert_element_type.417
  1086.9 4.2 convert_element_type.413
  1091.2 4.2 convert_element_type.411
  1095.4 251.8 %all-reduce.11.cloned.1.call-done = (bf16[1024,2048]{1,0:T(8,128)(2,1)}, bf16[1024,2048]{1,0:T(8,128)(2,1)}) async-done(((bf16[1024,2048]{1,0:T(8,128)(2,1)}, bf16[1024,2048]{1,0:T(8,128)(2,1)}), (bf16[1024,2048]{1,0:T(8,128)(2,1)}, bf16[1024,2048]{1,0:T(8,128)(2,1)})) %all-reduce.11.cloned.1.call-update) | async-done | bytes 8388624 | tf_op jit(solution)/shard_map/psum | solution.py:138
  1351.9 7.1 fusion.21
  1359.1 6.8 fusion.56
  1365.9 40.4 %all-reduce.1 = (f32[2048]{0:T(1024)}, f32[2048]{0:T(1024)}) all-reduce(f32[2048]{0:T(1024)S(1)} %get-tuple-element.57, f32[2048]{0:T(1024)S(1)} %get-tuple-element.70), channel_id=1, replica_groups=mesh['dp'=8,'tensor'=4] {'dp','tensor'}, use_global_device_ids=true, to_apply=%region_22.23 | all-reduce | flops 4096 | bytes 32768 | tf_op jit(solution)/shard_map/psum | solution.py:234
  1406.3 7.4 convert_element_type.419
  1413.7 20.7 %all-gather.19.cloned.1.call-done = bf16[2048,1280]{1,0:T(8,128)(2,1)} async-done(((bf16[256,1280]{1,0:T(8,128)(2,1)}), bf16[2048,1280]{1,0:T(8,128)(2,1)}) %all-gather.19.cloned.1.call-update) | async-done | bytes 5242896 | tf_op jit(solution)/shard_map/all_gather | solution.py:277
  1434.4 7.5 convert_element_type.421
  1442.0 36.4 %all-gather.21.cloned.1.call-done = bf16[1280,2048]{1,0:T(8,128)(2,1)} async-done(((bf16[1280,256]{1,0:T(8,128)(2,1)}), bf16[1280,2048]{1,0:T(8,128)(2,1)}) %all-gather.21.cloned.1.call-update) | async-done | bytes 5242896 | tf_op jit(solution)/shard_map/all_gather | solution.py:280
  1478.4 8.0 convert_element_type.423
  (204 shorter events, 56.3 us)
Async XLA Ops:
  7.2 139.4 %copy-start = (bf16[512,2048]{1,0:T(8,128)(2,1)S(1)}, bf16[512,2048]{1,0:T(8,128)(2,1)}, u32[]{:S(2)}) copy-start(bf16[512,2048]{1,0:T(8,128)(2,1)} %param.19) | copy-start | bytes 6291460
  7.2 299.1 %all-reduce.7.cloned.1.call-start = ((), (), s32[]{:S(2)}) async-start(), calls=%async_computation.7 | async-start | bytes 8388608 | tf_op jit(solution)/shard_map/psum | solution.py:130
  7.3 3.2 copy-start.46
  10.5 6.7 copy-start.42
  13.1 96.5 %copy-start.24 = (bf16[1024,512]{0,1:T(8,128)(2,1)}, bf16[1024,512]{0,1:T(8,128)(2,1)S(1)}, u32[]{:S(2)}) copy-start(bf16[1024,512]{0,1:T(8,128)(2,1)S(1)} %convolution_convert_fusion.10) | copy-start | bytes 3145732
  15.7 93.9 %copy-start.17 = (bf16[1024,512]{0,1:T(8,128)(2,1)}, bf16[1024,512]{0,1:T(8,128)(2,1)S(1)}, u32[]{:S(2)}) copy-start(bf16[1024,512]{0,1:T(8,128)(2,1)S(1)} %convolution_convert_fusion.9) | copy-start | bytes 3145732
  24.2 23.3 %copy-start.20 = (s32[524288]{0:T(1024)}, s32[524288]{0:T(1024)S(1)}, u32[]{:S(2)}) copy-start(s32[524288]{0:T(1024)S(1)} %fusion.51) | copy-start | bytes 6291460
  49.1 23.8 %copy-start.22 = (s32[524288]{0:T(1024)}, s32[524288]{0:T(1024)S(1)}, u32[]{:S(2)}) copy-start(s32[524288]{0:T(1024)S(1)} %fusion.50) | copy-start | bytes 6291460
  73.6 29.4 %copy-start.30 = (bf16[1024,512]{0,1:T(8,128)(2,1)S(1)}, bf16[1024,512]{0,1:T(8,128)(2,1)}, u32[]{:S(2)}) copy-start(bf16[1024,512]{0,1:T(8,128)(2,1)} %convolution_convert_fusion.11) | copy-start | bytes 3145732
  95.1 10.6 copy-start.2
  131.0 10.6 copy-start.3
  151.0 160.3 %copy-start.40 = (f32[2048]{0:T(1024)S(1)}, f32[2048]{0:T(1024)}, u32[]{:S(2)}) copy-start(f32[2048]{0:T(1024)} %param.24) | copy-start | bytes 24580
  151.0 369.2 %all-reduce.9.cloned.1.call-start = ((), (), s32[]{:S(2)}) async-start(), calls=%async_computation.8 | async-start | bytes 8388608 | tf_op jit(solution)/shard_map/psum | solution.py:152
  306.3 5.1 copy-start.5
  306.3 5.9 copy-start.14
  306.3 8.7 slice-start.4
  312.2 214.8 %copy-start.41 = (f32[1024]{0:T(1024)}, f32[1024]{0:T(1024)S(1)}, u32[]{:S(2)}) copy-start(f32[1024]{0:T(1024)S(1)} %add_rsqrt_fusion) | copy-start | bytes 12292
  315.0 18.7 %copy-start.26 = (bf16[1024,2048]{1,0:T(8,128)(2,1)}, bf16[1024,2048]{1,0:T(8,128)(2,1)S(1)}, u32[]{:S(2)}) copy-start(bf16[1024,2048]{1,0:T(8,128)(2,1)S(1)} %multiply_convert_fusion) | copy-start | bytes 12582916
  315.0 7.3 copy-start.31
  333.8 21.1 %copy-start.54 = (bf16[1024,1280]{1,0:T(8,128)(2,1)}, bf16[1024,1280]{1,0:T(8,128)(2,1)S(1)}, u32[]{:S(2)}) copy-start(bf16[1024,1280]{1,0:T(8,128)(2,1)S(1)} %get-tuple-element.63) | copy-start | bytes 7864324
  347.0 7.9 copy-start.55
  366.1 342.2 %reduce-scatter.12.cloned.1.call-start = ((), (), s32[]{:S(2)}) async-start(), calls=%async_computation.13 | async-start | bytes 2359296 | tf_op jit(solution)/shard_map/reduce_scatter | solution.py:242
  520.2 6.8 copy-start.6
  520.2 7.1 copy-start.15
  520.2 8.3 copy-start.16
  538.6 20.2 %slice-start = ((s8[16777216]{0:T(1024)(128)(4,1)}), s8[4194304]{0:T(1024)(128)(4,1)S(1)}, s32[]{:S(2)}) async-start(s8[16777216]{0:T(1024)(128)(4,1)} %bitcast.179), calls=%async_computation.24 | async-start | bytes 8388608
  538.6 20.2 %slice-start.1 = ((s8[16777216]{0:T(1024)(128)(4,1)}), s8[4194304]{0:T(1024)(128)(4,1)S(1)}, s32[]{:S(2)}) async-start(s8[16777216]{0:T(1024)(128)(4,1)} %bitcast.179), calls=%async_computation.25 | async-start | bytes 8388608
  545.5 13.4 slice-start.2
  545.5 13.4 slice-start.3
  563.1 9.9 copy-start.7
  563.1 9.9 copy-start.43
  563.1 9.8 copy-start.47
  577.3 131.5 %reduce-scatter.14.cloned.1.call-start = ((), (), s32[]{:S(2)}) async-start(), calls=%async_computation.15 | async-start | bytes 2359296 | tf_op jit(solution)/shard_map/reduce_scatter | solution.py:245
  577.4 19.0 %copy-start.25 = (bf16[1024,512]{0,1:T(8,128)(2,1)S(1)}, bf16[1024,512]{0,1:T(8,128)(2,1)}, u32[]{:S(2)}) copy-start(bf16[1024,512]{0,1:T(8,128)(2,1)} %copy-done.24) | copy-start | bytes 3145732
  596.4 3.5 copy-start.13
  596.4 3.5 copy-start.39
  618.8 90.8 %reduce-scatter.10.cloned.1.call-start = ((), (), s32[]{:S(2)}) async-start(), calls=%async_computation.11 | async-start | bytes 2359296 | tf_op jit(solution)/shard_map/reduce_scatter | solution.py:239
  638.0 4.3 copy-start.11
  638.0 5.3 copy-start.8
  643.3 4.3 copy-start.18
  647.5 105.6 %reduce-scatter.8.cloned.1.call-start = ((), (), s32[]{:S(2)}) async-start(), calls=%async_computation.9 | async-start | bytes 2359296 | tf_op jit(solution)/shard_map/reduce_scatter | solution.py:236
  647.6 6.3 copy-start.12
  656.7 4.2 copy-start.36
  660.9 152.8 %reduce-scatter.16.cloned.1.call-start = ((), (), s32[]{:S(2)}) async-start(), calls=%async_computation.17 | async-start | bytes 5898240 | tf_op jit(solution)/shard_map/reduce_scatter | solution.py:248
  671.0 203.1 %reduce-scatter.18.cloned.1.call-start = ((), (), s32[]{:S(2)}) async-start(), calls=%async_computation.19 | async-start | bytes 5898240 | tf_op jit(solution)/shard_map/reduce_scatter | solution.py:251
  681.0 253.1 %reduce-scatter.20.cloned.1.call-start = ((), (), s32[]{:S(2)}) async-start(), calls=%async_computation.21 | async-start | bytes 5898240 | tf_op jit(solution)/shard_map/reduce_scatter | solution.py:254
  681.0 9.1 copy-start.27
  690.1 10.6 copy-start.32
  708.2 370.4 %all-gather.13.cloned.1.call-start = ((), (), s32[]{:S(2)}) async-start(), calls=%async_computation.14 | async-start | bytes 2359296 | tf_op jit(solution)/shard_map/all_gather | solution.py:268
  708.8 374.0 %all-gather.15.cloned.1.call-start = ((), (), s32[]{:S(2)}) async-start(), calls=%async_computation.16 | async-start | bytes 2359296 | tf_op jit(solution)/shard_map/all_gather | solution.py:271
  709.5 377.4 %all-gather.11.cloned.1.call-start = ((), (), s32[]{:S(2)}) async-start(), calls=%async_computation.12 | async-start | bytes 2359296 | tf_op jit(solution)/shard_map/all_gather | solution.py:265
  710.1 381.0 %all-gather.9.cloned.1.call-start = ((), (), s32[]{:S(2)}) async-start(), calls=%async_computation.10 | async-start | bytes 2359296 | tf_op jit(solution)/shard_map/all_gather | solution.py:262
  753.2 10.5 copy-start.34
  753.2 594.0 %all-reduce.11.cloned.1.call-start = ((), (), s32[]{:S(2)}) async-start(), calls=%async_computation.23 | async-start | bytes 16777216 | tf_op jit(solution)/shard_map/psum | solution.py:138
  753.2 10.4 copy-start.49
  774.8 631.5 %all-gather.17.cloned.1.call-start = ((), (), s32[]{:S(2)}) async-start(), calls=%async_computation.18 | async-start | bytes 5898240 | tf_op jit(solution)/shard_map/all_gather | solution.py:274
  813.8 620.7 %all-gather.19.cloned.1.call-start = ((), (), s32[]{:S(2)}) async-start(), calls=%async_computation.20 | async-start | bytes 5898240 | tf_op jit(solution)/shard_map/all_gather | solution.py:277
  874.1 604.3 %all-gather.21.cloned.1.call-start = ((), (), s32[]{:S(2)}) async-start(), calls=%async_computation.22 | async-start | bytes 5898240 | tf_op jit(solution)/shard_map/all_gather | solution.py:280
  934.1 6.8 copy-start.52
  961.4 18.1 %copy-start.21 = (s32[524288]{0:T(1024)S(1)}, s32[524288]{0:T(1024)}, u32[]{:S(2)}) copy-start(s32[524288]{0:T(1024)} %copy-done.20) | copy-start | bytes 6291460
  979.5 34.5 %copy-start.23 = (s32[524288]{0:T(1024)S(1)}, s32[524288]{0:T(1024)}, u32[]{:S(2)}) copy-start(s32[524288]{0:T(1024)} %copy-done.22) | copy-start | bytes 6291460
  1347.2 3.4 copy-start.10
  1347.2 4.7 copy-start.19
  1434.4 52.0 %copy-start.1 = (bf16[512,2048]{1,0:T(8,128)(2,1)S(1)}, bf16[512,2048]{1,0:T(8,128)(2,1)}, u32[]{:S(2)}) copy-start(bf16[512,2048]{1,0:T(8,128)(2,1)} %param.19) | copy-start | bytes 6291460
  (15 other events, 30.5 us)
Sparse Core Ops, SparseCore 0:
  151.1 155.0 all-reduce.6
  366.2 153.9 all-reduce.8
  577.4 41.1 reduce-scatter.11
  622.1 41.2 reduce-scatter.13
  666.6 41.1 reduce-scatter.9
  711.9 41.2 reduce-scatter.7
  757.1 56.5 reduce-scatter.15
  817.5 56.5 reduce-scatter.17
  877.5 56.5 reduce-scatter.19
  936.0 28.3 all-gather.12
  966.4 28.1 all-gather.14
  996.5 27.8 all-gather.10
  1026.5 27.9 all-gather.8
  1057.1 290.1 all-reduce.10
  1349.1 41.7 all-gather.16
  1392.8 41.6 all-gather.18
  1436.3 42.0 all-gather.20
where the time goes:
time: 1500 us; the launch traced here: 1490 us
  waiting for transfers between devices  822 us (55%)
  matrix products  375 us (25%)
  other arithmetic  155 us (10%)
  blocking collectives  62.8 us (4%)
  local copies, waits for them, and re-layouts  61.6 us (4%)
  between operations  15.9 us (1%)
    psum x1, waiting for transfers between devices, shards(): lax.psum(ffn_part.astype(jnp.bfloat16), 'tensor').astype(jnp.float32)  252 us
    psum x1, waiting for transfers between devices, shards(): lax.psum(attn_part.astype(jnp.bfloat16), 'tensor').astype(jnp.float32)  155 us
    psum x1, waiting for transfers between devices, shards(): lax.psum(norm_ffn_part.astype(jnp.bfloat16), 'tensor').astype(jnp.float32)  154 us
    dot_general x2, matrix products, shards(): lax.dot_general(onehot, score_sums[block_index].reshape(head_count, block...  69.4 us
    dot_general x9, matrix products, project(): return jnp.dot(left_side, right_side, preferred_element_type=jnp.float32)  62.2 us
    unnamed x133, local copies, waits for them, and re-layouts  60.7 us
    reduce_scatter x1, waiting for transfers between devices, shards(): lax.psum_scatter(up_grad.astype(jnp.bfloat16), 'dp', scatter_dimension=0,...  60.3 us
    reduce_scatter x1, waiting for transfers between devices, shards(): lax.psum_scatter(down_grad.astype(jnp.bfloat16), 'dp', scatter_dimension=...  59.9 us
  transfers between devices with their start and end apart: 17, of which 9 were waited for; matrix products, arithmetic and copies ran while one was open for 21% of the time, Pallas kernels for 0%

commit v1 on v0

v1 whole, which is shorter than its diff:
```python
import functools

import jax
import jax.numpy as jnp
from jax import lax
from jax.experimental import pallas as pl
from jax.experimental.pallas import tpu as pltpu
from jax.sharding import PartitionSpec as P

thresholds = (12, 16, 23, 32, 46, 64, 91)
highest = lax.Precision.HIGHEST
tile = 256
kinds = 5
group_pairs = 1
lanes = 128
bf16 = jnp.bfloat16
f32 = jnp.float32


def buckets_of(offset):
    distance = jnp.abs(offset)
    far_bucket = jnp.full(distance.shape, 8, jnp.int32)
    for bound_value in thresholds:
        far_bucket = far_bucket + (distance >= bound_value).astype(jnp.int32)
    near_bucket = jnp.where(distance < 8, distance, far_bucket)
    return near_bucket + 16 * (offset > 0).astype(jnp.int32)


def offset_onehot(bucket_count):
    span = lax.broadcasted_iota(jnp.int32, (kinds, 2 * tile), 0)
    place = lax.broadcasted_iota(jnp.int32, (kinds, 2 * tile), 1)
    offset = tile * (span - 2) - (place - tile)
    bucket = buckets_of(offset).reshape(1, kinds * 2 * tile)
    labels = jnp.arange(bucket_count, dtype=jnp.int32)[:, None]
    return (bucket == labels).astype(f32)


def dot_nt(left_side, right_side, **more):
    return lax.dot_general(
        left_side, right_side, (((1,), (1,)), ((), ())), preferred_element_type=f32, **more
    )


def dot_nn(left_side, right_side):
    return lax.dot_general(
        left_side, right_side, (((1,), (0,)), ((), ())), preferred_element_type=f32
    )


def fill_bias(line_ref, bias_ref, spans):
    middle = spans // 2
    for half in range(bias_ref.shape[0]):
        for span in range(spans):
            rows = slice(span * tile, (span + 1) * tile)
            near = span - middle
            if abs(near) > 1:
                place = 0 if near < 0 else 4
                bias_ref[half, rows, :] = jnp.broadcast_to(
                    line_ref[half, place, 0:1][None, :], (tile, tile)
                )
            else:
                line = jnp.broadcast_to(line_ref[half, near + 2][None, :], (tile, 2 * tile))
                turned = pltpu.roll(line, tile, 1, stride=1, stride_axis=0)
                bias_ref[half, rows, :] = turned[:, :tile]


def unskew(part):
    group = 8
    gathered = jnp.zeros((group, 2 * tile), f32)
    for start in range(0, tile, group):
        piece = part[start : start + group]
        wide = jnp.concatenate([piece, jnp.zeros_like(piece)], axis=1)
        gathered = gathered + pltpu.roll(wide, tile - start, 1)
    line = gathered[0:1]
    for shift in range(1, group):
        line = line + pltpu.roll(gathered[shift : shift + 1], 2 * tile - shift, 1)
    return line


def half_mask(shape, half):
    lane = lax.broadcasted_iota(jnp.int32, shape, len(shape) - 1)
    return (lane < lanes // 2) if half == 0 else (lane >= lanes // 2)


def keep_half(value, half):
    return jnp.where(half_mask(value.shape, half), value, jnp.zeros_like(value))


def by_count(count, most, run):
    for number in range(1, most + 1):
        pl.when(count == number)(functools.partial(run, number))


def pair_columns(pair):
    return slice(pair * lanes, (pair + 1) * lanes)


def forward_kernel(
    block_count, first_ref, last_ref, q_ref, k_ref, v_ref, seg_row_ref, seg_col_ref, line_ref,
    out_ref, lse_ref, bias_ref, vt_ref,
):
    row = pl.program_id(0)
    mid = lanes // 2
    group = q_ref.shape[2] // lanes
    fill_bias(line_ref, bias_ref, 2 * block_count - 1)
    for pair in range(group):
        values_t = jnp.transpose(v_ref[0, :, pair_columns(pair)].astype(f32)).astype(bf16)
        place = lax.broadcasted_iota(jnp.int32, values_t.shape, 0)
        ones = jnp.ones_like(values_t)
        vt_ref[2 * pair] = jnp.where(place < mid, values_t, ones)
        vt_ref[2 * pair + 1] = jnp.where(place < mid, ones, values_t)

    @pl.loop(0, block_count)
    def _(block):
        first = first_ref[row * block_count + block]
        last = last_ref[row * block_count + block]
        here = pl.ds(pl.multiple_of(block * tile, tile), tile)

        def run(number):
            rows = pl.ds(pl.multiple_of(first * tile, tile), number * tile)
            shift = first - block + block_count - 1
            bias_rows = pl.ds(pl.multiple_of(shift * tile, tile), number * tile)
            same = seg_col_ref[0, rows, :] == seg_row_ref[0, :, here]
            for pair in range(group):
                keys = k_ref[0, rows, pair_columns(pair)]
                q_pair = q_ref[0, here, pair_columns(pair)]
                sums = []
                tops = []
                for half in range(2):
                    head = 2 * pair + half
                    scores = dot_nt(keys, keep_half(q_pair, half)) + bias_ref[head, bias_rows, :]
                    scores = jnp.where(same, scores, -1000000000.0)
                    top = jnp.max(scores, axis=0, keepdims=True)
                    weights = jnp.exp(scores - top).astype(bf16)
                    sums.append(dot_nn(vt_ref[head, :, rows], weights))
                    tops.append(top)
                total_0 = sums[0][mid : mid + 1]
                total_1 = sums[1][0:1]
                mixed_t = jnp.concatenate(
                    [sums[0][:mid] / total_0, sums[1][mid:] / total_1], axis=0
                )
                out_ref[0, here, pair_columns(pair)] = jnp.transpose(mixed_t).astype(bf16)
                lse_ref[0, pair, :, here] = jnp.concatenate(
                    [tops[0] + jnp.log(total_0), tops[1] + jnp.log(total_1)], axis=0
                )

        by_count(last - first + 1, block_count, run)


def backward_kernel(
    block_count, first_ref, last_ref, q_ref, k_ref, v_ref, grad_ref, out_ref, lse_ref, seg_row_ref,
    seg_col_ref, line_ref, dq_ref, dk_ref, dv_ref, sums_ref,
    bias_ref, gbias_ref, kt_ref, dk_acc, dv_acc,
):
    row = pl.program_id(0)
    mid = lanes // 2
    group = q_ref.shape[2] // lanes
    spans = 2 * block_count - 1
    fill_bias(line_ref, bias_ref, spans)
    for pair in range(group):
        keys_t = jnp.transpose(k_ref[0, :, pair_columns(pair)].astype(f32)).astype(bf16)
        place = lax.broadcasted_iota(jnp.int32, keys_t.shape, 0)
        zeros = jnp.zeros_like(keys_t)
        kt_ref[2 * pair] = jnp.where(place < mid, keys_t, zeros)
        kt_ref[2 * pair + 1] = jnp.where(place < mid, zeros, keys_t)
    gbias_ref[...] = jnp.zeros_like(gbias_ref)
    dk_acc[...] = jnp.zeros_like(dk_acc)
    dv_acc[...] = jnp.zeros_like(dv_acc)

    @pl.loop(0, block_count)
    def _(block):
        first = first_ref[row * block_count + block]
        last = last_ref[row * block_count + block]
        here = pl.ds(pl.multiple_of(block * tile, tile), tile)

        def run(number):
            rows = pl.ds(pl.multiple_of(first * tile, tile), number * tile)
            shift = first - block + block_count - 1
            bias_rows = pl.ds(pl.multiple_of(shift * tile, tile), number * tile)
            same = seg_col_ref[0, rows, :] == seg_row_ref[0, :, here]
            for pair in range(group):
                columns = pair_columns(pair)
                keys = k_ref[0, rows, columns]
                values = v_ref[0, rows, columns]
                q_pair = q_ref[0, here, columns]
                grad_pair = grad_ref[0, here, columns]
                product = grad_pair.astype(f32) * out_ref[0, here, columns].astype(f32)
                dq_t = dk = dv = None
                for half in range(2):
                    head = 2 * pair + half
                    q_half = keep_half(q_pair, half)
                    grad_half = keep_half(grad_pair, half)
                    picker = half_mask((8, lanes), half).astype(f32)
                    delta = dot_nt(picker, product, precision=highest)[0:1]
                    scores = dot_nt(keys, q_half) + bias_ref[head, bias_rows, :]
                    scores = jnp.where(same, scores, -1000000000.0)
                    weights = jnp.exp(scores - lse_ref[0, pair, half : half + 1, here])
                    grad_scores = weights * (dot_nt(values, grad_half) - delta)
                    gbias_ref[head, bias_rows, :] = gbias_ref[head, bias_rows, :] + grad_scores
                    low_scores = grad_scores.astype(bf16)
                    dv_part = dot_nn(weights.astype(bf16), grad_half)
                    dk_part = dot_nn(low_scores, q_half)
                    dq_part = dot_nn(kt_ref[head, :, rows], low_scores)
                    dv = dv_part if half == 0 else dv + dv_part
                    dk = dk_part if half == 0 else dk + dk_part
                    dq_t = dq_part if half == 0 else dq_t + dq_part
                dv_acc[rows, columns] = dv_acc[rows, columns] + dv
                dk_acc[rows, columns] = dk_acc[rows, columns] + dk
                dq_ref[0, here, columns] = jnp.transpose(dq_t).astype(bf16)

        by_count(last - first + 1, block_count, run)

    dk_ref[0] = dk_acc[...].astype(bf16)
    dv_ref[0] = dv_acc[...].astype(bf16)
    for head in range(2 * group):
        far = [None, None]
        for span in range(spans):
            near = span - spans // 2
            part = gbias_ref[head, span * tile : (span + 1) * tile, :]
            if abs(near) > 1:
                side = 0 if near < 0 else 1
                far[side] = part if far[side] is None else far[side] + part
            else:
                sums_ref[0, head, near + 2] = unskew(part)[0]
        for side in range(2):
            wide = jnp.sum(far[side], axis=0, keepdims=True)
            wide = jnp.concatenate([wide, jnp.zeros_like(wide)], axis=1)
            sums_ref[0, head, 4 * side] = wide[0]


def block_range(segments, block_count):
    rows = segments.shape[0]
    blocks = segments.reshape(rows, block_count, tile)
    first_seg = blocks[:, :, 0]
    last_seg = blocks[:, :, tile - 1]
    first = jnp.sum((last_seg[:, None, :] < first_seg[:, :, None]).astype(jnp.int32), axis=-1)
    last = jnp.sum((first_seg[:, None, :] <= last_seg[:, :, None]).astype(jnp.int32), axis=-1) - 1
    return first.reshape(-1), last.reshape(-1)


def grouping(width, length):
    pairs = width // lanes
    group = group_pairs if pairs % group_pairs == 0 else 1
    whole = pl.BlockSpec((1, length, group * lanes), lambda r, h, *_: (r, 0, h))
    seg_row = pl.BlockSpec((1, 1, length), lambda r, h, *_: (r, 0, 0))
    seg_col = pl.BlockSpec((1, length, 1), lambda r, h, *_: (r, 0, 0))
    line = pl.BlockSpec((2 * group, kinds, 2 * tile), lambda r, h, *_: (h, 0, 0))
    total = pl.BlockSpec((1, group, 2, length), lambda r, h, *_: (r, h, 0, 0))
    sums = pl.BlockSpec((1, 2 * group, kinds, 2 * tile), lambda r, h, *_: (r, h, 0, 0))
    return pairs, group, whole, seg_row, seg_col, line, total, sums


def attend(queries, keys, values, segments, lines):
    rows, length, width = queries.shape
    block_count = length // tile
    spans = 2 * block_count - 1
    first, last = block_range(segments, block_count)
    pairs, group, whole, seg_row, seg_col, line, total, _ = grouping(width, length)
    return pl.pallas_call(
        functools.partial(forward_kernel, block_count),
        out_shape=(
            jax.ShapeDtypeStruct((rows, length, width), bf16),
            jax.ShapeDtypeStruct((rows, pairs, 2, length), f32),
        ),
        grid_spec=pltpu.PrefetchScalarGridSpec(
            num_scalar_prefetch=2,
            grid=(rows, pairs // group),
            in_specs=[whole, whole, whole, seg_row, seg_col, line],
            out_specs=[whole, total],
            scratch_shapes=[
                pltpu.VMEM((2 * group, spans * tile, tile), f32),
                pltpu.VMEM((2 * group, lanes, length), bf16),
            ],
        ),
        name="attend",
    )(first, last, queries, keys, values, segments[:, None, :], segments[:, :, None], lines)


def attend_back(queries, keys, values, grad_mixed, mixed, totals, segments, lines):
    rows, length, width = queries.shape
    block_count = length // tile
    spans = 2 * block_count - 1
    first, last = block_range(segments, block_count)
    pairs, group, whole, seg_row, seg_col, line, total, sums = grouping(width, length)
    shape = jax.ShapeDtypeStruct((rows, length, width), bf16)
    return pl.pallas_call(
        functools.partial(backward_kernel, block_count),
        out_shape=(
            shape, shape, shape,
            jax.ShapeDtypeStruct((rows, 2 * pairs, kinds, 2 * tile), f32),
        ),
        grid_spec=pltpu.PrefetchScalarGridSpec(
            num_scalar_prefetch=2,
            grid=(rows, pairs // group),
            in_specs=[whole, whole, whole, whole, whole, total, seg_row, seg_col, line],
            out_specs=[whole, whole, whole, sums],
            scratch_shapes=[
                pltpu.VMEM((2 * group, spans * tile, tile), f32),
                pltpu.VMEM((2 * group, spans * tile, tile), f32),
                pltpu.VMEM((2 * group, lanes, length), bf16),
                pltpu.VMEM((length, group * lanes), f32),
                pltpu.VMEM((length, group * lanes), f32),
            ],
        ),
        name="attend_back",
    )(
        first, last, queries, keys, values, grad_mixed, mixed, totals,
        segments[:, None, :], segments[:, :, None], lines,
    )


def project(left_side, right_side):
    return jnp.dot(left_side, right_side, preferred_element_type=f32)


def project_back(left_side, right_side):
    return dot_nt(left_side, right_side)


def weight_term(left_side, right_side):
    return lax.dot_general(
        left_side, right_side, (((0,), (0,)), ((), ())), preferred_element_type=f32
    ).astype(bf16)


def norm_scale(signal):
    return lax.rsqrt(jnp.mean(signal * signal, axis=-1, keepdims=True) + 1e-06)


def norm_back(signal, rms_scale, gain_vec, grad_normed):
    grad_hat = grad_normed * gain_vec
    inner_mean = jnp.mean(grad_hat * signal, axis=-1, keepdims=True)
    return rms_scale * (grad_hat - signal * rms_scale * rms_scale * inner_mean)


def gain_term(signal, rms_scale, grad_normed):
    return jnp.sum(grad_normed * signal * rms_scale, axis=0)


def shards(
    inputs, segments, cotangent, w_query, w_key, w_value, w_out, w_gate, w_up, w_down,
    gain_attn, gain_ffn, bias_table,
):
    row_count, length, model_width = inputs.shape
    shares = lax.axis_size("tensor")
    share_rows = length // shares
    first_row = lax.axis_index("tensor") * share_rows
    bucket_count, head_count = bias_table.shape
    local_width = w_query.shape[1]
    token_count = row_count * length
    plane = (row_count, length, model_width)
    heads_shape = (row_count, length, local_width)
    share_shape = (row_count, share_rows, model_width)

    def take_share(signal):
        part = lax.dynamic_slice_in_dim(
            signal.reshape(row_count, length, -1), first_row, share_rows, 1
        )
        return part.reshape(row_count * share_rows, -1)

    def scatter(part):
        summed = lax.psum_scatter(
            part.astype(bf16).reshape(plane), "tensor", scatter_dimension=1, tiled=True
        )
        return summed.reshape(row_count * share_rows, model_width).astype(f32)

    flat_inputs = inputs.reshape(token_count, model_width).astype(f32)
    grad_out = cotangent.reshape(token_count, model_width)
    scale_attn = norm_scale(flat_inputs)
    normed = (flat_inputs * scale_attn * gain_attn).astype(bf16)
    queries = project(normed, w_query).astype(bf16).reshape(heads_shape)
    keys = project(normed, w_key).astype(bf16).reshape(heads_shape)
    values = project(normed, w_value).astype(bf16).reshape(heads_shape)
    onehot = offset_onehot(bucket_count)
    lines = jnp.dot(jnp.transpose(bias_table), onehot, precision=highest)
    lines = lines.reshape(head_count, kinds, 2 * tile)
    mixed, totals = attend(queries, keys, values, segments, lines)
    mixed_flat = mixed.reshape(token_count, local_width)
    attn_part = project(mixed_flat, w_out)
    attn_total = lax.psum(attn_part.astype(bf16), "tensor").astype(f32)
    grad_hidden = project_back(grad_out, w_down)
    middle = flat_inputs + attn_total
    scale_ffn = norm_scale(middle)
    normed_ffn = (middle * scale_ffn * gain_ffn).astype(bf16)
    gate_pre = project(normed_ffn, w_gate)
    up_pre = project(normed_ffn, w_up)
    act_value, act_pull = jax.vjp(lambda signal: jax.nn.gelu(signal, approximate=True), gate_pre)
    hidden = (act_value * up_pre).astype(bf16)
    grad_gate = act_pull(grad_hidden * up_pre)[0].astype(bf16)
    grad_up = (grad_hidden * act_value).astype(bf16)
    norm_ffn_part = project_back(grad_gate, w_gate) + project_back(grad_up, w_up)
    grad_normed_ffn = lax.psum(norm_ffn_part.astype(bf16), "tensor").astype(f32)
    ffn_share = scatter(project(hidden, w_down))
    middle_share = take_share(middle)
    output = (middle_share + ffn_share).reshape(share_shape).astype(bf16)
    down_grad = weight_term(hidden, grad_out)
    gate_up_grad = weight_term(normed_ffn, jnp.concatenate([grad_gate, grad_up], axis=1))
    grad_middle = grad_out.astype(f32) + norm_back(middle, scale_ffn, gain_ffn, grad_normed_ffn)
    gain_ffn_part = gain_term(middle_share, take_share(scale_ffn), take_share(grad_normed_ffn))
    grad_branch = grad_middle.astype(bf16)
    out_grad = weight_term(mixed_flat, grad_branch)
    grad_mixed = project_back(grad_branch, w_out).astype(bf16).reshape(heads_shape)
    grad_query, grad_key, grad_value, sums = attend_back(
        queries, keys, values, grad_mixed, mixed, totals, segments, lines
    )
    grad_query = grad_query.reshape(token_count, local_width)
    grad_key = grad_key.reshape(token_count, local_width)
    grad_value = grad_value.reshape(token_count, local_width)
    sums = jnp.sum(sums, axis=0).reshape(head_count, -1)
    table_grad = lax.dot_general(onehot, sums, (((1,), (1,)), ((), ())), precision=highest)
    norm_attn_part = (
        project_back(grad_query, w_query)
        + project_back(grad_key, w_key)
        + project_back(grad_value, w_value)
    )
    grad_normed_attn = scatter(norm_attn_part)
    qkv_grad = weight_term(normed, jnp.concatenate([grad_query, grad_key, grad_value], axis=1))
    inputs_share = take_share(flat_inputs)
    scale_share = take_share(scale_attn)
    grad_input = take_share(grad_middle) + norm_back(
        inputs_share, scale_share, gain_attn, grad_normed_attn
    )
    input_grad = grad_input.reshape(share_shape).astype(bf16)
    gain_attn_part = gain_term(inputs_share, scale_share, grad_normed_attn)
    gain_attn_grad, gain_ffn_grad = lax.psum((gain_attn_part, gain_ffn_part), ("dp", "tensor"))
    table_grad = lax.psum(table_grad, "dp")

    def reduce_all(grad, axis):
        part = lax.psum_scatter(grad, "dp", scatter_dimension=axis, tiled=True)
        return lax.all_gather(part, "dp", axis=axis, tiled=True)

    gate_up_grad = reduce_all(gate_up_grad, 0)
    down_grad = reduce_all(down_grad, 1).astype(f32)
    out_grad = reduce_all(out_grad, 1).astype(f32)
    qkv_grad = reduce_all(qkv_grad, 0)
    gate_grad, up_grad = jnp.split(gate_up_grad.astype(f32), 2, axis=1)
    query_grad, key_grad, value_grad = jnp.split(qkv_grad.astype(f32), 3, axis=1)
    return (
        output, input_grad, query_grad, key_grad, value_grad, out_grad, gate_grad, up_grad,
        down_grad, gain_attn_grad, gain_ffn_grad, table_grad,
    )


def solution(mesh):
    return jax.shard_map(
        shards,
        mesh=mesh,
        in_specs=(
            P("dp", None, None),
            P("dp", None),
            P("dp", None, None),
            P(None, "tensor"),
            P(None, "tensor"),
            P(None, "tensor"),
            P("tensor", None),
            P(None, "tensor"),
            P(None, "tensor"),
            P("tensor", None),
            P(),
            P(),
            P(None, "tensor"),
        ),
        out_specs=(
            P("dp", "tensor", None),
            P("dp", "tensor", None),
            P(None, "tensor"),
            P(None, "tensor"),
            P(None, "tensor"),
            P("tensor", None),
            P(None, "tensor"),
            P(None, "tensor"),
            P("tensor", None),
            P(),
            P(),
            P(None, "tensor"),
        ),
        check_vma=False,
    )
```

time: 1500 us -> 1080 us (0.72)
  matrix products: 375 us -> 139 us
  waiting for transfers between devices: 822 us -> 719 us
  other arithmetic: 155 us -> 65.9 us
  Pallas kernels: 0 us -> 52.3 us
  local copies, waits for them, and re-layouts: 61.6 us -> 28.9 us
    psum x3 -> x2, waiting for transfers between devices: 561 us -> 313 us  [the longest x1 159 us: shards(): attn_total = lax.psum(attn_part.astype(bf16), 'tensor').astype(f32)]
    dot_general x32 -> x16, matrix products: 328 us -> 96.1 us  [the longest x7 52 us: dot_nt(): lax.dot_general(left_side, right_side, (((1,), (1,)), ((), ())), preferre...]
    reduce_scatter x7 -> x6, waiting for transfers between devices: 202 us -> 284 us  [the longest x4 155 us: reduce_all(): part = lax.psum_scatter(grad, 'dp', scatter_dimension=axis, tiled=True)]
    all_gather x7 -> x4, waiting for transfers between devices: 57.2 us -> 121 us  [reduce_all(): return lax.all_gather(part, 'dp', axis=axis, tiled=True)]
    unnamed x133 -> x64, local copies, waits for them, and re-layouts: 60.7 us -> 5.41 us
    pallas_call x0 -> x2, Pallas kernels: none -> 52.3 us  [the longest x1 30.1 us: attend_back(): pl.pallas_call(functools.partial(backward_kernel, block_count), out_shape...]
    unnamed x7 -> x3, other arithmetic: 39.2 us -> 1.39 us
    convert_element_type x11 -> x6, other arithmetic: 59.1 us -> 32.5 us  [the longest x1 8.02 us: shards(): down_grad = reduce_all(down_grad, 1).astype(f32)]
  transfers between devices with their start and end apart: 17 -> 12, of which waited for: 9 -> 10; matrix products, arithmetic and copies ran while one was open for 21% -> 10% of each run, Pallas kernels for 0% -> 3%
where the time goes in v1:
time: 1080 us; the launch traced here: 1070 us
  waiting for transfers between devices  719 us (67%)
  matrix products  139 us (13%)
  other arithmetic  65.9 us (6%)
  blocking collectives  52.9 us (5%)
  Pallas kernels  52.3 us (5%)
  local copies, waits for them, and re-layouts  28.9 us (3%)
  between operations  14.8 us (1%)
    psum x1, waiting for transfers between devices, shards(): attn_total = lax.psum(attn_part.astype(bf16), 'tensor').astype(f32)  159 us
    reduce_scatter x4, waiting for transfers between devices, reduce_all(): part = lax.psum_scatter(grad, 'dp', scatter_dimension=axis, tiled=True)  155 us
    psum x1, waiting for transfers between devices, shards(): grad_normed_ffn = lax.psum(norm_ffn_part.astype(bf16), 'tensor').astype(f32)  154 us
    reduce_scatter x2, waiting for transfers between devices, scatter(): lax.psum_scatter(part.astype(bf16).reshape(plane), 'tensor', scatter_dime...  130 us
    all_gather x4, waiting for transfers between devices, reduce_all(): return lax.all_gather(part, 'dp', axis=axis, tiled=True)  121 us
    dot_general x7, matrix products, dot_nt(): lax.dot_general(left_side, right_side, (((1,), (1,)), ((), ())), preferre...  52 us
    dot_general x7, matrix products, project(): return jnp.dot(left_side, right_side, preferred_element_type=f32)  43.6 us
    dot_general x4, matrix products, weight_term(): lax.dot_general(left_side, right_side, (((0,), (0,)), ((), ())), preferre...  42.6 us
  transfers between devices with their start and end apart: 12, of which 10 were waited for; matrix products, arithmetic and copies ran while one was open for 10% of the time, Pallas kernels for 3%

profile of v1, /device:TPU:17, one launch (start us, length us, event | category | flops | bytes accessed | tf_op | source)
XLA Modules:
  0.0 1073.7 jit_solution(7692280978514468057)
XLA Ops:
  7.3 0.5 broadcast.304
  7.8 1.4 reduce.5
  9.3 0.1 copy.40
  9.3 0.1 copy.39
  9.4 0.7 convert_reduce_fusion
  10.1 0.5 broadcast_add_fusion.last_ref
  10.6 3.1 fusion
  13.8 6.4 fusion.39.q_ref
  20.2 3.4 fusion.40.k_ref
  23.5 3.4 fusion.41.v_ref
  26.9 1.0 copy.35.seg_col_ref
  27.9 0.1 subtract_abs_fusion
  28.1 0.2 fusion.50
  28.3 0.7 copy.36.line_ref
  29.0 22.2 %attend.1 = (bf16[1,1024,512]{2,1,0:T(8,128)(2,1)}, f32[1,4,2,1024]{3,2,1,0:T(2,128)}) custom-call(s32[4]{0:T(128)} %get-tuple-element.27.first_ref, s32[4]{0:T(128)} %broadcast_add_fusion.last_ref, bf16[1,1024,512]{2,1,0:T(8,128)(2,1)} %fusion.39.q_ref, bf16[1,1024,512]{2,1,0:T(8,128)(2,1)} %fusion.40.k_ref, bf16[1,1024,512]{2,1,0:T(8,128)(2,1)} %fusion.41.v_ref, ...), custom_call_target="tpu_custom_call" | custom-call | tf_op jit(solution)/shard_map/attend/pallas_call | solution.py:259
  51.2 5.6 convolution_convert_fusion.3
  56.9 158.5 %all-reduce.4.cloned.1.call-done = bf16[1024,2048]{1,0:T(8,128)(2,1)} async-done(((bf16[1024,2048]{1,0:T(8,128)(2,1)}), bf16[1024,2048]{1,0:T(8,128)(2,1)}) %all-reduce.4.cloned.1.call-update) | async-done | bytes 4194320 | tf_op jit(solution)/shard_map/psum | solution.py:380
  215.4 5.0 multiply_reduce_fusion.1
  220.5 0.9 copy-done.5
  221.3 2.8 multiply_convert_fusion
  224.2 7.4 fusion.69
  231.6 7.4 fusion.70
  239.0 15.3 %multiply_convert_fusion.1 = (bf16[1024,1280]{1,0:T(8,128)(2,1)}, bf16[1024,1280]{1,0:T(8,128)(2,1)}, bf16[1024,1280]{1,0:T(8,128)(2,1)}) fusion(f32[1024,1280]{1,0:T(8,128)} %fusion.69, f32[1024,1280]{1,0:T(8,128)} %fusion.70, bf16[1280,2048]{1,0:T(8,128)(2,1)} %param.22, bf16[1,1024,2048]{2,1,0:T(8,128)(2,1)S(1)} %copy-done.10), kind=kOutput, calls=%fused_computation.27 | convolution fusion | flops 5402787840 | bytes 27787264 | tf_op jit(solution)/shard_map/dot_general | solution.py:39
  254.3 9.7 fusion.71
  264.0 9.6 add_convert_fusion.1
  273.7 154.1 %all-reduce.6.cloned.1.call-done = bf16[1024,2048]{1,0:T(8,128)(2,1)} async-done(((bf16[1024,2048]{1,0:T(8,128)(2,1)}), bf16[1024,2048]{1,0:T(8,128)(2,1)}) %all-reduce.6.cloned.1.call-update) | async-done | bytes 4194320 | tf_op jit(solution)/shard_map/psum | solution.py:392
  427.8 6.7 multiply_reduce_fusion
  434.5 0.3 copy-done.6
  434.9 9.3 multiply_add_fusion
  444.2 3.3 copy-done.7
  447.5 3.9 convolution_convert_fusion.4
  451.5 10.0 convolution_convert_fusion.1
  461.5 0.4 reduce-scatter.11.cloned.1.call-start
  462.0 7.1 fusion.42.grad_ref
  469.0 30.1 %attend_back.1 = (bf16[1,1024,512]{2,1,0:T(8,128)(2,1)}, bf16[1,1024,512]{2,1,0:T(8,128)(2,1)}, bf16[1,1024,512]{2,1,0:T(8,128)(2,1)}, f32[1,8,5,512]{3,2,1,0:T(8,128)}) custom-call(s32[4]{0:T(128)} %get-tuple-element.27.first_ref, s32[4]{0:T(128)} %broadcast_add_fusion.last_ref, bf16[1,1024,512]{2,1,0:T(8,128)(2,1)} %fusion.39.q_ref, ...), custom_call_target="tpu_custom_call" | custom-call | tf_op jit(solution)/shard_map/attend_back/pallas_call | solution.py:286
  499.1 11.5 %convolution_convert_fusion.2 = bf16[2048,1536]{1,0:T(8,128)(2,1)} fusion(bf16[1024,512]{1,0:T(8,128)(2,1)} %bitcast.115, bf16[1024,512]{1,0:T(8,128)(2,1)} %bitcast.127, bf16[1024,512]{1,0:T(8,128)(2,1)} %bitcast.128, bf16[1,1024,2048]{2,1,0:T(8,128)(2,1)} %param.13, f32[2048]{0:T(1024)S(1)} %copy-done.18, f32[1024]{0:T(1024)S(1)} %add_rsqrt_fusion.1), kind=kOutput, calls=%fused_computation.14 | convolution fusion | flops 6463422464 | bytes 13643776 | tf_op jit(solution)/shard_map/dot_general | solution.py:321
  510.7 17.2 %convolution_convert_fusion = bf16[2048,2560]{1,0:T(8,128)(2,1)} fusion(bf16[1024,2048]{1,0:T(8,128)(2,1)} %copy-done.8, bf16[1024,1280]{1,0:T(8,128)(2,1)} %get-tuple-element.32, bf16[1024,1280]{1,0:T(8,128)(2,1)} %get-tuple-element.33), kind=kOutput, calls=%fused_computation | convolution fusion | flops 10753146880 | bytes 19922944 | tf_op jit(solution)/shard_map/dot_general | solution.py:321
  528.0 10.2 convert_bitcast_fusion
  538.4 0.7 all-gather.7.cloned.1.call-update
  539.0 0.3 reduce-scatter.9.cloned.1.call-start
  539.3 2.4 fusion.60
  541.7 2.4 fusion.58
  544.1 5.6 fusion.13
  549.8 3.2 reduce-scatter.17.cloned.1.call-done
  553.1 65.5 %reduce-scatter.11.cloned.1.call-done = bf16[256,1536]{1,0:T(8,128)(2,1)} async-done(((bf16[2048,1536]{1,0:T(8,128)(2,1)}), bf16[256,1536]{1,0:T(8,128)(2,1)}) %reduce-scatter.11.cloned.1.call-update) | async-done | bytes 786448 | tf_op jit(solution)/shard_map/reduce_scatter | solution.py:429
  618.7 85.9 %reduce-scatter.15.cloned.1.call-done = bf16[256,2560]{1,0:T(8,128)(2,1)} async-done(((bf16[2048,2560]{1,0:T(8,128)(2,1)}), bf16[256,2560]{1,0:T(8,128)(2,1)}) %reduce-scatter.15.cloned.1.call-update) | async-done | bytes 1310736 | tf_op jit(solution)/shard_map/reduce_scatter | solution.py:429
  704.6 6.7 convert_element_type.194
  711.4 0.1 dynamic-slice.14
  711.5 6.7 convert_element_type.222
  718.2 0.2 fusion.49
  718.4 12.5 %psum.39 = f32[32,8]{0,1:T(8,128)} all-reduce(f32[32,8]{0,1:T(8,128)S(1)} %fusion.49), channel_id=1, replica_groups=mesh['dp'=8,'tensor'=4] {'dp'}, use_global_device_ids=true, to_apply=%region_18.19 | all-reduce | flops 256 | bytes 2048 | tf_op jit(solution)/shard_map/psum | solution.py:426
  730.9 54.0 %reduce-scatter.7.cloned.1.call-done = bf16[1,256,2048]{2,1,0:T(8,128)(2,1)} async-done(((bf16[1,1024,2048]{2,1,0:T(8,128)(2,1)}), bf16[1,256,2048]{2,1,0:T(8,128)(2,1)}) %reduce-scatter.7.cloned.1.call-update) | async-done | bytes 1048592 | tf_op jit(solution)/shard_map/reduce_scatter | solution.py:362
  784.9 4.0 multiply_reduce_fusion.2
  788.9 26.4 %all-gather.7.cloned.1.call-done = bf16[512,2048]{1,0:T(8,128)(2,1)} async-done(((bf16[512,256]{1,0:T(8,128)(2,1)}), bf16[512,2048]{1,0:T(8,128)(2,1)}) %all-gather.7.cloned.1.call-update) | async-done | bytes 2097168 | tf_op jit(solution)/shard_map/all_gather | solution.py:430
  815.3 4.1 convert_element_type.233
  819.5 75.7 %reduce-scatter.9.cloned.1.call-done = bf16[1,256,2048]{2,1,0:T(8,128)(2,1)} async-done(((bf16[1,1024,2048]{2,1,0:T(8,128)(2,1)}), bf16[1,256,2048]{2,1,0:T(8,128)(2,1)}) %reduce-scatter.9.cloned.1.call-update) | async-done | bytes 1048592 | tf_op jit(solution)/shard_map/reduce_scatter | solution.py:362
  895.2 2.5 fusion.29
  897.7 40.5 %all-reduce = (f32[2048]{0:T(1024)}, f32[2048]{0:T(1024)}) all-reduce(f32[2048]{0:T(1024)S(1)} %get-tuple-element.24, f32[2048]{0:T(1024)S(1)} %get-tuple-element.35), channel_id=1, replica_groups=mesh['dp'=8,'tensor'=4] {'dp','tensor'}, use_global_device_ids=true, to_apply=%region_15.16 | all-reduce | flops 4096 | bytes 32768 | tf_op jit(solution)/shard_map/psum | solution.py:425
  938.1 4.2 fusion.48
  942.3 8.0 convert_element_type.237
  950.3 37.7 %all-gather.5.cloned.1.call-done = bf16[2048,1536]{1,0:T(8,128)(2,1)} async-done(((bf16[256,1536]{1,0:T(8,128)(2,1)}), bf16[2048,1536]{1,0:T(8,128)(2,1)}) %all-gather.5.cloned.1.call-update) | async-done | bytes 6291472 | tf_op jit(solution)/shard_map/all_gather | solution.py:430
  988.0 8.1 fusion.67
  996.2 57.1 %all-gather.9.cloned.1.call-done = bf16[2048,2560]{1,0:T(8,128)(2,1)} async-done(((bf16[256,2560]{1,0:T(8,128)(2,1)}), bf16[2048,2560]{1,0:T(8,128)(2,1)}) %all-gather.9.cloned.1.call-update) | async-done | bytes 10485776 | tf_op jit(solution)/shard_map/all_gather | solution.py:430
  1053.2 13.4 %fusion.66 = (f32[2048,1280]{1,0:T(8,128)}, f32[2048,1280]{1,0:T(8,128)}) fusion(bf16[2048,2560]{1,0:T(8,128)(2,1)} %all-gather.9.cloned.1.call-done), kind=kLoop, calls=%fused_computation.99 | loop fusion | bytes 41943040 | tf_op jit(solution)/shard_map/split | solution.py:436
  (95 shorter events, 1.0 us)
Async XLA Ops:
  7.2 44.0 %copy-start = (bf16[512,2048]{1,0:T(8,128)(2,1)S(1)}, bf16[512,2048]{1,0:T(8,128)(2,1)}, u32[]{:S(2)}) copy-start(bf16[512,2048]{1,0:T(8,128)(2,1)} %param.19) | copy-start | bytes 6291460
  7.2 208.2 %all-reduce.4.cloned.1.call-start = ((), (), s32[]{:S(2)}) async-start(), calls=%async_computation.6 | async-start | bytes 8388608 | tf_op jit(solution)/shard_map/psum | solution.py:380
  13.7 6.4 copy-start.2
  13.7 6.4 copy-start.18
  13.8 6.4 copy-start.21
  20.2 3.4 copy-start.11
  23.5 3.4 copy-start.17
  23.5 4.5 copy-start.19
  28.1 0.9 copy-start.14
  56.8 163.6 %copy-start.16 = (f32[2048]{0:T(1024)S(1)}, f32[2048]{0:T(1024)}, u32[]{:S(2)}) copy-start(f32[2048]{0:T(1024)} %param.24) | copy-start | bytes 24580
  56.8 370.9 %all-reduce.6.cloned.1.call-start = ((), (), s32[]{:S(2)}) async-start(), calls=%async_computation.8 | async-start | bytes 8388608 | tf_op jit(solution)/shard_map/psum | solution.py:392
  215.4 5.1 copy-start.3
  215.4 5.9 copy-start.5
  215.4 8.8 slice-start
  221.3 2.9 slice-start.1
  221.3 10.3 slice-start.2
  224.2 7.4 copy-start.8
  224.2 7.4 slice-start.3
  231.6 7.4 copy-start.10
  254.2 9.7 copy-start.25
  273.6 264.7 %reduce-scatter.13.cloned.1.call-start = ((), (), s32[]{:S(2)}) async-start(), calls=%async_computation.12 | async-start | bytes 2359296 | tf_op jit(solution)/shard_map/reduce_scatter | solution.py:429
  427.8 6.8 copy-start.4
  427.8 7.1 copy-start.6
  434.9 12.6 %copy-start.9 = (bf16[1,1024,512]{2,1,0:T(8,128)(2,1)S(1)}, bf16[1,1024,512]{2,1,0:T(8,128)(2,1)}, u32[]{:S(2)}) copy-start(bf16[1,1024,512]{2,1,0:T(8,128)(2,1)} %get-tuple-element.18.out_ref) | copy-start | bytes 3145732
  444.2 3.3 copy-start.7
  451.4 101.6 %reduce-scatter.17.cloned.1.call-start = ((), (), s32[]{:S(2)}) async-start(), calls=%async_computation.16 | async-start | bytes 5898240 | tf_op jit(solution)/shard_map/reduce_scatter | solution.py:429
  461.5 157.1 %reduce-scatter.11.cloned.1.call-start = ((), (), s32[]{:S(2)}) async-start(), calls=%async_computation.10 | async-start | bytes 7077888 | tf_op jit(solution)/shard_map/reduce_scatter | solution.py:429
  510.7 193.9 %reduce-scatter.15.cloned.1.call-start = ((), (), s32[]{:S(2)}) async-start(), calls=%async_computation.14 | async-start | bytes 11796480 | tf_op jit(solution)/shard_map/reduce_scatter | solution.py:429
  527.9 11.3 %copy-start.20 = (bf16[2048,512]{1,0:T(8,128)(2,1)S(1)}, bf16[2048,512]{1,0:T(8,128)(2,1)}, u32[]{:S(2)}) copy-start(bf16[2048,512]{1,0:T(8,128)(2,1)} %param.16) | copy-start | bytes 6291460
  528.0 11.3 %copy-start.24 = (bf16[1,1024,512]{2,1,0:T(8,128)(2,1)S(1)}, bf16[1,1024,512]{2,1,0:T(8,128)(2,1)}, u32[]{:S(2)}) copy-start(bf16[1,1024,512]{2,1,0:T(8,128)(2,1)} %get-tuple-element.20) | copy-start | bytes 3145732
  528.0 256.9 %reduce-scatter.7.cloned.1.call-start = ((), (), s32[]{:S(2)}) async-start(), calls=%async_computation.7 | async-start | bytes 5242880 | tf_op jit(solution)/shard_map/reduce_scatter | solution.py:362
  538.3 277.1 %all-gather.7.cloned.1.call-start = ((), (), s32[]{:S(2)}) async-start(), calls=%async_computation.13 | async-start | bytes 2359296 | tf_op jit(solution)/shard_map/all_gather | solution.py:430
  539.0 356.1 %reduce-scatter.9.cloned.1.call-start = ((), (), s32[]{:S(2)}) async-start(), calls=%async_computation.9 | async-start | bytes 5242880 | tf_op jit(solution)/shard_map/reduce_scatter | solution.py:362
  539.3 2.4 copy-start.22
  539.3 2.4 copy-start.23
  541.7 2.4 copy-start.12
  549.8 392.5 %all-gather.11.cloned.1.call-start = ((), (), s32[]{:S(2)}) async-start(), calls=%async_computation.17 | async-start | bytes 5898240 | tf_op jit(solution)/shard_map/all_gather | solution.py:430
  553.1 434.9 %all-gather.5.cloned.1.call-start = ((), (), s32[]{:S(2)}) async-start(), calls=%async_computation.11 | async-start | bytes 7077888 | tf_op jit(solution)/shard_map/all_gather | solution.py:430
  618.6 434.6 %all-gather.9.cloned.1.call-start = ((), (), s32[]{:S(2)}) async-start(), calls=%async_computation.15 | async-start | bytes 11796480 | tf_op jit(solution)/shard_map/all_gather | solution.py:430
  704.6 6.9 copy-start.13
  711.5 6.7 copy-start.15
  1053.2 13.4 %copy-start.1 = (bf16[512,2048]{1,0:T(8,128)(2,1)S(1)}, bf16[512,2048]{1,0:T(8,128)(2,1)}, u32[]{:S(2)}) copy-start(bf16[512,2048]{1,0:T(8,128)(2,1)} %param.19) | copy-start | bytes 6291460
Sparse Core Ops, SparseCore 0:
  56.9 158.4 all-reduce.3
  273.8 153.9 all-reduce.5
  451.5 41.2 reduce-scatter.12
  496.4 56.6 reduce-scatter.16
  556.8 61.7 reduce-scatter.10
  623.0 81.5 reduce-scatter.14
  707.5 77.3 reduce-scatter.6
  786.8 28.5 all-gather.6
  818.2 76.8 reduce-scatter.8
  897.0 43.3 all-gather.10
  942.5 45.5 all-gather.4
  989.9 63.2 all-gather.8

commit v2 on v1

--- a/solution.py
+++ b/solution.py
@@ -12,6 +12,7 @@
 tile = 256
 kinds = 5
 group_pairs = 1
+line_chunks = 8
 lanes = 128
 bf16 = jnp.bfloat16
 f32 = jnp.float32
@@ -309,6 +310,130 @@
     )
 
 
+mesh_ids = pl.DeviceIdType.MESH
+
+
+def greet_line(me, count, axis):
+    barrier = pltpu.get_barrier_semaphore()
+    has_left, has_right = me > 0, me < count - 1
+    for there, step in ((has_left, -1), (has_right, 1)):
+        @pl.when(there)
+        def _():
+            pl.semaphore_signal(barrier, inc=1, device_id={axis: me + step}, device_id_type=mesh_ids)
+    pl.semaphore_wait(barrier, has_left.astype(jnp.int32) + has_right.astype(jnp.int32))
+
+
+def add_low(left_side, right_side):
+    return (left_side.astype(f32) + right_side.astype(f32)).astype(bf16)
+
+
+def line_sum_kernel(axis, count, chunks, part_ref, out_ref, land_ref, sum_ref, send_sem, recv_sem, bsend_sem, brecv_sem):
+    me = lax.axis_index(axis)
+    tokens = part_ref.shape[0]
+    size = tokens // (2 * chunks)
+    greet_line(me, count, axis)
+
+    def rows(flow, chunk):
+        return pl.ds(pl.multiple_of((flow * chunks + chunk) * size, size), size)
+
+    def toward(flow):
+        return me + 1 if flow == 0 else me - 1
+
+    def back(flow):
+        return me - 1 if flow == 0 else me + 1
+
+    def place(flow):
+        return me if flow == 0 else count - 1 - me
+
+    def sum_copy(flow, chunk, source_ref):
+        here = rows(flow, chunk)
+        return pltpu.make_async_remote_copy(
+            src_ref=source_ref.at[here], dst_ref=land_ref.at[here],
+            send_sem=send_sem.at[flow, chunk], recv_sem=recv_sem.at[flow, chunk],
+            device_id={axis: toward(flow)}, device_id_type=mesh_ids,
+        )
+
+    def out_copy(flow, chunk):
+        here = rows(flow, chunk)
+        return pltpu.make_async_remote_copy(
+            src_ref=out_ref.at[here], dst_ref=out_ref.at[here],
+            send_sem=bsend_sem.at[flow, chunk], recv_sem=brecv_sem.at[flow, chunk],
+            device_id={axis: back(flow)}, device_id_type=mesh_ids,
+        )
+
+    def step(time, carry):
+        for flow in range(2):
+            chunk = time - place(flow)
+            here = rows(flow, chunk)
+            valid = (chunk >= 0) & (chunk < chunks)
+
+            @pl.when(valid & (place(flow) == 0))
+            def _():
+                sum_copy(flow, chunk, part_ref).start()
+
+            @pl.when(valid & (place(flow) > 0))
+            def _():
+                sum_copy(flow, chunk, sum_ref).wait_recv()
+
+            @pl.when(valid & (place(flow) > 0) & (place(flow) < count - 1))
+            def _():
+                sum_ref[here, :] = add_low(land_ref[here, :], part_ref[here, :])
+                sum_copy(flow, chunk, sum_ref).start()
+
+            @pl.when(valid & (place(flow) == count - 1))
+            def _():
+                out_ref[here, :] = add_low(land_ref[here, :], part_ref[here, :])
+                out_copy(flow, chunk).start()
+        for flow in range(2):
+            chunk = time - 2 * (count - 1) + place(flow)
+            valid = (chunk >= 0) & (chunk < chunks) & (place(flow) < count - 1)
+
+            @pl.when(valid)
+            def _():
+                out_copy(flow, chunk).wait_recv()
+
+            @pl.when(valid & (place(flow) > 0))
+            def _():
+                out_copy(flow, chunk).start()
+        return carry
+
+    lax.fori_loop(0, chunks + 2 * (count - 1), step, 0)
+
+    def drain(chunk, carry):
+        for flow in range(2):
+            @pl.when(place(flow) < count - 1)
+            def _():
+                sum_copy(flow, chunk, part_ref).wait_send()
+
+            @pl.when(place(flow) > 0)
+            def _():
+                out_copy(flow, chunk).wait_send()
+        return carry
+
+    lax.fori_loop(0, chunks, drain, 0)
+
+
+def line_sum(part, axis, chunks, cid):
+    count = lax.axis_size(axis)
+    tokens, width = part.shape
+    return pl.pallas_call(
+        functools.partial(line_sum_kernel, axis, count, chunks),
+        out_shape=jax.ShapeDtypeStruct(part.shape, bf16),
+        in_specs=[pl.BlockSpec(memory_space=pltpu.VMEM)],
+        out_specs=pl.BlockSpec(memory_space=pltpu.VMEM),
+        scratch_shapes=[
+            pltpu.VMEM(part.shape, bf16),
+            pltpu.VMEM(part.shape, bf16),
+            pltpu.SemaphoreType.DMA((2, chunks)),
+            pltpu.SemaphoreType.DMA((2, chunks)),
+            pltpu.SemaphoreType.DMA((2, chunks)),
+            pltpu.SemaphoreType.DMA((2, chunks)),
+        ],
+        compiler_params=pltpu.CompilerParams(collective_id=cid, has_side_effects=True),
+        name="line_sum",
+    )(part)
+
+
 def project(left_side, right_side):
     return jnp.dot(left_side, right_side, preferred_element_type=f32)
 
@@ -377,7 +502,7 @@
     mixed, totals = attend(queries, keys, values, segments, lines)
     mixed_flat = mixed.reshape(token_count, local_width)
     attn_part = project(mixed_flat, w_out)
-    attn_total = lax.psum(attn_part.astype(bf16), "tensor").astype(f32)
+    attn_total = line_sum(attn_part.astype(bf16), "tensor", line_chunks, 0).astype(f32)
     grad_hidden = project_back(grad_out, w_down)
     middle = flat_inputs + attn_total
     scale_ffn = norm_scale(middle)
@@ -389,7 +514,7 @@
     grad_gate = act_pull(grad_hidden * up_pre)[0].astype(bf16)
     grad_up = (grad_hidden * act_value).astype(bf16)
     norm_ffn_part = project_back(grad_gate, w_gate) + project_back(grad_up, w_up)
-    grad_normed_ffn = lax.psum(norm_ffn_part.astype(bf16), "tensor").astype(f32)
+    grad_normed_ffn = line_sum(norm_ffn_part.astype(bf16), "tensor", line_chunks, 0).astype(f32)
     ffn_share = scatter(project(hidden, w_down))
     middle_share = take_share(middle)
     output = (middle_share + ffn_share).reshape(share_shape).astype(bf16)

time: 1080 us -> 1000 us (0.926)
  waiting for transfers between devices: 719 us -> 405 us
  Pallas kernels: 52.3 us -> 289 us
    psum x2 -> x0, waiting for transfers between devices: 313 us -> none  [the longest x1 159 us: shards(): attn_total = lax.psum(attn_part.astype(bf16), 'tensor').astype(f32)]
    pallas_call x0 -> x2, Pallas kernels: none -> 228 us  [line_sum(): pl.pallas_call(functools.partial(line_sum_kernel, axis, count, chunks), o...]
    reduce_scatter x2, waiting for transfers between devices: 130 us -> 152 us  [scatter(): lax.psum_scatter(part.astype(bf16).reshape(plane), 'tensor', scatter_dime...]
    all_gather x4, waiting for transfers between devices: 121 us -> 101 us  [reduce_all(): return lax.all_gather(part, 'dp', axis=axis, tiled=True)]
  transfers between devices with their start and end apart: 12 -> 10, of which waited for: 10 -> 8; matrix products, arithmetic and copies ran while one was open for 10% -> 11% of each run, Pallas kernels for 3% -> 3%
where the time goes in v2:
time: 1000 us; the launch traced here: 997 us
  waiting for transfers between devices  405 us (40%)
  Pallas kernels  289 us (29%)
  matrix products  143 us (14%)
  other arithmetic  64.5 us (6%)
  blocking collectives  52.9 us (5%)
  local copies, waits for them, and re-layouts  26.8 us (3%)
  between operations  15.1 us (2%)
    pallas_call x2, Pallas kernels, line_sum(): pl.pallas_call(functools.partial(line_sum_kernel, axis, count, chunks), o...  228 us
    reduce_scatter x2, waiting for transfers between devices, scatter(): lax.psum_scatter(part.astype(bf16).reshape(plane), 'tensor', scatter_dime...  152 us
    reduce_scatter x4, waiting for transfers between devices, reduce_all(): part = lax.psum_scatter(grad, 'dp', scatter_dimension=axis, tiled=True)  151 us
    all_gather x4, waiting for transfers between devices, reduce_all(): return lax.all_gather(part, 'dp', axis=axis, tiled=True)  101 us
    dot_general x7, matrix products, dot_nt(): lax.dot_general(left_side, right_side, (((1,), (1,)), ((), ())), preferre...  52.6 us
    dot_general x4, matrix products, weight_term(): lax.dot_general(left_side, right_side, (((0,), (0,)), ((), ())), preferre...  46.3 us
    dot_general x7, matrix products, project(): return jnp.dot(left_side, right_side, preferred_element_type=f32)  43.7 us
    psum x1, blocking collectives, shards(): lax.psum((gain_attn_part, gain_ffn_part), ('dp', 'tensor'))  40.5 us
  transfers between devices with their start and end apart: 10, of which 8 were waited for; matrix products, arithmetic and copies ran while one was open for 11% of the time, Pallas kernels for 3%

profile of v2, /device:TPU:17, one launch (start us, length us, event | category | flops | bytes accessed | tf_op | source)
XLA Modules:
  0.0 996.9 jit_solution(11898181051956181071)
XLA Ops:
  7.3 0.5 broadcast.304
  7.8 1.4 reduce.5
  9.3 0.1 copy.40
  9.3 0.1 copy.39
  9.4 0.7 convert_reduce_fusion
  10.1 0.5 broadcast_add_fusion.last_ref
  10.6 3.1 fusion
  13.8 6.4 fusion.39.q_ref
  20.2 3.4 fusion.40.k_ref
  23.5 3.4 fusion.41.v_ref
  26.9 1.0 copy.35.seg_col_ref
  28.0 0.1 subtract_abs_fusion
  28.1 0.2 fusion.50
  28.3 0.7 copy.36.line_ref
  29.0 25.8 %attend.1 = (bf16[1,1024,512]{2,1,0:T(8,128)(2,1)}, f32[1,4,2,1024]{3,2,1,0:T(2,128)}) custom-call(s32[4]{0:T(128)} %get-tuple-element.27.first_ref, s32[4]{0:T(128)} %broadcast_add_fusion.last_ref, bf16[1,1024,512]{2,1,0:T(8,128)(2,1)} %fusion.39.q_ref, bf16[1,1024,512]{2,1,0:T(8,128)(2,1)} %fusion.40.k_ref, bf16[1,1024,512]{2,1,0:T(8,128)(2,1)} %fusion.41.v_ref, ...), custom_call_target="tpu_custom_call" | custom-call | tf_op jit(solution)/shard_map/attend/pallas_call | solution.py:260
  54.9 5.6 convolution_convert_fusion.3.part_ref
  60.4 115.7 %line_sum.2 = bf16[1024,2048]{1,0:T(8,128)(2,1)} custom-call(bf16[1024,2048]{1,0:T(8,128)(2,1)} %convolution_convert_fusion.3.part_ref), custom_call_target="tpu_custom_call" | custom-call | tf_op jit(solution)/shard_map/line_sum/pallas_call | solution.py:419
  176.1 5.0 multiply_reduce_fusion.1
  181.2 0.8 copy-done.6
  182.0 2.7 multiply_convert_fusion
  184.8 7.4 fusion.69
  192.2 7.4 fusion.70
  199.5 15.3 %multiply_convert_fusion.1 = (bf16[1024,1280]{1,0:T(8,128)(2,1)}, bf16[1024,1280]{1,0:T(8,128)(2,1)}, bf16[1024,1280]{1,0:T(8,128)(2,1)}) fusion(f32[1024,1280]{1,0:T(8,128)} %fusion.69, f32[1024,1280]{1,0:T(8,128)} %fusion.70, bf16[1280,2048]{1,0:T(8,128)(2,1)} %param.22, bf16[1,1024,2048]{2,1,0:T(8,128)(2,1)S(1)} %copy-done.11), kind=kOutput, calls=%fused_computation.27 | convolution fusion | flops 5402787840 | bytes 27787264 | tf_op jit(solution)/shard_map/dot_general | solution.py:40
  214.8 10.4 %fusion.71 = f32[1024,2048]{1,0:T(8,128)} fusion(bf16[1024,1280]{1,0:T(8,128)(2,1)} %get-tuple-element.33, bf16[2048,1280]{1,0:T(8,128)(2,1)S(1)} %bitcast.124), kind=kOutput, calls=%fused_computation.104 | convolution fusion | flops 5368709120 | bytes 16252928 | tf_op jit(solution)/shard_map/dot_general | solution.py:40
  225.2 9.4 add_convert_fusion.1.part_ref
  234.6 112.6 %line_sum.3 = bf16[1024,2048]{1,0:T(8,128)(2,1)} custom-call(bf16[1024,2048]{1,0:T(8,128)(2,1)} %add_convert_fusion.1.part_ref), custom_call_target="tpu_custom_call" | custom-call | tf_op jit(solution)/shard_map/line_sum/pallas_call | solution.py:419
  347.3 6.7 multiply_reduce_fusion
  354.1 0.3 copy-done.7
  354.4 1.2 copy-done.8
  355.6 10.2 %multiply_add_fusion = (f32[1024,2048]{1,0:T(8,128)}, f32[1024,2048]{1,0:T(8,128)}) fusion(bf16[1,1024,2048]{2,1,0:T(8,128)(2,1)} %param.15, f32[1024]{0:T(1024)S(1)} %broadcast_multiply_fusion, bf16[1024,2048]{1,0:T(8,128)(2,1)S(1)} %copy-done.8, f32[2048]{0:T(1024)S(1)} %copy-done.17, f32[1024]{0:T(1024)S(1)} %add_rsqrt_fusion, ...), kind=kLoop, calls=%fused_computation.8 | loop fusion | flops 25165824 | bytes 33570816 | tf_op jit(solution)/shard_map/add | solution.py:523
  365.8 7.1 convolution_convert_fusion.4
  372.9 10.1 %convolution_convert_fusion.1 = bf16[1280,2048]{1,0:T(8,128)(2,1)} fusion(bf16[1024,1280]{1,0:T(8,128)(2,1)} %get-tuple-element.34, bf16[1,1024,2048]{2,1,0:T(8,128)(2,1)} %param.15), kind=kOutput, calls=%fused_computation.13 | convolution fusion | flops 5371330560 | bytes 12058624 | tf_op jit(solution)/shard_map/dot_general | solution.py:446
  383.1 7.1 fusion.42.grad_ref
  390.2 34.9 %attend_back.1 = (bf16[1,1024,512]{2,1,0:T(8,128)(2,1)}, bf16[1,1024,512]{2,1,0:T(8,128)(2,1)}, bf16[1,1024,512]{2,1,0:T(8,128)(2,1)}, f32[1,8,5,512]{3,2,1,0:T(8,128)}) custom-call(s32[4]{0:T(128)} %get-tuple-element.27.first_ref, s32[4]{0:T(128)} %broadcast_add_fusion.last_ref, bf16[1,1024,512]{2,1,0:T(8,128)(2,1)} %fusion.39.q_ref, ...), custom_call_target="tpu_custom_call" | custom-call | tf_op jit(solution)/shard_map/attend_back/pallas_call | solution.py:287
  425.1 12.0 %convolution_convert_fusion.2 = bf16[2048,1536]{1,0:T(8,128)(2,1)} fusion(bf16[1024,512]{1,0:T(8,128)(2,1)} %bitcast.115, bf16[1024,512]{1,0:T(8,128)(2,1)} %bitcast.127, bf16[1024,512]{1,0:T(8,128)(2,1)} %bitcast.128, bf16[1,1024,2048]{2,1,0:T(8,128)(2,1)} %param.13, f32[2048]{0:T(1024)S(1)} %copy-done.19, f32[1024]{0:T(1024)S(1)} %add_rsqrt_fusion.1), kind=kOutput, calls=%fused_computation.14 | convolution fusion | flops 6463422464 | bytes 13643776 | tf_op jit(solution)/shard_map/dot_general | solution.py:446
  437.2 17.1 %convolution_convert_fusion = bf16[2048,2560]{1,0:T(8,128)(2,1)} fusion(bf16[1024,2048]{1,0:T(8,128)(2,1)} %copy-done.9, bf16[1024,1280]{1,0:T(8,128)(2,1)} %get-tuple-element.32, bf16[1024,1280]{1,0:T(8,128)(2,1)} %get-tuple-element.33), kind=kOutput, calls=%fused_computation | convolution fusion | flops 10753146880 | bytes 19922944 | tf_op jit(solution)/shard_map/dot_general | solution.py:446
  454.4 0.5 all-gather.7.cloned.1.call-update
  454.9 10.2 %convert_bitcast_fusion = bf16[1,1024,2048]{2,1,0:T(8,128)(2,1)} fusion(bf16[1024,1280]{1,0:T(8,128)(2,1)} %get-tuple-element.34, bf16[1280,2048]{1,0:T(8,128)(2,1)} %param.22), kind=kOutput, calls=%fused_computation.34 | convolution fusion | flops 5370806272 | bytes 12058624 | tf_op jit(solution)/shard_map/dot_general | solution.py:438
  465.2 0.3 reduce-scatter.9.cloned.1.call-start
  465.5 2.4 fusion.60
  468.0 2.4 fusion.58
  470.3 5.6 fusion.13
  476.0 0.4 reduce-scatter.17.cloned.1.call-done
  476.4 0.3 all-gather.11.cloned.1.call-update
  476.8 64.8 %reduce-scatter.11.cloned.1.call-done = bf16[256,1536]{1,0:T(8,128)(2,1)} async-done(((bf16[2048,1536]{1,0:T(8,128)(2,1)}), bf16[256,1536]{1,0:T(8,128)(2,1)}) %reduce-scatter.11.cloned.1.call-update) | async-done | bytes 786448 | tf_op jit(solution)/shard_map/reduce_scatter | solution.py:554
  541.7 85.9 %reduce-scatter.15.cloned.1.call-done = bf16[256,2560]{1,0:T(8,128)(2,1)} async-done(((bf16[2048,2560]{1,0:T(8,128)(2,1)}), bf16[256,2560]{1,0:T(8,128)(2,1)}) %reduce-scatter.15.cloned.1.call-update) | async-done | bytes 1310736 | tf_op jit(solution)/shard_map/reduce_scatter | solution.py:554
  627.6 6.8 convert_element_type.222
  634.4 4.4 convert_element_type.194
  638.8 0.1 dynamic-slice.14
  639.0 0.2 fusion.49
  639.2 12.4 %psum.23 = f32[32,8]{0,1:T(8,128)} all-reduce(f32[32,8]{0,1:T(8,128)S(1)} %fusion.49), channel_id=1, replica_groups=mesh['dp'=8,'tensor'=4] {'dp'}, use_global_device_ids=true, to_apply=%region_16.17 | all-reduce | flops 256 | bytes 2048 | tf_op jit(solution)/shard_map/psum | solution.py:551
  651.6 6.5 all-gather.7.cloned.1.call-done
  658.1 4.1 convert_element_type.233
  662.2 75.6 %reduce-scatter.7.cloned.1.call-done = bf16[1,256,2048]{2,1,0:T(8,128)(2,1)} async-done(((bf16[1,1024,2048]{2,1,0:T(8,128)(2,1)}), bf16[1,256,2048]{2,1,0:T(8,128)(2,1)}) %reduce-scatter.7.cloned.1.call-update) | async-done | bytes 1048592 | tf_op jit(solution)/shard_map/reduce_scatter | solution.py:487
  737.8 4.0 multiply_reduce_fusion.2
  741.9 76.1 %reduce-scatter.9.cloned.1.call-done = bf16[1,256,2048]{2,1,0:T(8,128)(2,1)} async-done(((bf16[1,1024,2048]{2,1,0:T(8,128)(2,1)}), bf16[1,256,2048]{2,1,0:T(8,128)(2,1)}) %reduce-scatter.9.cloned.1.call-update) | async-done | bytes 1048592 | tf_op jit(solution)/shard_map/reduce_scatter | solution.py:487
  818.0 2.5 fusion.29
  820.5 40.5 %all-reduce = (f32[2048]{0:T(1024)}, f32[2048]{0:T(1024)}) all-reduce(f32[2048]{0:T(1024)S(1)} %get-tuple-element.24, f32[2048]{0:T(1024)S(1)} %get-tuple-element.35), channel_id=1, replica_groups=mesh['dp'=8,'tensor'=4] {'dp','tensor'}, use_global_device_ids=true, to_apply=%region_13.14 | all-reduce | flops 4096 | bytes 32768 | tf_op jit(solution)/shard_map/psum | solution.py:550
  861.0 4.2 fusion.48
  865.2 8.0 convert_element_type.237
  873.2 37.8 %all-gather.5.cloned.1.call-done = bf16[2048,1536]{1,0:T(8,128)(2,1)} async-done(((bf16[256,1536]{1,0:T(8,128)(2,1)}), bf16[2048,1536]{1,0:T(8,128)(2,1)}) %all-gather.5.cloned.1.call-update) | async-done | bytes 6291472 | tf_op jit(solution)/shard_map/all_gather | solution.py:555
  911.0 8.1 fusion.67
  919.2 57.0 %all-gather.9.cloned.1.call-done = bf16[2048,2560]{1,0:T(8,128)(2,1)} async-done(((bf16[256,2560]{1,0:T(8,128)(2,1)}), bf16[2048,2560]{1,0:T(8,128)(2,1)}) %all-gather.9.cloned.1.call-update) | async-done | bytes 10485776 | tf_op jit(solution)/shard_map/all_gather | solution.py:555
  976.2 13.4 %fusion.66 = (f32[2048,1280]{1,0:T(8,128)}, f32[2048,1280]{1,0:T(8,128)}) fusion(bf16[2048,2560]{1,0:T(8,128)(2,1)} %all-gather.9.cloned.1.call-done), kind=kLoop, calls=%fused_computation.99 | loop fusion | bytes 41943040 | tf_op jit(solution)/shard_map/split | solution.py:561
  (93 shorter events, 0.9 us)
Async XLA Ops:
  7.2 47.7 %copy-start = (bf16[512,2048]{1,0:T(8,128)(2,1)S(1)}, bf16[512,2048]{1,0:T(8,128)(2,1)}, u32[]{:S(2)}) copy-start(bf16[512,2048]{1,0:T(8,128)(2,1)} %param.19) | copy-start | bytes 6291460
  7.2 447.2 %reduce-scatter.13.cloned.1.call-start = ((), (), s32[]{:S(2)}) async-start(), calls=%async_computation.10 | async-start | bytes 2359296 | tf_op jit(solution)/shard_map/reduce_scatter | solution.py:554
  13.7 6.4 copy-start.2
  13.7 6.4 copy-start.19
  13.8 6.4 copy-start.22
  20.2 3.4 copy-start.12
  23.5 3.4 copy-start.18
  23.5 4.5 copy-start.20
  28.1 0.9 copy-start.15
  176.1 5.1 copy-start.3
  176.1 5.9 copy-start.6
  176.1 5.9 copy-start.17
  176.1 8.6 slice-start
  182.0 2.7 slice-start.1
  182.0 10.1 %slice-start.2 = ((s8[5242880]{0:T(1024)(128)(4,1)}), s8[4194304]{0:T(1024)(128)(4,1)S(1)}, s32[]{:S(2)}) async-start(s8[5242880]{0:T(1024)(128)(4,1)} %bitcast.125), calls=%async_computation.18 | async-start | bytes 8388608
  184.7 7.4 copy-start.9
  184.8 7.4 slice-start.3
  192.1 7.4 copy-start.11
  214.8 10.4 %copy-start.26 = (bf16[1024,1280]{1,0:T(8,128)(2,1)S(1)}, bf16[1024,1280]{1,0:T(8,128)(2,1)}, u32[]{:S(2)}) copy-start(bf16[1024,1280]{1,0:T(8,128)(2,1)} %get-tuple-element.32) | copy-start | bytes 7864324
  347.3 6.8 copy-start.4
  347.3 7.1 copy-start.7
  347.3 8.3 copy-start.8
  355.6 10.2 %copy-start.10 = (bf16[1,1024,512]{2,1,0:T(8,128)(2,1)S(1)}, bf16[1,1024,512]{2,1,0:T(8,128)(2,1)}, u32[]{:S(2)}) copy-start(bf16[1,1024,512]{2,1,0:T(8,128)(2,1)} %get-tuple-element.18.out_ref) | copy-start | bytes 3145732
  372.8 103.6 %reduce-scatter.17.cloned.1.call-start = ((), (), s32[]{:S(2)}) async-start(), calls=%async_computation.14 | async-start | bytes 5898240 | tf_op jit(solution)/shard_map/reduce_scatter | solution.py:554
  383.1 158.6 %reduce-scatter.11.cloned.1.call-start = ((), (), s32[]{:S(2)}) async-start(), calls=%async_computation.8 | async-start | bytes 7077888 | tf_op jit(solution)/shard_map/reduce_scatter | solution.py:554
  437.1 190.4 %reduce-scatter.15.cloned.1.call-start = ((), (), s32[]{:S(2)}) async-start(), calls=%async_computation.12 | async-start | bytes 11796480 | tf_op jit(solution)/shard_map/reduce_scatter | solution.py:554
  454.3 203.8 %all-gather.7.cloned.1.call-start = ((), (), s32[]{:S(2)}) async-start(), calls=%async_computation.11 | async-start | bytes 2359296 | tf_op jit(solution)/shard_map/all_gather | solution.py:555
  454.9 10.6 %copy-start.21 = (bf16[2048,512]{1,0:T(8,128)(2,1)S(1)}, bf16[2048,512]{1,0:T(8,128)(2,1)}, u32[]{:S(2)}) copy-start(bf16[2048,512]{1,0:T(8,128)(2,1)} %param.16) | copy-start | bytes 6291460
  454.9 10.6 %copy-start.25 = (bf16[1,1024,512]{2,1,0:T(8,128)(2,1)S(1)}, bf16[1,1024,512]{2,1,0:T(8,128)(2,1)}, u32[]{:S(2)}) copy-start(bf16[1,1024,512]{2,1,0:T(8,128)(2,1)} %get-tuple-element.20) | copy-start | bytes 3145732
  454.9 283.0 %reduce-scatter.7.cloned.1.call-start = ((), (), s32[]{:S(2)}) async-start(), calls=%async_computation.6 | async-start | bytes 5242880 | tf_op jit(solution)/shard_map/reduce_scatter | solution.py:487
  465.2 352.8 %reduce-scatter.9.cloned.1.call-start = ((), (), s32[]{:S(2)}) async-start(), calls=%async_computation.7 | async-start | bytes 5242880 | tf_op jit(solution)/shard_map/reduce_scatter | solution.py:487
  465.5 2.4 copy-start.23
  465.5 2.4 copy-start.24
  467.9 2.4 copy-start.13
  476.0 389.2 %all-gather.11.cloned.1.call-start = ((), (), s32[]{:S(2)}) async-start(), calls=%async_computation.15 | async-start | bytes 5898240 | tf_op jit(solution)/shard_map/all_gather | solution.py:555
  476.7 434.3 %all-gather.5.cloned.1.call-start = ((), (), s32[]{:S(2)}) async-start(), calls=%async_computation.9 | async-start | bytes 7077888 | tf_op jit(solution)/shard_map/all_gather | solution.py:555
  541.6 434.6 %all-gather.9.cloned.1.call-start = ((), (), s32[]{:S(2)}) async-start(), calls=%async_computation.13 | async-start | bytes 11796480 | tf_op jit(solution)/shard_map/all_gather | solution.py:555
  627.6 6.8 copy-start.5
  634.4 4.5 copy-start.14
  634.4 4.6 copy-start.16
  976.2 13.4 %copy-start.1 = (bf16[512,2048]{1,0:T(8,128)(2,1)S(1)}, bf16[512,2048]{1,0:T(8,128)(2,1)}, u32[]{:S(2)}) copy-start(bf16[512,2048]{1,0:T(8,128)(2,1)} %param.19) | copy-start | bytes 6291460
Sparse Core Ops, SparseCore 0:
  373.0 43.0 reduce-scatter.12
  419.8 56.5 reduce-scatter.16
  479.8 61.7 reduce-scatter.10
  545.9 81.5 reduce-scatter.14
  629.4 28.6 all-gather.6
  660.9 76.8 reduce-scatter.6
  740.7 77.2 reduce-scatter.8
  820.0 43.3 all-gather.10
  865.5 45.5 all-gather.4
  912.9 63.2 all-gather.8

commit v3 on v2

--- a/solution.py
+++ b/solution.py
@@ -13,6 +13,9 @@
 kinds = 5
 group_pairs = 1
 line_chunks = 8
+tail_columns = 256
+tail_subs = 4
+tail_lag = 2
 lanes = 128
 bf16 = jnp.bfloat16
 f32 = jnp.float32
@@ -323,10 +326,6 @@
     pl.semaphore_wait(barrier, has_left.astype(jnp.int32) + has_right.astype(jnp.int32))
 
 
-def add_low(left_side, right_side):
-    return (left_side.astype(f32) + right_side.astype(f32)).astype(bf16)
-
-
 def line_sum_kernel(axis, count, chunks, part_ref, out_ref, land_ref, sum_ref, send_sem, recv_sem, bsend_sem, brecv_sem):
     me = lax.axis_index(axis)
     tokens = part_ref.shape[0]
@@ -434,6 +433,459 @@
     )(part)
 
 
+def add_low(left_side, right_side):
+    return (left_side.astype(f32) + right_side.astype(f32)).astype(bf16)
+
+
+def greet(line_axis, line_count, cube_axis, cube_bits):
+    barrier = pltpu.get_barrier_semaphore()
+    peers = 0
+    if line_count > 1:
+        me = lax.axis_index(line_axis)
+        for there, step in ((me > 0, -1), (me < line_count - 1, 1)):
+            @pl.when(there)
+            def _():
+                pl.semaphore_signal(
+                    barrier, inc=1, device_id={line_axis: me + step}, device_id_type=mesh_ids
+                )
+            peers = peers + there.astype(jnp.int32)
+    if cube_bits:
+        me = lax.axis_index(cube_axis)
+        for bit in range(cube_bits):
+            pl.semaphore_signal(
+                barrier, inc=1, device_id={cube_axis: cube_peer(me, bit)}, device_id_type=mesh_ids
+            )
+        peers = peers + cube_bits
+    pl.semaphore_wait(barrier, peers)
+
+
+def bit_of(place, bit):
+    return place // 2**bit % 2
+
+
+def cube_peer(place, bit):
+    return place + (1 - 2 * bit_of(place, bit)) * 2**bit
+
+
+class LineScatter:
+    def __init__(self, axis, count, subs, part_ref, share_ref, land_ref, send_sem, recv_sem):
+        self.axis, self.count, self.subs = axis, count, subs
+        self.part_ref, self.share_ref, self.land_ref = part_ref, share_ref, land_ref
+        self.send_sem, self.recv_sem = send_sem, recv_sem
+        self.me = lax.axis_index(axis)
+        self.share = part_ref.shape[0] // count
+        self.size = self.share // subs
+        self.length = (count - 1) * subs
+        self.steps = self.length + count - 1
+
+    @staticmethod
+    def scratch(count, subs, shape):
+        items = (2, (count - 1) * subs)
+        return [
+            pltpu.VMEM((2,) + shape, bf16),
+            pltpu.SemaphoreType.DMA(items),
+            pltpu.SemaphoreType.DMA(items),
+        ]
+
+    def place(self, flow):
+        return self.me if flow == 0 else self.count - 1 - self.me
+
+    def owner(self, flow, item):
+        return self.count - 1 - item // self.subs
+
+    def rows(self, flow, item):
+        along = self.owner(flow, item)
+        owner = along if flow == 0 else self.count - 1 - along
+        start = owner * self.share + item % self.subs * self.size
+        return pl.ds(pl.multiple_of(start, self.size), self.size)
+
+    def copy(self, flow, item, source):
+        here = self.rows(flow, item)
+        return pltpu.make_async_remote_copy(
+            src_ref=source.at[here], dst_ref=self.land_ref.at[flow, here],
+            send_sem=self.send_sem.at[flow, item], recv_sem=self.recv_sem.at[flow, item],
+            device_id={self.axis: self.me + 1 if flow == 0 else self.me - 1},
+            device_id_type=mesh_ids,
+        )
+
+    def step(self, time):
+        for flow in range(2):
+            place = self.place(flow)
+            item = time - place
+            safe = jnp.clip(item, 0, self.length - 1)
+            along = self.owner(flow, safe)
+            valid = (item >= 0) & (item < self.length) & (along >= place)
+            here = self.rows(flow, safe)
+
+            @pl.when(valid & (place == 0))
+            def _():
+                self.copy(flow, safe, self.part_ref).start()
+
+            @pl.when(valid & (place > 0))
+            def _():
+                self.copy(flow, safe, self.part_ref).wait_recv()
+
+            @pl.when(valid & (place > 0) & (along > place))
+            def _():
+                self.land_ref[flow, here, :] = add_low(
+                    self.land_ref[flow, here, :], self.part_ref[here, :]
+                )
+                self.copy(flow, safe, self.land_ref.at[flow]).start()
+
+    def finish(self):
+        def total(sub, carry):
+            size = self.size
+            start = pl.multiple_of(self.me * self.share + sub * size, size)
+            here = pl.ds(start, size)
+            mine = pl.ds(pl.multiple_of(sub * size, size), size)
+            value = self.part_ref[here, :].astype(f32)
+
+            @pl.when(self.me == 0)
+            def _():
+                self.share_ref[mine, :] = value + self.land_ref[1, here, :].astype(f32)
+
+            @pl.when(self.me == self.count - 1)
+            def _():
+                self.share_ref[mine, :] = value + self.land_ref[0, here, :].astype(f32)
+
+            @pl.when((self.me > 0) & (self.me < self.count - 1))
+            def _():
+                self.share_ref[mine, :] = (
+                    value + self.land_ref[0, here, :].astype(f32)
+                    + self.land_ref[1, here, :].astype(f32)
+                )
+            return carry
+
+        lax.fori_loop(0, self.subs, total, 0)
+
+        def drain(item, carry):
+            for flow in range(2):
+                @pl.when(self.owner(flow, item) > self.place(flow))
+                def _():
+                    self.copy(flow, item, self.part_ref).wait_send()
+            return carry
+
+        lax.fori_loop(0, self.length, drain, 0)
+
+
+class CubeSum:
+    def __init__(self, axis, bits, data_ref, total_ref, land_refs, send_sem, recv_sem, back_send_sem,
+                 back_recv_sem, lag, ready, done):
+        self.axis, self.bits, self.lag = axis, bits, lag
+        self.ready, self.done = ready, done
+        self.data_ref, self.total_ref, self.land_refs = data_ref, total_ref, land_refs
+        self.sems = (send_sem, recv_sem, back_send_sem, back_recv_sem)
+        self.me = lax.axis_index(axis)
+        self.chunks, self.rows = data_ref.shape[0], data_ref.shape[1]
+        self.last = 2 * bits
+        self.steps = self.chunks + self.last * lag
+
+    @staticmethod
+    def scratch(bits, chunks, rows, columns):
+        lands = [pltpu.VMEM((chunks, rows // 2, columns), bf16)]
+        for phase in range(1, bits):
+            lands.append(pltpu.VMEM((chunks, rows // 2 ** (phase + 1), columns), bf16))
+        return lands + [pltpu.SemaphoreType.DMA((bits, 2, chunks)) for _ in range(4)]
+
+    def order(self, flow):
+        inner = list(range(1, self.bits))
+        return inner if flow == 0 else inner[::-1]
+
+    def flows(self, phase):
+        return (0,) if phase == 0 else (0, 1)
+
+    def spans(self, phase, flow):
+        size = self.rows // 2
+        kept = bit_of(self.me, 0) * size
+        sent = (1 - bit_of(self.me, 0)) * size
+        if phase == 0:
+            return kept, sent, size, 0
+        size = size // 2
+        base = kept + flow * size
+        for bit in self.order(flow)[:phase]:
+            size = size // 2
+            kept = base + bit_of(self.me, bit) * size
+            sent = base + (1 - bit_of(self.me, bit)) * size
+            base = kept
+        return kept, sent, size, bit
+
+    def there(self, start, size):
+        return pl.ds(pl.multiple_of(start, size), size)
+
+    def landing(self, phase, flow, chunk):
+        size = self.spans(phase, flow)[2]
+        return self.land_refs[phase].at[chunk, flow * size : (flow + 1) * size]
+
+    def copy(self, phase, flow, chunk):
+        kept, sent, size, bit = self.spans(phase, flow)
+        return pltpu.make_async_remote_copy(
+            src_ref=self.data_ref.at[chunk, self.there(sent, size)],
+            dst_ref=self.landing(phase, flow, chunk),
+            send_sem=self.sems[0].at[phase, flow, chunk],
+            recv_sem=self.sems[1].at[phase, flow, chunk],
+            device_id={self.axis: cube_peer(self.me, bit)}, device_id_type=mesh_ids,
+        )
+
+    def back_copy(self, phase, flow, chunk, arriving=False):
+        kept, sent, size, bit = self.spans(phase, flow)
+        here = self.total_ref.at[chunk, self.there(sent if arriving else kept, size)]
+        return pltpu.make_async_remote_copy(
+            src_ref=here, dst_ref=here,
+            send_sem=self.sems[2].at[phase, flow, chunk],
+            recv_sem=self.sems[3].at[phase, flow, chunk],
+            device_id={self.axis: cube_peer(self.me, bit)}, device_id_type=mesh_ids,
+        )
+
+    def add(self, phase, flow, chunk):
+        kept, sent, size, bit = self.spans(phase, flow)
+        piece = min(size, 128)
+        land = self.land_refs[phase]
+        target = self.total_ref if phase == self.bits - 1 else self.data_ref
+
+        def some(index, carry):
+            here = pl.ds(pl.multiple_of(kept + index * piece, piece), piece)
+            from_here = pl.ds(pl.multiple_of(flow * size + index * piece, piece), piece)
+            target[chunk, here, :] = add_low(
+                self.data_ref[chunk, here, :], land[chunk, from_here, :]
+            )
+            return carry
+
+        lax.fori_loop(0, size // piece, some, 0)
+
+    def stage(self, stage, chunk):
+        bits = self.bits
+        if stage == 0:
+            self.ready(chunk)
+            self.copy(0, 0, chunk).start()
+        elif stage <= bits:
+            for flow in self.flows(stage - 1):
+                self.copy(stage - 1, flow, chunk).wait_recv()
+                self.add(stage - 1, flow, chunk)
+                if stage < bits and stage > 1:
+                    self.copy(stage, flow, chunk).start()
+                if stage == bits:
+                    self.back_copy(stage - 1, flow, chunk).start()
+            if stage == 1 and stage < bits:
+                for flow in range(2):
+                    self.copy(1, flow, chunk).start()
+        else:
+            phase = 2 * bits - stage
+            for flow in self.flows(phase):
+                self.back_copy(phase, flow, chunk, True).wait_recv()
+                if phase > 1:
+                    self.back_copy(phase - 1, flow, chunk).start()
+            if phase == 1:
+                self.back_copy(0, 0, chunk).start()
+            if phase == 0:
+                self.done(chunk)
+
+    def step(self, time):
+        for stage in range(self.last, -1, -1):
+            chunk = time - stage * self.lag
+
+            @pl.when((chunk >= 0) & (chunk < self.chunks))
+            def _():
+                self.stage(stage, chunk)
+
+    def finish(self):
+        def drain(chunk, carry):
+            for phase in range(self.bits):
+                for flow in self.flows(phase):
+                    self.copy(phase, flow, chunk).wait_send()
+                    self.back_copy(phase, flow, chunk).wait_send()
+            return carry
+
+        lax.fori_loop(0, self.chunks, drain, 0)
+
+
+class SmallSum:
+    def __init__(self, cube_axis, bits, line_axis, count, gap, own_ref, cube_ref, all_ref, work_ref, land_ref,
+                 line_ref, send_sem, recv_sem, line_send_sem, line_recv_sem):
+        self.cube_axis, self.bits, self.line_axis, self.count = cube_axis, bits, line_axis, count
+        self.gap = gap
+        self.own_ref, self.cube_ref, self.all_ref = own_ref, cube_ref, all_ref
+        self.work_ref, self.land_ref, self.line_ref = work_ref, land_ref, line_ref
+        self.sems = (send_sem, recv_sem, line_send_sem, line_recv_sem)
+        self.me = lax.axis_index(cube_axis)
+        self.line_me = lax.axis_index(line_axis)
+        self.steps = (bits + 1) * gap + 1
+
+    @staticmethod
+    def scratch(bits, count, shape):
+        return [
+            pltpu.VMEM((bits,) + shape, f32),
+            pltpu.VMEM((bits,) + shape, f32),
+            pltpu.VMEM((count,) + shape, f32),
+            pltpu.SemaphoreType.DMA((bits,)),
+            pltpu.SemaphoreType.DMA((bits,)),
+            pltpu.SemaphoreType.DMA((count,)),
+            pltpu.SemaphoreType.DMA((count,)),
+        ]
+
+    def cube_copy(self, bit):
+        source = self.own_ref if bit == 0 else self.work_ref.at[bit - 1]
+        return pltpu.make_async_remote_copy(
+            src_ref=source, dst_ref=self.land_ref.at[bit],
+            send_sem=self.sems[0].at[bit], recv_sem=self.sems[1].at[bit],
+            device_id={self.cube_axis: cube_peer(self.me, bit)}, device_id_type=mesh_ids,
+        )
+
+    def line_copy(self, there, slot):
+        return pltpu.make_async_remote_copy(
+            src_ref=self.work_ref.at[self.bits - 1], dst_ref=self.line_ref.at[slot],
+            send_sem=self.sems[2].at[there], recv_sem=self.sems[3].at[slot],
+            device_id={self.line_axis: there}, device_id_type=mesh_ids,
+        )
+
+    def step(self, time):
+        for turn in range(self.bits + 2):
+            pl.when(time == turn * self.gap)(functools.partial(self.turn, turn))
+
+    def turn(self, turn):
+        bits = self.bits
+        if 0 < turn <= bits:
+            self.cube_copy(turn - 1).wait_recv()
+            before = self.own_ref[...] if turn == 1 else self.work_ref[turn - 2]
+            self.work_ref[turn - 1] = before + self.land_ref[turn - 1]
+        if turn < bits:
+            self.cube_copy(turn).start()
+        elif turn == bits:
+            self.cube_ref[...] = self.work_ref[bits - 1]
+            self.line_ref[self.line_me] = self.work_ref[bits - 1]
+            for there in range(self.count):
+                @pl.when(there != self.line_me)
+                def _():
+                    self.line_copy(there, self.line_me).start()
+        else:
+            for slot in range(self.count):
+                @pl.when(slot != self.line_me)
+                def _():
+                    self.line_copy(slot, slot).wait_recv()
+            total = self.line_ref[0]
+            for slot in range(1, self.count):
+                total = total + self.line_ref[slot]
+            self.all_ref[...] = total
+
+    def finish(self):
+        for bit in range(self.bits):
+            self.cube_copy(bit).wait_send()
+        for there in range(self.count):
+            @pl.when(there != self.line_me)
+            def _():
+                self.line_copy(there, self.line_me).wait_send()
+
+
+def tail_kernel(line_axis, count, subs, cube_axis, bits, lag, widths, *refs):
+    part_ref, small_ref, *grad_refs = refs[: 2 + len(widths)]
+    share_ref, small_cube_ref, small_all_ref, sums_ref = refs[2 + len(widths) : 6 + len(widths)]
+    scratch = list(refs[6 + len(widths) :])
+    data_ref, total_ref, load_sem, store_sem = scratch[:4]
+    line_scratch, scratch = scratch[4:7], scratch[7:]
+    cube_scratch, small_scratch = scratch[: bits + 4], scratch[bits + 4 :]
+    chunks, _, columns = data_ref.shape
+
+    def load(chunk, source):
+        return pltpu.make_async_copy(source, data_ref.at[chunk], load_sem.at[chunk])
+
+    def store(chunk):
+        there = pl.ds(pl.multiple_of(chunk * columns, columns), columns)
+        return pltpu.make_async_copy(
+            total_ref.at[chunk], sums_ref.at[:, there], store_sem.at[chunk]
+        )
+
+    chunk = 0
+    for grad_ref, width in zip(grad_refs, widths):
+        for start in range(0, width, columns):
+            load(chunk, grad_ref.at[:, start : start + columns]).start()
+            chunk += 1
+    greet(line_axis, count, cube_axis, bits)
+    parts = [
+        LineScatter(line_axis, count, subs, part_ref, share_ref, *line_scratch),
+        CubeSum(
+            cube_axis, bits, data_ref, total_ref, cube_scratch[:bits], *cube_scratch[bits:], lag,
+            lambda chunk: load(chunk, grad_refs[0].at[:, :columns]).wait(),
+            lambda chunk: store(chunk).start(),
+        ),
+        SmallSum(
+            cube_axis, bits, line_axis, count, 2, small_ref, small_cube_ref, small_all_ref,
+            *small_scratch,
+        ),
+    ]
+
+    def step(time, carry):
+        for part in parts:
+            part.step(time)
+        return carry
+
+    lax.fori_loop(0, max(part.steps for part in parts), step, 0)
+    for part in parts:
+        part.finish()
+
+    def stored(chunk, carry):
+        store(chunk).wait()
+        return carry
+
+    lax.fori_loop(0, chunks, stored, 0)
+
+
+def tail_sums(part, small, grads, line_axis, cube_axis, columns, subs, lag, cid):
+    count = lax.axis_size(line_axis)
+    bits = lax.axis_size(cube_axis).bit_length() - 1
+    rows = grads[0].shape[0]
+    widths = tuple(grad.shape[1] for grad in grads)
+    chunks = sum(widths) // columns
+    vmem = pl.BlockSpec(memory_space=pltpu.VMEM)
+    hbm = pl.BlockSpec(memory_space=pl.ANY)
+    small_shape = jax.ShapeDtypeStruct(small.shape, f32)
+    return pl.pallas_call(
+        functools.partial(tail_kernel, line_axis, count, subs, cube_axis, bits, lag, widths),
+        out_shape=(
+            jax.ShapeDtypeStruct((part.shape[0] // count, part.shape[1]), f32),
+            small_shape,
+            small_shape,
+            jax.ShapeDtypeStruct((rows, sum(widths)), bf16),
+        ),
+        in_specs=[vmem, vmem] + [hbm] * len(grads),
+        out_specs=[vmem, vmem, vmem, hbm],
+        scratch_shapes=[
+            pltpu.VMEM((chunks, rows, columns), bf16),
+            pltpu.VMEM((chunks, rows, columns), bf16),
+            pltpu.SemaphoreType.DMA((chunks,)),
+            pltpu.SemaphoreType.DMA((chunks,)),
+            *LineScatter.scratch(count, subs, part.shape),
+            *CubeSum.scratch(bits, chunks, rows, columns),
+            *SmallSum.scratch(bits, count, small.shape),
+        ],
+        compiler_params=pltpu.CompilerParams(
+            collective_id=cid, has_side_effects=True, vmem_limit_bytes=63 * 2**20
+        ),
+        name="tail_sums",
+    )(part, small, *grads)
+
+
+def line_scatter(part, axis):
+    count = lax.axis_size(axis)
+    me = lax.axis_index(axis)
+    share = part.shape[0] // count
+
+    def block(owner):
+        owner = jnp.clip(owner, 0, count - 1)
+        return lax.dynamic_slice_in_dim(part, owner * share, share, 0)
+
+    right = [(index, index + 1) for index in range(count - 1)]
+    left = [(index + 1, index) for index in range(count - 1)]
+    from_left = from_right = None
+    for time in range(count - 1):
+        to_right = block(count - 1 - time + me)
+        to_left = block(time - (count - 1) + me)
+        if time > 0:
+            to_right = add_low(to_right, from_left)
+            to_left = add_low(to_left, from_right)
+        from_left = lax.ppermute(to_right, axis, right)
+        from_right = lax.ppermute(to_left, axis, left)
+    return block(me).astype(f32) + from_left.astype(f32) + from_right.astype(f32)
+
+
 def project(left_side, right_side):
     return jnp.dot(left_side, right_side, preferred_element_type=f32)
 
@@ -456,10 +908,6 @@
     grad_hat = grad_normed * gain_vec
     inner_mean = jnp.mean(grad_hat * signal, axis=-1, keepdims=True)
     return rms_scale * (grad_hat - signal * rms_scale * rms_scale * inner_mean)
-
-
-def gain_term(signal, rms_scale, grad_normed):
-    return jnp.sum(grad_normed * signal * rms_scale, axis=0)
 
 
 def shards(
@@ -482,12 +930,6 @@
             signal.reshape(row_count, length, -1), first_row, share_rows, 1
         )
         return part.reshape(row_count * share_rows, -1)
-
-    def scatter(part):
-        summed = lax.psum_scatter(
-            part.astype(bf16).reshape(plane), "tensor", scatter_dimension=1, tiled=True
-        )
-        return summed.reshape(row_count * share_rows, model_width).astype(f32)
 
     flat_inputs = inputs.reshape(token_count, model_width).astype(f32)
     grad_out = cotangent.reshape(token_count, model_width)
@@ -514,16 +956,28 @@
     grad_gate = act_pull(grad_hidden * up_pre)[0].astype(bf16)
     grad_up = (grad_hidden * act_value).astype(bf16)
     norm_ffn_part = project_back(grad_gate, w_gate) + project_back(grad_up, w_up)
-    grad_normed_ffn = line_sum(norm_ffn_part.astype(bf16), "tensor", line_chunks, 0).astype(f32)
-    ffn_share = scatter(project(hidden, w_down))
-    middle_share = take_share(middle)
-    output = (middle_share + ffn_share).reshape(share_shape).astype(bf16)
+    normed_ffn_hat = middle * scale_ffn
+    gain_ffn_part = jnp.sum(norm_ffn_part * normed_ffn_hat, axis=0)
+    gate_up_grad = weight_term(normed_ffn, jnp.concatenate([grad_gate, grad_up], axis=1))
     down_grad = weight_term(hidden, grad_out)
-    gate_up_grad = weight_term(normed_ffn, jnp.concatenate([grad_gate, grad_up], axis=1))
+    norm_ffn_low, gate_up_grad, down_grad = lax.optimization_barrier(
+        (norm_ffn_part.astype(bf16), gate_up_grad, down_grad)
+    )
+    grad_normed_ffn = line_sum(norm_ffn_low, "tensor", line_chunks, 0).astype(f32)
+
+    def reduce_all(grad, axis):
+        part = lax.psum_scatter(grad, "dp", scatter_dimension=axis, tiled=True)
+        return lax.all_gather(part, "dp", axis=axis, tiled=True)
+
+    gate_up_grad = reduce_all(gate_up_grad, 0)
+    down_grad = reduce_all(down_grad, 1).astype(f32)
+    gate_grad, up_grad = jnp.split(gate_up_grad.astype(f32), 2, axis=1)
+    ffn_part = project(hidden, w_down).astype(bf16)
+    ffn_part, grad_normed_ffn = lax.optimization_barrier((ffn_part, grad_normed_ffn))
+    ffn_share = line_scatter(ffn_part, "tensor")
+    output = (take_share(middle) + ffn_share).reshape(share_shape).astype(bf16)
     grad_middle = grad_out.astype(f32) + norm_back(middle, scale_ffn, gain_ffn, grad_normed_ffn)
-    gain_ffn_part = gain_term(middle_share, take_share(scale_ffn), take_share(grad_normed_ffn))
     grad_branch = grad_middle.astype(bf16)
-    out_grad = weight_term(mixed_flat, grad_branch)
     grad_mixed = project_back(grad_branch, w_out).astype(bf16).reshape(heads_shape)
     grad_query, grad_key, grad_value, sums = attend_back(
         queries, keys, values, grad_mixed, mixed, totals, segments, lines
@@ -538,28 +992,25 @@
         + project_back(grad_key, w_key)
         + project_back(grad_value, w_value)
     )
-    grad_normed_attn = scatter(norm_attn_part)
+    gain_attn_part = jnp.sum(norm_attn_part * (flat_inputs * scale_attn), axis=0)
     qkv_grad = weight_term(normed, jnp.concatenate([grad_query, grad_key, grad_value], axis=1))
+    out_grad = weight_term(grad_branch, mixed_flat)
+    table_line = jnp.pad(table_grad.reshape(-1), (0, model_width - bucket_count * head_count))
+    small = jnp.stack([gain_attn_part, gain_ffn_part, table_line])
+    small = jnp.pad(small, ((0, 8 - small.shape[0]), (0, 0)))
+    grad_normed_attn, small_cube, small_all, attn_sums = tail_sums(
+        norm_attn_part.astype(bf16), small, [qkv_grad, out_grad], "tensor", "dp",
+        tail_columns, tail_subs, tail_lag, 1,
+    )
+    query_grad, key_grad, value_grad, out_grad = jnp.split(attn_sums.astype(f32), 4, axis=1)
+    out_grad = jnp.transpose(out_grad)
+    gain_attn_grad, gain_ffn_grad = small_all[0], small_all[1]
+    table_grad = small_cube[2, : bucket_count * head_count].reshape(bucket_count, head_count)
     inputs_share = take_share(flat_inputs)
-    scale_share = take_share(scale_attn)
     grad_input = take_share(grad_middle) + norm_back(
-        inputs_share, scale_share, gain_attn, grad_normed_attn
+        inputs_share, take_share(scale_attn), gain_attn, grad_normed_attn
     )
     input_grad = grad_input.reshape(share_shape).astype(bf16)
-    gain_attn_part = gain_term(inputs_share, scale_share, grad_normed_attn)
-    gain_attn_grad, gain_ffn_grad = lax.psum((gain_attn_part, gain_ffn_part), ("dp", "tensor"))
-    table_grad = lax.psum(table_grad, "dp")
-
-    def reduce_all(grad, axis):
-        part = lax.psum_scatter(grad, "dp", scatter_dimension=axis, tiled=True)
-        return lax.all_gather(part, "dp", axis=axis, tiled=True)
-
-    gate_up_grad = reduce_all(gate_up_grad, 0)
-    down_grad = reduce_all(down_grad, 1).astype(f32)
-    out_grad = reduce_all(out_grad, 1).astype(f32)
-    qkv_grad = reduce_all(qkv_grad, 0)
-    gate_grad, up_grad = jnp.split(gate_up_grad.astype(f32), 2, axis=1)
-    query_grad, key_grad, value_grad = jnp.split(qkv_grad.astype(f32), 3, axis=1)
     return (
         output, input_grad, query_grad, key_grad, value_grad, out_grad, gate_grad, up_grad,
         down_grad, gain_attn_grad, gain_ffn_grad, table_grad,

time: 1000 us -> 902 us (0.902)
  waiting for transfers between devices: 405 us -> 180 us
  Pallas kernels: 289 us -> 408 us
  blocking collectives: 52.9 us -> 0 us
  starting transfers between devices: 0.65 us -> 22.4 us
  other arithmetic: 64.5 us -> 84.2 us
  local copies, waits for them, and re-layouts: 26.8 us -> 41.9 us
    reduce_scatter x2 -> x0, waiting for transfers between devices: 152 us -> none  [scatter(): lax.psum_scatter(part.astype(bf16).reshape(plane), 'tensor', scatter_dime...]
    pallas_call x0 -> x1, Pallas kernels: none -> 125 us  [tail_sums(): pl.pallas_call(functools.partial(tail_kernel, line_axis, count, subs, cub...]
    all_gather x4 -> x2, waiting for transfers between devices: 101 us -> 0.01 us  [reduce_all(): return lax.all_gather(part, 'dp', axis=axis, tiled=True)]
    psum x2 -> x0, blocking collectives: 52.9 us -> none  [the longest x1 40.5 us: shards(): lax.psum((gain_attn_part, gain_ffn_part), ('dp', 'tensor'))]
    ppermute x0 -> x6, waiting for transfers between devices: none -> 26.3 us  [the longest x3 26.3 us: line_scatter(): from_right = lax.ppermute(to_left, axis, left)]
    ppermute x0 -> x6, starting transfers between devices: none -> 22.2 us  [the longest x3 11.6 us: line_scatter(): from_right = lax.ppermute(to_left, axis, left)]
    convert_element_type x2 -> x6, other arithmetic: 10.9 us -> 29.1 us  [the longest x1 11.3 us: shards(): attn_sums.astype(f32)]
    dot_general x7, matrix products: 52.6 us -> 65.4 us  [dot_nt(): lax.dot_general(left_side, right_side, (((1,), (1,)), ((), ())), preferre...]
  transfers between devices with their start and end apart: 10 -> 10, of which waited for: 8 -> 4; matrix products, arithmetic and copies ran while one was open for 11% -> 16% of each run, Pallas kernels for 3% -> 30%
where the time goes in v3:
time: 902 us; the launch traced here: 894 us
  Pallas kernels  408 us (45%)
  waiting for transfers between devices  180 us (20%)
  matrix products  143 us (16%)
  other arithmetic  84.2 us (9%)
  local copies, waits for them, and re-layouts  41.9 us (5%)
  starting transfers between devices  22.4 us (2%)
  between operations  14.8 us (2%)
    pallas_call x2, Pallas kernels, line_sum(): pl.pallas_call(functools.partial(line_sum_kernel, axis, count, chunks), o...  220 us
    reduce_scatter x2, waiting for transfers between devices, reduce_all(): part = lax.psum_scatter(grad, 'dp', scatter_dimension=axis, tiled=True)  153 us
    pallas_call x1, Pallas kernels, tail_sums(): pl.pallas_call(functools.partial(tail_kernel, line_axis, count, subs, cub...  125 us
    dot_general x7, matrix products, dot_nt(): lax.dot_general(left_side, right_side, (((1,), (1,)), ((), ())), preferre...  65.4 us
    dot_general x7, matrix products, project(): return jnp.dot(left_side, right_side, preferred_element_type=f32)  40.4 us
    pallas_call x1, Pallas kernels, attend_back(): pl.pallas_call(functools.partial(backward_kernel, block_count), out_shape...  36.7 us
    dot_general x4, matrix products, weight_term(): lax.dot_general(left_side, right_side, (((0,), (0,)), ((), ())), preferre...  36.3 us
    ppermute x3, waiting for transfers between devices, line_scatter(): from_right = lax.ppermute(to_left, axis, left)  26.3 us
  transfers between devices with their start and end apart: 10, of which 4 were waited for; matrix products, arithmetic and copies ran while one was open for 16% of the time, Pallas kernels for 30%

profile of v3, /device:TPU:17, one launch (start us, length us, event | category | flops | bytes accessed | tf_op | source)
XLA Modules:
  0.0 893.6 jit_solution(2416873989200923783)
XLA Ops:
  7.8 1.3 reduce.9
  9.4 0.8 convert_reduce_fusion
  10.7 3.1 fusion
  13.9 6.4 fusion.32.q_ref
  20.3 3.4 fusion.33.k_ref
  23.7 3.4 fusion.34.v_ref
  27.0 1.0 copy.40.seg_col_ref
  28.4 0.7 copy.41.line_ref
  29.1 26.2 %attend.1 = (bf16[1,1024,512]{2,1,0:T(8,128)(2,1)}, f32[1,4,2,1024]{3,2,1,0:T(2,128)}) custom-call(s32[4]{0:T(128)} %get-tuple-element.81.first_ref, s32[4]{0:T(128)} %broadcast_add_fusion.last_ref, bf16[1,1024,512]{2,1,0:T(8,128)(2,1)} %fusion.32.q_ref, bf16[1,1024,512]{2,1,0:T(8,128)(2,1)} %fusion.33.k_ref, bf16[1,1024,512]{2,1,0:T(8,128)(2,1)} %fusion.34.v_ref, ...), custom_call_target="tpu_custom_call" | custom-call | tf_op jit(solution)/shard_map/attend/pallas_call | solution.py:263
  55.3 5.6 convolution_convert_fusion.4.part_ref
  60.9 109.6 %line_sum.2 = bf16[1024,2048]{1,0:T(8,128)(2,1)} custom-call(bf16[1024,2048]{1,0:T(8,128)(2,1)} %convolution_convert_fusion.4.part_ref), custom_call_target="tpu_custom_call" | custom-call | tf_op jit(solution)/shard_map/line_sum/pallas_call | solution.py:418
  170.5 5.0 multiply_reduce_fusion.3
  175.6 0.8 copy-done.6
  176.4 2.7 multiply_convert_fusion
  179.2 7.3 fusion.60
  186.5 7.3 fusion.61
  193.8 14.9 %multiply_convert_fusion.2 = (bf16[1024,1280]{1,0:T(8,128)(2,1)}, bf16[1024,1280]{1,0:T(8,128)(2,1)}, bf16[1024,1280]{1,0:T(8,128)(2,1)S(1)}) fusion(f32[1024,1280]{1,0:T(8,128)} %fusion.60, f32[1024,1280]{1,0:T(8,128)} %fusion.61, bf16[1280,2048]{1,0:T(8,128)(2,1)} %param.22, bf16[1,1024,2048]{2,1,0:T(8,128)(2,1)S(1)} %copy-done.10), kind=kOutput, calls=%fused_computation.27 | convolution fusion | flops 5402787840 | bytes 27787264 | tf_op jit(solution)/shard_map/dot_general | solution.py:43
  208.6 10.5 %fusion.62 = f32[1024,2048]{1,0:T(8,128)} fusion(bf16[1024,1280]{1,0:T(8,128)(2,1)} %get-tuple-element.85, bf16[2048,1280]{1,0:T(8,128)(2,1)S(1)} %bitcast.137), kind=kOutput, calls=%fused_computation.111 | convolution fusion | flops 5368709120 | bytes 16252928 | tf_op jit(solution)/shard_map/dot_general | solution.py:43
  219.2 15.9 %convolution_convert_fusion = bf16[2048,2560]{1,0:T(8,128)(2,1)} fusion(bf16[1024,2048]{1,0:T(8,128)(2,1)S(1)} %multiply_convert_fusion, bf16[1024,1280]{1,0:T(8,128)(2,1)} %get-tuple-element.84, bf16[1024,1280]{1,0:T(8,128)(2,1)} %get-tuple-element.85), kind=kOutput, calls=%fused_computation | convolution fusion | flops 10753146880 | bytes 19922944 | tf_op jit(solution)/shard_map/dot_general | solution.py:898
  235.0 12.8 %fusion.59 = (bf16[1024,2048]{1,0:T(8,128)(2,1)}, f32[1024,2048]{1,0:T(8,128)}) fusion(f32[1024,2048]{1,0:T(8,128)} %fusion.62, bf16[1024,1280]{1,0:T(8,128)(2,1)} %get-tuple-element.84, bf16[2048,1280]{1,0:T(8,128)(2,1)} %param.21), kind=kOutput, calls=%fused_computation.108 | convolution fusion | flops 5372903424 | bytes 28835840 | tf_op jit(solution)/shard_map/dot_general | solution.py:43
  247.8 7.4 convolution_convert_fusion.2
  255.3 0.7 reduce-scatter.3.cloned.1.call-update
  256.1 67.0 %reduce-scatter.5.cloned.1.call-done = bf16[1280,256]{1,0:T(8,128)(2,1)} async-done(((bf16[1280,2048]{1,0:T(8,128)(2,1)}), bf16[1280,256]{1,0:T(8,128)(2,1)}) %reduce-scatter.5.cloned.1.call-update) | async-done | bytes 655376 | tf_op jit(solution)/shard_map/reduce_scatter | solution.py:969
  323.2 86.0 %reduce-scatter.3.cloned.1.call-done = bf16[256,2560]{1,0:T(8,128)(2,1)} async-done(((bf16[2048,2560]{1,0:T(8,128)(2,1)}), bf16[256,2560]{1,0:T(8,128)(2,1)}) %reduce-scatter.3.cloned.1.call-update) | async-done | bytes 1310736 | tf_op jit(solution)/shard_map/reduce_scatter | solution.py:969
  409.2 110.6 %line_sum.3 = bf16[1024,2048]{1,0:T(8,128)(2,1)} custom-call(bf16[1024,2048]{1,0:T(8,128)(2,1)} %get-tuple-element.28.part_ref), custom_call_target="tpu_custom_call" | custom-call | tf_op jit(solution)/shard_map/line_sum/pallas_call | solution.py:418
  519.8 6.8 convert_element_type.253
  526.6 7.1 convolution_convert_fusion.3
  533.8 2.7 constant_dynamic-slice_fusion.1
  536.5 4.1 collective-permute-start
  540.7 1.9 collective-permute-start.3
  542.6 6.7 convert_element_type.228
  549.3 9.6 %multiply_reduce_fusion = (f32[2048]{0:T(1024)}, f32[1024]{0:T(1024)S(1)}) fusion(f32[1024,2048]{1,0:T(8,128)} %get-tuple-element.105, f32[1024]{0:T(1024)S(1)} %add_rsqrt_fusion, bf16[1024,2048]{1,0:T(8,128)(2,1)S(1)} %copy-done.7, bf16[1,1024,2048]{2,1,0:T(8,128)(2,1)S(1)} %copy-done.4, f32[1024,2048]{1,0:T(8,128)} %convert_element_type.253, ...), kind=kLoop, calls=%fused_computation.5 | loop fusion | flops 18871296 | bytes 25190400 | tf_op jit(solution)/shard_map/reduce_sum | solution.py:960
  558.9 0.6 broadcast_multiply_fusion
  559.5 9.8 %multiply_add_fusion = (f32[1024,2048]{1,0:T(8,128)}, f32[1024,2048]{1,0:T(8,128)}) fusion(f32[1024,2048]{1,0:T(8,128)S(1)} %bitcast.120, bf16[1,1024,2048]{2,1,0:T(8,128)(2,1)} %param.15, f32[1024]{0:T(1024)} %broadcast_multiply_fusion, f32[2048]{0:T(1024)S(1)} %copy-done.16, f32[1024]{0:T(1024)S(1)} %add_rsqrt_fusion, bf16[1024,2048]{1,0:T(8,128)(2,1)S(1)} %copy-done.7, ...), kind=kLoop, calls=%fused_computation.8 | loop fusion | flops 23068672 | bytes 37765120 | tf_op jit(solution)/shard_map/add | solution.py:979
  569.4 7.3 fusion.35.grad_ref
  576.7 36.7 %attend_back.1 = (bf16[1,1024,512]{2,1,0:T(8,128)(2,1)}, bf16[1,1024,512]{2,1,0:T(8,128)(2,1)}, bf16[1,1024,512]{2,1,0:T(8,128)(2,1)}, f32[1,8,5,512]{3,2,1,0:T(8,128)}) custom-call(s32[4]{0:T(128)} %get-tuple-element.81.first_ref, s32[4]{0:T(128)} %broadcast_add_fusion.last_ref, bf16[1,1024,512]{2,1,0:T(8,128)(2,1)} %fusion.32.q_ref, ...), custom_call_target="tpu_custom_call" | custom-call | tf_op jit(solution)/shard_map/attend_back/pallas_call | solution.py:290
  613.4 1.0 copy.50
  614.4 4.4 fusion.53
  618.9 5.8 fusion.51
  624.7 3.7 convolution_convert_fusion.5.refs_3_
  628.4 9.3 %convolution_convert_fusion.1.refs_2_ = bf16[2048,1536]{1,0:T(8,128)(2,1)} fusion(bf16[1024,512]{1,0:T(8,128)(2,1)S(1)} %bitcast.123, bf16[1024,512]{1,0:T(8,128)(2,1)S(1)} %bitcast.143, bf16[1024,512]{1,0:T(8,128)(2,1)S(1)} %bitcast.142, bf16[1,1024,2048]{2,1,0:T(8,128)(2,1)S(1)} %copy-done.5, f32[2048]{0:T(1024)S(1)} %copy-done.22, f32[1024]{0:T(1024)S(1)} %copy-done.24), kind=kOutput, calls=%fused_computation.13 | convolution fusion | flops 6463422464 | bytes 13643776 | tf_op jit(solution)/shard_map/dot_general | solution.py:898
  637.7 9.7 %multiply_reduce_fusion.1 = (f32[2048]{0:T(1024)S(1)}, bf16[1024,2048]{1,0:T(8,128)(2,1)}) fusion(bf16[1,1024,2048]{2,1,0:T(8,128)(2,1)S(1)} %copy-done.5, f32[1024]{0:T(1024)S(1)} %copy-done.24, bf16[2048,512]{1,0:T(8,128)(2,1)} %param.18, bf16[1,1024,512]{2,1,0:T(8,128)(2,1)} %get-tuple-element.34, f32[1024,2048]{1,0:T(8,128)S(1)} %fusion.53, ...), kind=kOutput, calls=%fused_computation.6 | convolution fusion | flops 2162161664 | bytes 28323840 | tf_op jit(solution)/shard_map/dot_general | solution.py:43
  647.5 2.9 add_convert_fusion.4
  650.4 4.5 collective-permute-start.1
  655.4 0.7 select_maximum_fusion.refs_1_
  656.0 124.8 %tail_sums.1 = (f32[256,2048]{1,0:T(8,128)}, f32[8,2048]{1,0:T(8,128)}, f32[8,2048]{1,0:T(8,128)}, bf16[2048,2048]{1,0:T(8,128)(2,1)}) custom-call(bf16[1024,2048]{1,0:T(8,128)(2,1)} %get-tuple-element.91.refs_0_, f32[8,2048]{1,0:T(8,128)} %select_maximum_fusion.refs_1_, bf16[2048,1536]{1,0:T(8,128)(2,1)} %convolution_convert_fusion.1.refs_2_, ...), custom_call_target="tpu_custom_call" | custom-call | tf_op jit(solution)/shard_map/tail_sums/pallas_call | solution.py:840
  780.8 11.3 %convert_element_type.279 = f32[2048,2048]{1,0:T(8,128)} convert(bf16[2048,2048]{1,0:T(8,128)(2,1)} %get-tuple-element.37) | non-fusion elementwise | flops 4194304 | bytes 25165824 | tf_op jit(solution)/shard_map/convert_element_type | solution.py:1005
  792.1 4.6 slice_bitcast_fusion
  796.7 5.3 copy.45
  802.1 4.5 add_convert_fusion.3
  806.6 5.7 collective-permute-start.4
  812.3 0.7 slice_reduce_fusion
  813.1 0.7 copy.46
  813.8 2.1 fusion.25
  815.9 4.0 fusion.41
  819.9 1.9 collective-permute-start.2
  821.8 13.4 %collective-permute-done.4 = bf16[256,2048]{1,0:T(8,128)(2,1)S(1)} collective-permute-done((bf16[256,2048]{1,0:T(8,128)(2,1)}, bf16[256,2048]{1,0:T(8,128)(2,1)S(1)}, u32[]{:S(2)}, u32[]{:S(2)}) %collective-permute-start.4) | collective-permute-done | bytes 1048608 | tf_op jit(solution)/shard_map/ppermute | solution.py:885
  835.7 4.0 collective-permute-start.5
  839.7 1.5 fusion.57
  841.2 8.1 fusion.56
  849.3 12.8 %collective-permute-done.5 = bf16[256,2048]{1,0:T(8,128)(2,1)S(1)} collective-permute-done((bf16[256,2048]{1,0:T(8,128)(2,1)S(1)}, bf16[256,2048]{1,0:T(8,128)(2,1)S(1)}, u32[]{:S(2)}, u32[]{:S(2)}) %collective-permute-start.5) | collective-permute-done | bytes 1048608 | tf_op jit(solution)/shard_map/ppermute | solution.py:885
  862.2 3.2 fusion.38
  865.4 8.0 convert_element_type.281
  873.4 13.3 %fusion.55 = (f32[2048,1280]{1,0:T(8,128)}, f32[2048,1280]{1,0:T(8,128)}) fusion(bf16[2048,2560]{1,0:T(8,128)(2,1)} %all-gather.3.cloned.1.call-done), kind=kLoop, calls=%fused_computation.104 | loop fusion | bytes 41943040 | tf_op jit(solution)/shard_map/split | solution.py:974
  (123 shorter events, 3.1 us)
Async XLA Ops:
  7.2 21.0 %copy-start = (f32[32,8]{0,1:T(8,128)S(1)}, f32[32,8]{0,1:T(8,128)}, u32[]{:S(2)}) copy-start(f32[32,8]{0,1:T(8,128)} %param.25) | copy-start | bytes 3076
  7.2 315.9 %reduce-scatter.5.cloned.1.call-start = ((), (), s32[]{:S(2)}) async-start(), calls=%async_computation.4 | async-start | bytes 5898240 | tf_op jit(solution)/shard_map/reduce_scatter | solution.py:969
  13.8 9.8 %copy-start.23 = (f32[1024]{0:T(1024)}, f32[1024]{0:T(1024)S(1)}, u32[]{:S(2)}) copy-start(f32[1024]{0:T(1024)S(1)} %add_rsqrt_fusion.1) | copy-start | bytes 12292
  13.8 6.4 copy-start.2
  13.8 6.4 copy-start.21
  13.9 6.4 copy-start.26
  20.2 3.4 copy-start.12
  23.6 3.4 copy-start.17
  23.6 31.6 %copy-start.25 = (bf16[512,2048]{1,0:T(8,128)(2,1)S(1)}, bf16[512,2048]{1,0:T(8,128)(2,1)}, u32[]{:S(2)}) copy-start(bf16[512,2048]{1,0:T(8,128)(2,1)} %param.19) | copy-start | bytes 6291460
  28.2 0.9 copy-start.18
  170.5 5.1 copy-start.3
  170.5 5.9 copy-start.6
  170.5 5.9 copy-start.16
  170.5 8.6 slice-start.4
  176.4 2.8 slice-start.5
  176.4 10.1 %slice-start.6 = ((s8[5242880]{0:T(1024)(128)(4,1)}), s8[4194304]{0:T(1024)(128)(4,1)S(1)}, s32[]{:S(2)}) async-start(s8[5242880]{0:T(1024)(128)(4,1)} %bitcast.138), calls=%async_computation.12 | async-start | bytes 8388608
  179.2 7.3 slice-start.7
  186.5 7.3 copy-start.10
  208.6 39.2 %copy-start.30 = (bf16[1024,1280]{1,0:T(8,128)(2,1)}, bf16[1024,1280]{1,0:T(8,128)(2,1)S(1)}, u32[]{:S(2)}) copy-start(bf16[1024,1280]{1,0:T(8,128)(2,1)S(1)} %get-tuple-element.86) | copy-start | bytes 7864324
  235.0 12.8 %copy-start.11 = (bf16[1,1024,2048]{2,1,0:T(8,128)(2,1)S(1)}, bf16[1,1024,2048]{2,1,0:T(8,128)(2,1)}, u32[]{:S(2)}) copy-start(bf16[1,1024,2048]{2,1,0:T(8,128)(2,1)} %param.15) | copy-start | bytes 12582916
  255.3 153.8 %reduce-scatter.3.cloned.1.call-start = ((), (), s32[]{:S(2)}) async-start(), calls=%async_computation.2 | async-start | bytes 11796480 | tf_op jit(solution)/shard_map/reduce_scatter | solution.py:969
  256.1 609.3 %all-gather.5.cloned.1.call-start = ((), (), s32[]{:S(2)}) async-start(), calls=%async_computation.5 | async-start | bytes 5898240 | tf_op jit(solution)/shard_map/all_gather | solution.py:970
  323.1 550.3 %all-gather.3.cloned.1.call-start = ((), (), s32[]{:S(2)}) async-start(), calls=%async_computation.3 | async-start | bytes 11796480 | tf_op jit(solution)/shard_map/all_gather | solution.py:970
  409.2 117.4 %slice-start.8 = ((s8[5242880]{0:T(1024)(128)(4,1)}), s8[1048576]{0:T(1024)(128)(4,1)S(1)}, s32[]{:S(2)}) async-start(s8[5242880]{0:T(1024)(128)(4,1)} %bitcast.140), calls=%async_computation.14 | async-start | bytes 2097152
  519.8 6.8 slice-start.9
  519.8 6.8 copy-start.31
  536.5 110.9 %collective-permute-start = (bf16[256,2048]{1,0:T(8,128)(2,1)S(1)}, bf16[256,2048]{1,0:T(8,128)(2,1)}, u32[]{:S(2)}, u32[]{:S(2)}) collective-permute-start(bf16[256,2048]{1,0:T(8,128)(2,1)S(1)} %get-tuple-element.96), channel_id=1, source_target_pairs={{0,1},{1,2},{2,3},{4,5},{5,6},{6,7},{8,9},{9,10},{10,11},{12,13},{... | collective-permute-start | bytes 3145736 | tf_op jit(solution)/shard_map/ppermute | solution.py:884
  540.7 261.4 %collective-permute-start.3 = (bf16[256,2048]{1,0:T(8,128)(2,1)}, bf16[256,2048]{1,0:T(8,128)(2,1)}, u32[]{:S(2)}, u32[]{:S(2)}) collective-permute-start(bf16[256,2048]{1,0:T(8,128)(2,1)} %get-tuple-element.97), channel_id=1, source_target_pairs={{1,0},{2,1},{3,2},{5,4},{6,5},{7,6},{9,8},{10,9},{11,10},{13,12},{... | collective-permute-start | bytes 3145736 | tf_op jit(solution)/shard_map/ppermute | solution.py:885
  542.6 6.7 copy-start.4
  542.6 6.7 copy-start.7
  549.3 10.2 %slice-start = ((s8[8388608]{0:T(1024)(128)(4,1)}), s8[4194304]{0:T(1024)(128)(4,1)S(1)}, s32[]{:S(2)}) async-start(s8[8388608]{0:T(1024)(128)(4,1)} %bitcast.119), calls=%async_computation.6 | async-start | bytes 8388608
  549.3 10.2 %slice-start.1 = ((s8[8388608]{0:T(1024)(128)(4,1)}), s8[4194304]{0:T(1024)(128)(4,1)S(1)}, s32[]{:S(2)}) async-start(s8[8388608]{0:T(1024)(128)(4,1)} %bitcast.119), calls=%async_computation.7 | async-start | bytes 8388608
  614.3 4.5 copy-start.27
  614.4 4.5 copy-start.29
  614.4 10.3 %slice-start.2 = ((s8[8388608]{0:T(1024)(128)(4,1)}), s8[4194304]{0:T(1024)(128)(4,1)S(1)}, s32[]{:S(2)}) async-start(s8[8388608]{0:T(1024)(128)(4,1)} %bitcast.121), calls=%async_computation.8 | async-start | bytes 8388608
  618.8 5.8 slice-start.3
  618.8 5.8 copy-start.14
  624.6 3.8 copy-start.5
  624.6 3.7 copy-start.13
  624.7 3.7 copy-start.22
  624.7 3.7 copy-start.24
  624.7 3.7 copy-start.28
  637.7 17.2 %copy-start.19 = (s32[2560]{0:T(1024)S(1)}, s32[2560]{0:T(1024)}, u32[]{:S(2)}) copy-start(s32[2560]{0:T(1024)} %copy-done.18) | copy-start | bytes 30724
  637.7 17.6 %copy-start.20 = (f32[2048]{0:T(1024)S(1)}, f32[2048]{0:T(1024)}, u32[]{:S(2)}) copy-start(f32[2048]{0:T(1024)} %get-tuple-element.78) | copy-start | bytes 24580
  650.4 151.7 %collective-permute-start.1 = (bf16[256,2048]{1,0:T(8,128)(2,1)}, bf16[256,2048]{1,0:T(8,128)(2,1)}, u32[]{:S(2)}, u32[]{:S(2)}) collective-permute-start(bf16[256,2048]{1,0:T(8,128)(2,1)} %add_convert_fusion.4), channel_id=1, source_target_pairs={{0,1},{1,2},{2,3},{4,5},{5,6},{6,7},{8,9},{9,10},{10,11},{12,13},{... | collective-permute-start | bytes 3145736 | tf_op jit(solution)/shard_map/ppermute | solution.py:884
  802.0 11.8 %copy-start.9 = (f32[256,2048]{1,0:T(8,128)S(1)}, f32[256,2048]{1,0:T(8,128)}, u32[]{:S(2)}) copy-start(f32[256,2048]{1,0:T(8,128)} %get-tuple-element.36) | copy-start | bytes 6291460
  806.6 28.6 %collective-permute-start.4 = (bf16[256,2048]{1,0:T(8,128)(2,1)}, bf16[256,2048]{1,0:T(8,128)(2,1)S(1)}, u32[]{:S(2)}, u32[]{:S(2)}) collective-permute-start(bf16[256,2048]{1,0:T(8,128)(2,1)} %get-tuple-element.95), channel_id=1, source_target_pairs={{1,0},{2,1},{3,2},{5,4},{6,5},{7,6},{9,8},{10,9},{11,10},{13,12},{... | collective-permute-start | bytes 3145736 | tf_op jit(solution)/shard_map/ppermute | solution.py:885
  813.8 6.1 copy-start.15
  813.8 21.4 %copy-start.8 = (bf16[1024,2048]{1,0:T(8,128)(2,1)S(1)}, bf16[1024,2048]{1,0:T(8,128)(2,1)}, u32[]{:S(2)}) copy-start(bf16[1024,2048]{1,0:T(8,128)(2,1)} %convolution_convert_fusion.3) | copy-start | bytes 12582916
  819.9 29.4 %collective-permute-start.2 = (bf16[256,2048]{1,0:T(8,128)(2,1)S(1)}, bf16[256,2048]{1,0:T(8,128)(2,1)S(1)}, u32[]{:S(2)}, u32[]{:S(2)}) collective-permute-start(bf16[256,2048]{1,0:T(8,128)(2,1)S(1)} %copy-done.15), channel_id=1, source_target_pairs={{0,1},{1,2},{2,3},{4,5},{5,6},{6,7},{8,9},{9,10},{10,11},{12,13},{... | collective-permute-start | bytes 3145736 | tf_op jit(solution)/shard_map/ppermute | solution.py:884
  835.7 26.5 %collective-permute-start.5 = (bf16[256,2048]{1,0:T(8,128)(2,1)S(1)}, bf16[256,2048]{1,0:T(8,128)(2,1)S(1)}, u32[]{:S(2)}, u32[]{:S(2)}) collective-permute-start(bf16[256,2048]{1,0:T(8,128)(2,1)S(1)} %add_convert_fusion.1), channel_id=1, source_target_pairs={{1,0},{2,1},{3,2},{5,4},{6,5},{7,6},{9,8},{10,9},{11,10},{13,12},{... | collective-permute-start | bytes 3145736 | tf_op jit(solution)/shard_map/ppermute | solution.py:885
  873.4 13.3 %copy-start.1 = (f32[32,8]{0,1:T(8,128)S(1)}, f32[32,8]{0,1:T(8,128)}, u32[]{:S(2)}) copy-start(f32[32,8]{0,1:T(8,128)} %param.25) | copy-start | bytes 3076
Sparse Core Ops, SparseCore 0:
  255.4 67.6 reduce-scatter.4
  327.6 81.5 reduce-scatter.2
  411.2 42.4 all-gather.4
  455.6 63.2 all-gather.2

commit v4 on v3

--- a/solution.py
+++ b/solution.py
@@ -19,6 +19,10 @@
 lanes = 128
 bf16 = jnp.bfloat16
 f32 = jnp.float32
+
+
+def cost(micros):
+    return pl.CostEstimate(flops=micros * 10**9, bytes_accessed=10**6, transcendentals=0)
 
 
 def buckets_of(offset):
@@ -276,6 +280,7 @@
                 pltpu.VMEM((2 * group, lanes, length), bf16),
             ],
         ),
+        cost_estimate=cost(25),
         name="attend",
     )(first, last, queries, keys, values, segments[:, None, :], segments[:, :, None], lines)
 
@@ -306,6 +311,7 @@
                 pltpu.VMEM((length, group * lanes), f32),
             ],
         ),
+        cost_estimate=cost(35),
         name="attend_back",
     )(
         first, last, queries, keys, values, grad_mixed, mixed, totals,
@@ -314,123 +320,6 @@
 
 
 mesh_ids = pl.DeviceIdType.MESH
-
-
-def greet_line(me, count, axis):
-    barrier = pltpu.get_barrier_semaphore()
-    has_left, has_right = me > 0, me < count - 1
-    for there, step in ((has_left, -1), (has_right, 1)):
-        @pl.when(there)
-        def _():
-            pl.semaphore_signal(barrier, inc=1, device_id={axis: me + step}, device_id_type=mesh_ids)
-    pl.semaphore_wait(barrier, has_left.astype(jnp.int32) + has_right.astype(jnp.int32))
-
-
-def line_sum_kernel(axis, count, chunks, part_ref, out_ref, land_ref, sum_ref, send_sem, recv_sem, bsend_sem, brecv_sem):
-    me = lax.axis_index(axis)
-    tokens = part_ref.shape[0]
-    size = tokens // (2 * chunks)
-    greet_line(me, count, axis)
-
-    def rows(flow, chunk):
-        return pl.ds(pl.multiple_of((flow * chunks + chunk) * size, size), size)
-
-    def toward(flow):
-        return me + 1 if flow == 0 else me - 1
-
-    def back(flow):
-        return me - 1 if flow == 0 else me + 1
-
-    def place(flow):
-        return me if flow == 0 else count - 1 - me
-
-    def sum_copy(flow, chunk, source_ref):
-        here = rows(flow, chunk)
-        return pltpu.make_async_remote_copy(
-            src_ref=source_ref.at[here], dst_ref=land_ref.at[here],
-            send_sem=send_sem.at[flow, chunk], recv_sem=recv_sem.at[flow, chunk],
-            device_id={axis: toward(flow)}, device_id_type=mesh_ids,
-        )
-
-    def out_copy(flow, chunk):
-        here = rows(flow, chunk)
-        return pltpu.make_async_remote_copy(
-            src_ref=out_ref.at[here], dst_ref=out_ref.at[here],
-            send_sem=bsend_sem.at[flow, chunk], recv_sem=brecv_sem.at[flow, chunk],
-            device_id={axis: back(flow)}, device_id_type=mesh_ids,
-        )
-
-    def step(time, carry):
-        for flow in range(2):
-            chunk = time - place(flow)
-            here = rows(flow, chunk)
-            valid = (chunk >= 0) & (chunk < chunks)
-
-            @pl.when(valid & (place(flow) == 0))
-            def _():
-                sum_copy(flow, chunk, part_ref).start()
-
-            @pl.when(valid & (place(flow) > 0))
-            def _():
-                sum_copy(flow, chunk, sum_ref).wait_recv()
-
-            @pl.when(valid & (place(flow) > 0) & (place(flow) < count - 1))
-            def _():
-                sum_ref[here, :] = add_low(land_ref[here, :], part_ref[here, :])
-                sum_copy(flow, chunk, sum_ref).start()
-
-            @pl.when(valid & (place(flow) == count - 1))
-            def _():
-                out_ref[here, :] = add_low(land_ref[here, :], part_ref[here, :])
-                out_copy(flow, chunk).start()
-        for flow in range(2):
-            chunk = time - 2 * (count - 1) + place(flow)
-            valid = (chunk >= 0) & (chunk < chunks) & (place(flow) < count - 1)
-
-            @pl.when(valid)
-            def _():
-                out_copy(flow, chunk).wait_recv()
-
-            @pl.when(valid & (place(flow) > 0))
-            def _():
-                out_copy(flow, chunk).start()
-        return carry
-
-    lax.fori_loop(0, chunks + 2 * (count - 1), step, 0)
-
-    def drain(chunk, carry):
-        for flow in range(2):
-            @pl.when(place(flow) < count - 1)
-            def _():
-                sum_copy(flow, chunk, part_ref).wait_send()
-
-            @pl.when(place(flow) > 0)
-            def _():
-                out_copy(flow, chunk).wait_send()
-        return carry
-
-    lax.fori_loop(0, chunks, drain, 0)
-
-
-def line_sum(part, axis, chunks, cid):
-    count = lax.axis_size(axis)
-    tokens, width = part.shape
-    return pl.pallas_call(
-        functools.partial(line_sum_kernel, axis, count, chunks),
-        out_shape=jax.ShapeDtypeStruct(part.shape, bf16),
-        in_specs=[pl.BlockSpec(memory_space=pltpu.VMEM)],
-        out_specs=pl.BlockSpec(memory_space=pltpu.VMEM),
-        scratch_shapes=[
-            pltpu.VMEM(part.shape, bf16),
-            pltpu.VMEM(part.shape, bf16),
-            pltpu.SemaphoreType.DMA((2, chunks)),
-            pltpu.SemaphoreType.DMA((2, chunks)),
-            pltpu.SemaphoreType.DMA((2, chunks)),
-            pltpu.SemaphoreType.DMA((2, chunks)),
-        ],
-        compiler_params=pltpu.CompilerParams(collective_id=cid, has_side_effects=True),
-        name="line_sum",
-    )(part)
 
 
 def add_low(left_side, right_side):
@@ -775,10 +664,351 @@
                 self.line_copy(there, self.line_me).wait_send()
 
 
-def tail_kernel(line_axis, count, subs, cube_axis, bits, lag, widths, *refs):
+class LineSum:
+    def __init__(self, axis, count, chunks, part_ref, total_ref, land_ref, send_sem, recv_sem,
+                 back_send_sem, back_recv_sem, ready):
+        self.axis, self.count, self.chunks, self.ready = axis, count, chunks, ready
+        self.part_ref, self.total_ref, self.land_ref = part_ref, total_ref, land_ref
+        self.sems = (send_sem, recv_sem, back_send_sem, back_recv_sem)
+        self.me = lax.axis_index(axis)
+        self.size = part_ref.shape[0] // (2 * chunks)
+        self.steps = chunks + 2 * (count - 1)
+
+    @staticmethod
+    def scratch(chunks, shape):
+        return [pltpu.VMEM(shape, bf16)] * 3 + [pltpu.SemaphoreType.DMA((2, chunks))] * 4
+
+    def start(self, flow, chunk):
+        return pl.multiple_of((flow * self.chunks + chunk) * self.size, self.size)
+
+    def place(self, flow):
+        return self.me if flow == 0 else self.count - 1 - self.me
+
+    def copy(self, flow, chunk, source_ref):
+        here = pl.ds(self.start(flow, chunk), self.size)
+        return pltpu.make_async_remote_copy(
+            src_ref=source_ref.at[here], dst_ref=self.land_ref.at[here],
+            send_sem=self.sems[0].at[flow, chunk], recv_sem=self.sems[1].at[flow, chunk],
+            device_id={self.axis: self.me + 1 if flow == 0 else self.me - 1},
+            device_id_type=mesh_ids,
+        )
+
+    def back_copy(self, flow, chunk):
+        here = self.total_ref.at[pl.ds(self.start(flow, chunk), self.size)]
+        return pltpu.make_async_remote_copy(
+            src_ref=here, dst_ref=here,
+            send_sem=self.sems[2].at[flow, chunk], recv_sem=self.sems[3].at[flow, chunk],
+            device_id={self.axis: self.me - 1 if flow == 0 else self.me + 1},
+            device_id_type=mesh_ids,
+        )
+
+    def step(self, time):
+        last = self.count - 1
+        for flow in range(2):
+            place = self.place(flow)
+            chunk = time - place
+            valid = (chunk >= 0) & (chunk < self.chunks)
+            here = pl.ds(self.start(flow, chunk), self.size)
+
+            @pl.when(valid & (place == 0))
+            def _():
+                self.copy(flow, chunk, self.part_ref).start()
+
+            @pl.when(valid & (place > 0))
+            def _():
+                self.copy(flow, chunk, self.part_ref).wait_recv()
+
+            @pl.when(valid & (place > 0) & (place < last))
+            def _():
+                self.land_ref[here, :] = add_low(self.land_ref[here, :], self.part_ref[here, :])
+                self.copy(flow, chunk, self.land_ref).start()
+
+            @pl.when(valid & (place == last))
+            def _():
+                self.total_ref[here, :] = add_low(self.land_ref[here, :], self.part_ref[here, :])
+                self.back_copy(flow, chunk).start()
+        for flow in range(2):
+            place = self.place(flow)
+            chunk = time - 2 * last + place
+            valid = (chunk >= 0) & (chunk < self.chunks)
+
+            @pl.when(valid & (place < last))
+            def _():
+                self.back_copy(flow, chunk).wait_recv()
+
+            @pl.when(valid & (place < last) & (place > 0))
+            def _():
+                self.back_copy(flow, chunk).start()
+
+            @pl.when(valid)
+            def _():
+                self.ready(flow, chunk, self.start(flow, chunk))
+
+    def finish(self):
+        last = self.count - 1
+
+        def drain(chunk, carry):
+            for flow in range(2):
+                @pl.when(self.place(flow) < last)
+                def _():
+                    self.copy(flow, chunk, self.part_ref).wait_send()
+
+                @pl.when(self.place(flow) > 0)
+                def _():
+                    self.back_copy(flow, chunk).wait_send()
+            return carry
+
+        lax.fori_loop(0, self.chunks, drain, 0)
+
+
+class BlockedProduct:
+    def __init__(self, left_ref, right_ref, transposed, out_ref, stage_ref, sem, first, before):
+        self.left_ref, self.right_ref, self.transposed = left_ref, right_ref, transposed
+        self.out_ref, self.stage_ref, self.sem = out_ref, stage_ref, sem
+        self.first, self.before = first, before
+        self.columns = stage_ref.shape[2]
+        self.blocks = out_ref.shape[1] // self.columns
+        self.steps = first + self.blocks
+
+    def store(self, block, slot):
+        there = pl.ds(pl.multiple_of(block * self.columns, self.columns), self.columns)
+        return pltpu.make_async_copy(
+            self.stage_ref.at[slot], self.out_ref.at[:, there], self.sem.at[slot]
+        )
+
+    def step(self, time):
+        block = time - self.first
+        slot = block % 2
+        start = pl.multiple_of(block * self.columns, self.columns)
+        there = pl.ds(start, self.columns)
+        pl.when(block == 0)(self.before)
+
+        @pl.when((block >= 2) & (block < self.blocks))
+        def _():
+            self.store(block - 2, slot).wait()
+
+        @pl.when((block >= 0) & (block < self.blocks))
+        def _():
+            def rows(index, carry):
+                here = pl.ds(pl.multiple_of(index * tile, tile), tile)
+                if self.transposed:
+                    value = dot_nt(self.left_ref[here, :], self.right_ref[there, :])
+                else:
+                    value = dot_nn(self.left_ref[here, :], self.right_ref[:, there])
+                self.stage_ref[slot, here, :] = value.astype(self.stage_ref.dtype)
+                return carry
+
+            lax.fori_loop(0, self.left_ref.shape[0] // tile, rows, 0)
+            self.store(block, slot).start()
+
+    def finish(self):
+        for block in range(max(self.blocks - 2, 0), self.blocks):
+            self.store(block, block % 2).wait()
+
+
+def run_parts(parts):
+    def step(time, carry):
+        for part in parts:
+            part.step(time)
+        return carry
+
+    lax.fori_loop(0, max(part.steps for part in parts), step, 0)
+    for part in parts:
+        part.finish()
+
+
+class Stores:
+    def __init__(self, chunks, size, start, pairs):
+        self.chunks, self.size, self.start, self.pairs = chunks, size, start, pairs
+
+    def copies(self, flow, chunk):
+        here = pl.ds(self.start(flow, chunk), self.size)
+        return [
+            pltpu.make_async_copy(source.at[here], target.at[here], sem.at[flow, chunk])
+            for source, target, sem in self.pairs
+        ]
+
+    def begin(self, flow, chunk):
+        for copy in self.copies(flow, chunk):
+            copy.start()
+
+    def finish(self):
+        def wait(chunk, carry):
+            for flow in range(2):
+                for copy in self.copies(flow, chunk):
+                    copy.wait()
+            return carry
+
+        lax.fori_loop(0, self.chunks, wait, 0)
+
+
+def enter_kernel(
+    axis, count, chunks, part_hbm, x_hbm, grad_hbm, w_hbm, gain_ref, total_hbm, normed_hbm, hidden_hbm,
+    x_ref, normed_ref, grad_ref, w_ref, stage_ref, load_sem, stage_sem, store_sem, *line_scratch,
+):
+    loads = [
+        pltpu.make_async_copy(source, target, load_sem.at[index])
+        for index, (source, target) in enumerate(
+            ((part_hbm, line_scratch[0]), (x_hbm, x_ref), (grad_hbm, grad_ref), (w_hbm, w_ref))
+        )
+    ]
+    for load in loads:
+        load.start()
+    greet(axis, count, None, 0)
+
+    def ready(flow, chunk, start):
+        here = pl.ds(start, line.size)
+        middle = x_ref[here, :].astype(f32) + line.total_ref[here, :].astype(f32)
+        scale = lax.rsqrt(jnp.mean(middle * middle, axis=-1, keepdims=True) + 1e-06)
+        normed_ref[here, :] = (middle * scale * gain_ref[...]).astype(bf16)
+        stores.begin(flow, chunk)
+
+    line = LineSum(axis, count, chunks, *line_scratch, ready)
+    stores = Stores(
+        chunks, line.size, line.start,
+        [(line.total_ref, total_hbm, store_sem.at[0]), (normed_ref, normed_hbm, store_sem.at[1])],
+    )
+
+    def before():
+        loads[1].wait()
+        loads[2].wait()
+        loads[3].wait()
+
+    product = BlockedProduct(
+        grad_ref, w_ref, True, hidden_hbm, stage_ref, stage_sem, 1, before
+    )
+    loads[0].wait()
+    run_parts([line, product])
+    stores.finish()
+
+
+def enter_ffn(part, x, grad, w_down, gain, axis, chunks, cid):
+    count = lax.axis_size(axis)
+    tokens, width = part.shape
+    hbm = pl.BlockSpec(memory_space=pl.ANY)
+    whole = pltpu.VMEM((tokens, width), bf16)
+    return pl.pallas_call(
+        functools.partial(enter_kernel, axis, count, chunks),
+        out_shape=(
+            jax.ShapeDtypeStruct((tokens, width), bf16),
+            jax.ShapeDtypeStruct((tokens, width), bf16),
+            jax.ShapeDtypeStruct((tokens, w_down.shape[0]), f32),
+        ),
+        in_specs=[hbm] * 4 + [pl.BlockSpec(memory_space=pltpu.VMEM)],
+        out_specs=[hbm] * 3,
+        scratch_shapes=[
+            whole, whole, whole, pltpu.VMEM(w_down.shape, bf16),
+            pltpu.VMEM((2, tokens, lanes), f32),
+            pltpu.SemaphoreType.DMA((4,)),
+            pltpu.SemaphoreType.DMA((2,)),
+            pltpu.SemaphoreType.DMA((2, 2, chunks)),
+            *LineSum.scratch(chunks, part.shape),
+        ],
+        compiler_params=pltpu.CompilerParams(
+            collective_id=cid, has_side_effects=True, vmem_limit_bytes=63 * 2**20
+        ),
+        cost_estimate=cost(110),
+        name="enter_ffn",
+    )(part, x, grad, w_down, gain[None])
+
+
+def leave_kernel(
+    axis, count, chunks, part_hbm, x_hbm, attn_hbm, grad_hbm, hidden_hbm, w_hbm, gain_ref,
+    branch_hbm, ffn_hbm, share_ref, sum_ref,
+    x_ref, attn_ref, grad_ref, hidden_ref, w_ref, branch_ref, stage_ref, load_sem, stage_sem, store_sem,
+    *line_scratch,
+):
+    loads = [
+        pltpu.make_async_copy(source, target, load_sem.at[index])
+        for index, (source, target) in enumerate(
+            (
+                (part_hbm, line_scratch[0]), (hidden_hbm, hidden_ref), (w_hbm, w_ref),
+                (x_hbm, x_ref), (attn_hbm, attn_ref), (grad_hbm, grad_ref),
+            )
+        )
+    ]
+    for load in loads:
+        load.start()
+    greet(axis, count, None, 0)
+    sum_ref[...] = jnp.zeros_like(sum_ref)
+    share_rows = share_ref.shape[0]
+
+    def ready(flow, chunk, start):
+        here = pl.ds(start, line.size)
+        middle = x_ref[here, :].astype(f32) + attn_ref[here, :].astype(f32)
+        scale = lax.rsqrt(jnp.mean(middle * middle, axis=-1, keepdims=True) + 1e-06)
+        grad_normed = line.total_ref[here, :].astype(f32)
+        hat = middle * scale
+        grad_hat = grad_normed * gain_ref[...]
+        inner = jnp.mean(grad_hat * hat, axis=-1, keepdims=True)
+        grad_middle = grad_ref[here, :].astype(f32) + scale * (grad_hat - hat * inner)
+        branch_ref[here, :] = grad_middle.astype(bf16)
+        sum_ref[...] = sum_ref[...] + jnp.sum(grad_normed * hat, axis=0, keepdims=True)
+
+        @pl.when(start // share_rows == line.me)
+        def _():
+            mine = pl.ds(pl.multiple_of(start % share_rows, line.size), line.size)
+            share_ref[mine, :] = grad_middle
+
+        stores.begin(flow, chunk)
+
+    line = LineSum(axis, count, chunks, *line_scratch, ready)
+    stores = Stores(
+        chunks, line.size, line.start, [(branch_ref, branch_hbm, store_sem)]
+    )
+
+    def before():
+        for load in loads[1:]:
+            load.wait()
+
+    product = BlockedProduct(
+        hidden_ref, w_ref, False, ffn_hbm, stage_ref, stage_sem, 0, before
+    )
+    loads[0].wait()
+    run_parts([line, product])
+    stores.finish()
+
+
+def leave_ffn(part, x, attn_total, grad, hidden, w_down, gain, axis, chunks, cid):
+    count = lax.axis_size(axis)
+    tokens, width = part.shape
+    hbm = pl.BlockSpec(memory_space=pl.ANY)
+    vmem = pl.BlockSpec(memory_space=pltpu.VMEM)
+    whole = pltpu.VMEM((tokens, width), bf16)
+    return pl.pallas_call(
+        functools.partial(leave_kernel, axis, count, chunks),
+        out_shape=(
+            jax.ShapeDtypeStruct((tokens, width), bf16),
+            jax.ShapeDtypeStruct((tokens, width), bf16),
+            jax.ShapeDtypeStruct((tokens // count, width), f32),
+            jax.ShapeDtypeStruct((1, width), f32),
+        ),
+        in_specs=[hbm] * 6 + [vmem],
+        out_specs=[hbm, hbm, vmem, vmem],
+        scratch_shapes=[
+            whole, whole, whole, pltpu.VMEM(hidden.shape, bf16), pltpu.VMEM(w_down.shape, bf16),
+            whole,
+            pltpu.VMEM((2, tokens, tile), bf16),
+            pltpu.SemaphoreType.DMA((6,)),
+            pltpu.SemaphoreType.DMA((2,)),
+            pltpu.SemaphoreType.DMA((2, chunks)),
+            *LineSum.scratch(chunks, part.shape),
+        ],
+        compiler_params=pltpu.CompilerParams(
+            collective_id=cid, has_side_effects=True, vmem_limit_bytes=63 * 2**20
+        ),
+        cost_estimate=cost(110),
+        name="leave_ffn",
+    )(part, x, attn_total, grad, hidden, w_down, gain[None])
+
+
+def tail_kernel(line_axis, count, subs, cube_axis, bits, lag, widths, out_width, *refs):
     part_ref, small_ref, *grad_refs = refs[: 2 + len(widths)]
-    share_ref, small_cube_ref, small_all_ref, sums_ref = refs[2 + len(widths) : 6 + len(widths)]
-    scratch = list(refs[6 + len(widths) :])
+    refs = refs[2 + len(widths) :]
+    share_ref, small_cube_ref, small_all_ref = refs[:3]
+    out_count = sum(widths) // out_width
+    sum_refs = refs[3 : 3 + out_count]
+    scratch = list(refs[3 + out_count :])
     data_ref, total_ref, load_sem, store_sem = scratch[:4]
     line_scratch, scratch = scratch[4:7], scratch[7:]
     cube_scratch, small_scratch = scratch[: bits + 4], scratch[bits + 4 :]
@@ -787,11 +1017,19 @@
     def load(chunk, source):
         return pltpu.make_async_copy(source, data_ref.at[chunk], load_sem.at[chunk])
 
-    def store(chunk):
-        there = pl.ds(pl.multiple_of(chunk * columns, columns), columns)
+    per_out = out_width // columns
+
+    def store(chunk, index=0):
+        there = pl.ds(pl.multiple_of(chunk % per_out * columns, columns), columns)
         return pltpu.make_async_copy(
-            total_ref.at[chunk], sums_ref.at[:, there], store_sem.at[chunk]
+            total_ref.at[chunk], sum_refs[index].at[:, there], store_sem.at[chunk]
         )
+
+    def store_any(chunk):
+        for index in range(out_count):
+            @pl.when(chunk // per_out == index)
+            def _():
+                store(chunk, index).start()
 
     chunk = 0
     for grad_ref, width in zip(grad_refs, widths):
@@ -804,7 +1042,7 @@
         CubeSum(
             cube_axis, bits, data_ref, total_ref, cube_scratch[:bits], *cube_scratch[bits:], lag,
             lambda chunk: load(chunk, grad_refs[0].at[:, :columns]).wait(),
-            lambda chunk: store(chunk).start(),
+            store_any,
         ),
         SmallSum(
             cube_axis, bits, line_axis, count, 2, small_ref, small_cube_ref, small_all_ref,
@@ -828,7 +1066,7 @@
     lax.fori_loop(0, chunks, stored, 0)
 
 
-def tail_sums(part, small, grads, line_axis, cube_axis, columns, subs, lag, cid):
+def tail_sums(part, small, grads, line_axis, cube_axis, out_width, columns, subs, lag, cid):
     count = lax.axis_size(line_axis)
     bits = lax.axis_size(cube_axis).bit_length() - 1
     rows = grads[0].shape[0]
@@ -838,15 +1076,17 @@
     hbm = pl.BlockSpec(memory_space=pl.ANY)
     small_shape = jax.ShapeDtypeStruct(small.shape, f32)
     return pl.pallas_call(
-        functools.partial(tail_kernel, line_axis, count, subs, cube_axis, bits, lag, widths),
+        functools.partial(
+            tail_kernel, line_axis, count, subs, cube_axis, bits, lag, widths, out_width
+        ),
         out_shape=(
             jax.ShapeDtypeStruct((part.shape[0] // count, part.shape[1]), f32),
             small_shape,
             small_shape,
-            jax.ShapeDtypeStruct((rows, sum(widths)), bf16),
+            *[jax.ShapeDtypeStruct((rows, out_width), bf16)] * (sum(widths) // out_width),
         ),
         in_specs=[vmem, vmem] + [hbm] * len(grads),
-        out_specs=[vmem, vmem, vmem, hbm],
+        out_specs=[vmem, vmem, vmem] + [hbm] * (sum(widths) // out_width),
         scratch_shapes=[
             pltpu.VMEM((chunks, rows, columns), bf16),
             pltpu.VMEM((chunks, rows, columns), bf16),
@@ -859,31 +1099,52 @@
         compiler_params=pltpu.CompilerParams(
             collective_id=cid, has_side_effects=True, vmem_limit_bytes=63 * 2**20
         ),
+        cost_estimate=cost(110),
         name="tail_sums",
     )(part, small, *grads)
 
 
-def line_scatter(part, axis):
-    count = lax.axis_size(axis)
-    me = lax.axis_index(axis)
-    share = part.shape[0] // count
-
-    def block(owner):
-        owner = jnp.clip(owner, 0, count - 1)
-        return lax.dynamic_slice_in_dim(part, owner * share, share, 0)
-
-    right = [(index, index + 1) for index in range(count - 1)]
-    left = [(index + 1, index) for index in range(count - 1)]
-    from_left = from_right = None
-    for time in range(count - 1):
-        to_right = block(count - 1 - time + me)
-        to_left = block(time - (count - 1) + me)
-        if time > 0:
-            to_right = add_low(to_right, from_left)
-            to_left = add_low(to_left, from_right)
-        from_left = lax.ppermute(to_right, axis, right)
-        from_right = lax.ppermute(to_left, axis, left)
-    return block(me).astype(f32) + from_left.astype(f32) + from_right.astype(f32)
+def after(value, other):
+    return lax.optimization_barrier((value, other))[0]
+
+
+class PermutedScatter:
+    def __init__(self, part, axis):
+        self.part, self.axis = part, axis
+        self.count = lax.axis_size(axis)
+        self.me = lax.axis_index(axis)
+        self.share = part.shape[0] // self.count
+        self.time = 0
+        self.arrived = None
+
+    def block(self, owner):
+        owner = jnp.clip(owner, 0, self.count - 1)
+        return lax.dynamic_slice_in_dim(self.part, owner * self.share, self.share, 0)
+
+    def hop(self, *others):
+        if self.time >= self.count - 1:
+            return others
+        to_right = self.block(self.count - 1 - self.time + self.me)
+        to_left = self.block(self.time - (self.count - 1) + self.me)
+        if self.arrived is not None:
+            to_right = add_low(to_right, self.arrived[0])
+            to_left = add_low(to_left, self.arrived[1])
+        to_right, to_left, *others = lax.optimization_barrier((to_right, to_left, *others))
+        right = [(index, index + 1) for index in range(self.count - 1)]
+        left = [(index + 1, index) for index in range(self.count - 1)]
+        self.arrived = (
+            lax.ppermute(to_right, self.axis, right), lax.ppermute(to_left, self.axis, left)
+        )
+        self.time += 1
+        return others
+
+    def total(self):
+        while self.time < self.count - 1:
+            self.hop()
+        return (
+            self.block(self.me).astype(f32)
+            + self.arrived[0].astype(f32) + self.arrived[1].astype(f32)
+        )
 
 
 def project(left_side, right_side):
@@ -944,11 +1205,10 @@
     mixed, totals = attend(queries, keys, values, segments, lines)
     mixed_flat = mixed.reshape(token_count, local_width)
     attn_part = project(mixed_flat, w_out)
-    attn_total = line_sum(attn_part.astype(bf16), "tensor", line_chunks, 0).astype(f32)
-    grad_hidden = project_back(grad_out, w_down)
-    middle = flat_inputs + attn_total
-    scale_ffn = norm_scale(middle)
-    normed_ffn = (middle * scale_ffn * gain_ffn).astype(bf16)
+    attn_total, normed_ffn, grad_hidden = enter_ffn(
+        attn_part.astype(bf16), inputs.reshape(token_count, model_width), grad_out, w_down,
+        gain_ffn, "tensor", line_chunks, 0,
+    )
     gate_pre = project(normed_ffn, w_gate)
     up_pre = project(normed_ffn, w_up)
     act_value, act_pull = jax.vjp(lambda signal: jax.nn.gelu(signal, approximate=True), gate_pre)
@@ -956,32 +1216,30 @@
     grad_gate = act_pull(grad_hidden * up_pre)[0].astype(bf16)
     grad_up = (grad_hidden * act_value).astype(bf16)
     norm_ffn_part = project_back(grad_gate, w_gate) + project_back(grad_up, w_up)
-    normed_ffn_hat = middle * scale_ffn
-    gain_ffn_part = jnp.sum(norm_ffn_part * normed_ffn_hat, axis=0)
     gate_up_grad = weight_term(normed_ffn, jnp.concatenate([grad_gate, grad_up], axis=1))
     down_grad = weight_term(hidden, grad_out)
     norm_ffn_low, gate_up_grad, down_grad = lax.optimization_barrier(
         (norm_ffn_part.astype(bf16), gate_up_grad, down_grad)
     )
-    grad_normed_ffn = line_sum(norm_ffn_low, "tensor", line_chunks, 0).astype(f32)
-
-    def reduce_all(grad, axis):
-        part = lax.psum_scatter(grad, "dp", scatter_dimension=axis, tiled=True)
-        return lax.all_gather(part, "dp", axis=axis, tiled=True)
-
-    gate_up_grad = reduce_all(gate_up_grad, 0)
-    down_grad = reduce_all(down_grad, 1).astype(f32)
-    gate_grad, up_grad = jnp.split(gate_up_grad.astype(f32), 2, axis=1)
-    ffn_part = project(hidden, w_down).astype(bf16)
-    ffn_part, grad_normed_ffn = lax.optimization_barrier((ffn_part, grad_normed_ffn))
-    ffn_share = line_scatter(ffn_part, "tensor")
-    output = (take_share(middle) + ffn_share).reshape(share_shape).astype(bf16)
-    grad_middle = grad_out.astype(f32) + norm_back(middle, scale_ffn, gain_ffn, grad_normed_ffn)
-    grad_branch = grad_middle.astype(bf16)
+    grad_branch, ffn_part, grad_middle_share, gain_ffn_part = leave_ffn(
+        norm_ffn_low, inputs.reshape(token_count, model_width), attn_total, grad_out, hidden, w_down,
+        gain_ffn, "tensor", line_chunks, 1,
+    )
+    gate_up_piece = lax.psum_scatter(gate_up_grad, "dp", scatter_dimension=0, tiled=True)
+    down_piece = lax.psum_scatter(down_grad, "dp", scatter_dimension=1, tiled=True)
+    down_piece = after(down_piece, grad_branch)
+    down_grad = lax.all_gather(down_piece, "dp", axis=1, tiled=True).astype(f32)
+    scatter = PermutedScatter(ffn_part, "tensor")
+    scatter.hop()
     grad_mixed = project_back(grad_branch, w_out).astype(bf16).reshape(heads_shape)
+    (grad_mixed,) = scatter.hop(grad_mixed)
     grad_query, grad_key, grad_value, sums = attend_back(
         queries, keys, values, grad_mixed, mixed, totals, segments, lines
     )
+    gate_up_piece = after(gate_up_piece, grad_query)
+    gate_up_grad = lax.all_gather(gate_up_piece, "dp", axis=0, tiled=True)
+    gate_grad, up_grad = jnp.split(gate_up_grad.astype(f32), 2, axis=1)
+    grad_query, grad_key, grad_value = scatter.hop(grad_query, grad_key, grad_value)
     grad_query = grad_query.reshape(token_count, local_width)
     grad_key = grad_key.reshape(token_count, local_width)
     grad_value = grad_value.reshape(token_count, local_width)
@@ -996,18 +1254,21 @@
     qkv_grad = weight_term(normed, jnp.concatenate([grad_query, grad_key, grad_value], axis=1))
     out_grad = weight_term(grad_branch, mixed_flat)
     table_line = jnp.pad(table_grad.reshape(-1), (0, model_width - bucket_count * head_count))
-    small = jnp.stack([gain_attn_part, gain_ffn_part, table_line])
+    small = jnp.stack([gain_attn_part, gain_ffn_part[0], table_line])
     small = jnp.pad(small, ((0, 8 - small.shape[0]), (0, 0)))
-    grad_normed_attn, small_cube, small_all, attn_sums = tail_sums(
+    ffn_share = scatter.total()
+    middle_share = take_share(inputs).astype(f32) + take_share(attn_total).astype(f32)
+    output = (middle_share + ffn_share).reshape(share_shape).astype(bf16)
+    grad_normed_attn, small_cube, small_all, *attn_sums = tail_sums(
         norm_attn_part.astype(bf16), small, [qkv_grad, out_grad], "tensor", "dp",
-        tail_columns, tail_subs, tail_lag, 1,
-    )
-    query_grad, key_grad, value_grad, out_grad = jnp.split(attn_sums.astype(f32), 4, axis=1)
+        local_width, tail_columns, tail_subs, tail_lag, 2,
+    )
+    query_grad, key_grad, value_grad, out_grad = [grad.astype(f32) for grad in attn_sums]
     out_grad = jnp.transpose(out_grad)
-    gain_attn_grad, gain_ffn_grad = small_all[0], small_all[1]
+    gain_attn_grad, gain_ffn_grad = small_all[0], small_cube[1]
     table_grad = small_cube[2, : bucket_count * head_count].reshape(bucket_count, head_count)
     inputs_share = take_share(flat_inputs)
-    grad_input = take_share(grad_middle) + norm_back(
+    grad_input = grad_middle_share + norm_back(
         inputs_share, take_share(scale_attn), gain_attn, grad_normed_attn
     )
     input_grad = grad_input.reshape(share_shape).astype(bf16)

time: 902 us -> 663 us (0.74)
  waiting for transfers between devices: 180 us -> 9.84 us
  other arithmetic: 84.2 us -> 49.5 us
  matrix products: 143 us -> 121 us
  local copies, waits for them, and re-layouts: 41.9 us -> 29.5 us
    reduce_scatter x2, waiting for transfers between devices: 153 us -> 0.04 us  [the longest x1 0.02 us: shards(): lax.psum_scatter(down_grad, 'dp', scatter_dimension=1, tiled=True)]
    dot_general x7 -> x6, matrix products: 65.4 us -> 44.7 us  [dot_nt(): lax.dot_general(left_side, right_side, (((1,), (1,)), ((), ())), preferre...]
    ppermute x6, waiting for transfers between devices: 26.3 us -> 9.05 us  [the longest x3 8.24 us: hop(): lax.ppermute(to_left, self.axis, left)]
    convert_element_type x5, other arithmetic: 32 us -> 20.3 us  [the longest x1 8.02 us: shards(): down_grad = lax.all_gather(down_piece, 'dp', axis=1, tiled=True).astype(f32)]
    add x1 -> x0, other arithmetic: 9.84 us -> none  [shards(): grad_out.astype(f32)]
    reduce_sum x1 -> x0, other arithmetic: 9.6 us -> none  [shards(): gain_ffn_part = jnp.sum(norm_ffn_part * normed_ffn_hat, axis=0)]
    dot_general x7 -> x6, matrix products: 40.4 us -> 38.1 us  [project(): return jnp.dot(left_side, right_side, preferred_element_type=f32)]
  transfers between devices with their start and end apart: 10 -> 10, of which waited for: 4 -> 2; matrix products, arithmetic and copies ran while one was open for 16% -> 15% of each run, Pallas kernels for 30% -> 42%
where the time goes in v4:
time: 663 us; the launch traced here: 657 us
  Pallas kernels  413 us (62%)
  matrix products  121 us (18%)
  other arithmetic  49.5 us (7%)
  local copies, waits for them, and re-layouts  29.5 us (4%)
  starting transfers between devices  19 us (3%)
  between operations  14.5 us (2%)
  waiting for transfers between devices  9.84 us (1%)
    pallas_call x1, Pallas kernels, tail_sums(): pl.pallas_call(functools.partial(tail_kernel, line_axis, count, subs, cub...  123 us
    pallas_call x1, Pallas kernels, leave_ffn(): pl.pallas_call(functools.partial(leave_kernel, axis, count, chunks), out_...  118 us
    pallas_call x1, Pallas kernels, enter_ffn(): pl.pallas_call(functools.partial(enter_kernel, axis, count, chunks), out_...  109 us
    dot_general x6, matrix products, dot_nt(): lax.dot_general(left_side, right_side, (((1,), (1,)), ((), ())), preferre...  44.7 us
    dot_general x4, matrix products, weight_term(): lax.dot_general(left_side, right_side, (((0,), (0,)), ((), ())), preferre...  38.1 us
    dot_general x6, matrix products, project(): return jnp.dot(left_side, right_side, preferred_element_type=f32)  38.1 us
    pallas_call x1, Pallas kernels, attend_back(): pl.pallas_call(functools.partial(backward_kernel, block_count), out_shape...  36.5 us
    pallas_call x1, Pallas kernels, attend(): pl.pallas_call(functools.partial(forward_kernel, block_count), out_shape=...  26.3 us
  transfers between devices with their start and end apart: 10, of which 2 were waited for; matrix products, arithmetic and copies ran while one was open for 15% of the time, Pallas kernels for 42%

profile of v4, /device:TPU:17, one launch (start us, length us, event | category | flops | bytes accessed | tf_op | source)
XLA Modules:
  0.0 656.7 jit_solution(16499677370112553542)
XLA Ops:
  7.3 0.5 broadcast.277
  7.8 1.3 reduce.9
  9.2 0.1 copy.49
  9.3 0.1 copy.48
  9.4 0.7 convert_reduce_fusion
  10.1 0.5 broadcast_add_fusion.last_ref
  10.6 3.1 multiply_reduce_fusion.1
  13.8 5.1 fusion.17.q_ref
  18.9 3.4 fusion.18.k_ref
  22.3 3.4 fusion.19.v_ref
  25.6 1.0 copy.40.seg_col_ref
  26.8 0.2 fusion.26
  27.0 0.7 copy.41.line_ref
  27.7 26.3 %attend.1 = (bf16[1,1024,512]{2,1,0:T(8,128)(2,1)}, f32[1,4,2,1024]{3,2,1,0:T(2,128)}) custom-call(s32[4]{0:T(128)} %get-tuple-element.119.first_ref, s32[4]{0:T(128)} %broadcast_add_fusion.last_ref, bf16[1,1024,512]{2,1,0:T(8,128)(2,1)} %fusion.17.q_ref, bf16[1,1024,512]{2,1,0:T(8,128)(2,1)} %fusion.18.k_ref, bf16[1,1024,512]{2,1,0:T(8,128)(2,1)} %fusion.19.v_ref, ...), custom_call_target="tpu_custom_call" | custom-call | flops 24999999488 | bytes 1000000 | tf_op jit(solution)/shard_map/attend/pallas_call | solution.py:267
  54.0 5.6 convolution_convert_fusion.3.part_hbm
  59.6 108.9 %enter_ffn.1 = (bf16[1024,2048]{1,0:T(8,128)(2,1)}, bf16[1024,2048]{1,0:T(8,128)(2,1)}, f32[1024,1280]{1,0:T(8,128)}) custom-call(bf16[1024,2048]{1,0:T(8,128)(2,1)} %convolution_convert_fusion.3.part_hbm, bf16[1024,2048]{1,0:T(8,128)(2,1)} %bitcast.82, bf16[1024,2048]{1,0:T(8,128)(2,1)} %bitcast.98, bf16[1280,2048]{1,0:T(8,128)(2,1)} %w_hbm.3, ...), custom_call_target="tpu_custom_call" | custom-call | flops 109999996928 | bytes 1000000 | tf_op jit(solution)/shard_map/enter_ffn/pallas_call | solution.py:890
  168.6 9.0 %fusion.41 = f32[1024,1280]{1,0:T(8,128)S(1)} fusion(bf16[1024,2048]{1,0:T(8,128)(2,1)} %get-tuple-element.50, bf16[2048,1280]{1,0:T(8,128)(2,1)} %param.20), kind=kOutput, calls=%fused_computation.86 | convolution fusion | flops 5368709120 | bytes 14680064 | tf_op jit(solution)/shard_map/dot_general | solution.py:1151
  177.7 11.6 %multiply_convert_fusion.1 = (bf16[1024,1280]{1,0:T(8,128)(2,1)S(1)}, bf16[1024,1280]{1,0:T(8,128)(2,1)}, bf16[1024,1280]{1,0:T(8,128)(2,1)}) fusion(f32[1024,1280]{1,0:T(8,128)S(1)} %fusion.41, f32[1024,1280]{1,0:T(8,128)} %get-tuple-element.49, bf16[1024,2048]{1,0:T(8,128)(2,1)S(1)} %copy-done.32, bf16[2048,1280]{1,0:T(8,128)(2,1)S(1)} %copy-done.23), kind=kOutput, calls=%fused_computation.20 | convolution fusion | flops 5402787840 | bytes 27787264 | tf_op jit(solution)/shard_map/dot_general | solution.py:1151
  189.3 10.6 %fusion.42 = f32[1024,2048]{1,0:T(8,128)} fusion(bf16[1024,1280]{1,0:T(8,128)(2,1)} %get-tuple-element.123, bf16[2048,1280]{1,0:T(8,128)(2,1)S(1)} %bitcast.97), kind=kOutput, calls=%fused_computation.87 | convolution fusion | flops 5368709120 | bytes 16252928 | tf_op jit(solution)/shard_map/dot_general | solution.py:47
  199.9 13.8 %convolution_convert_fusion = bf16[2048,2560]{1,0:T(8,128)(2,1)} fusion(bf16[1024,2048]{1,0:T(8,128)(2,1)S(1)} %copy-done.32, bf16[1024,1280]{1,0:T(8,128)(2,1)S(1)} %copy-done.33, bf16[1024,1280]{1,0:T(8,128)(2,1)S(1)} %copy-done.34), kind=kOutput, calls=%fused_computation | convolution fusion | flops 10753146880 | bytes 19922944 | tf_op jit(solution)/shard_map/dot_general | solution.py:1159
  213.7 11.9 %add_convert_fusion.part_hbm = bf16[1024,2048]{1,0:T(8,128)(2,1)} fusion(f32[1024,2048]{1,0:T(8,128)} %fusion.42, bf16[1024,1280]{1,0:T(8,128)(2,1)} %get-tuple-element.124, bf16[2048,1280]{1,0:T(8,128)(2,1)} %param.21), kind=kOutput, calls=%fused_computation.3 | convolution fusion | flops 5372903424 | bytes 20447232 | tf_op jit(solution)/shard_map/dot_general | solution.py:47
  225.5 7.5 %convolution_convert_fusion.2 = bf16[1280,2048]{1,0:T(8,128)(2,1)} fusion(bf16[1024,1280]{1,0:T(8,128)(2,1)S(1)} %get-tuple-element.122.hidden_hbm, bf16[1,1024,2048]{2,1,0:T(8,128)(2,1)S(1)} %copy-done.24), kind=kOutput, calls=%fused_computation.7 | convolution fusion | flops 5371330560 | bytes 12058624 | tf_op jit(solution)/shard_map/dot_general | solution.py:1159
  233.1 0.7 reduce-scatter.3.cloned.1.call-update
  233.8 117.9 %leave_ffn.1 = (bf16[1024,2048]{1,0:T(8,128)(2,1)}, bf16[1024,2048]{1,0:T(8,128)(2,1)}, f32[256,2048]{1,0:T(8,128)}, f32[1,2048]{1,0:T(1,128)}) custom-call(bf16[1024,2048]{1,0:T(8,128)(2,1)} %add_convert_fusion.part_hbm, bf16[1024,2048]{1,0:T(8,128)(2,1)} %bitcast.83, bf16[1024,2048]{1,0:T(8,128)(2,1)} %get-tuple-element.48.attn_hbm, ...), custom_call_target="tpu_custom_call" | custom-call | flops 109999996928 | bytes 1000000 | tf_op jit(solution)/shard_map/leave_ffn/pallas_call | solution.py:978
  351.8 1.7 constant_dynamic-slice_fusion
  353.5 1.9 collective-permute-start.1
  355.4 4.9 collective-permute-start
  360.3 6.5 fusion.20.grad_ref
  366.8 8.2 %collective-permute-done.1 = bf16[256,2048]{1,0:T(8,128)(2,1)S(1)} collective-permute-done((bf16[256,2048]{1,0:T(8,128)(2,1)S(1)}, bf16[256,2048]{1,0:T(8,128)(2,1)S(1)}, u32[]{:S(2)}, u32[]{:S(2)}) %collective-permute-start.1) | collective-permute-done | bytes 1048608 | tf_op jit(solution)/shard_map/ppermute | solution.py:1136
  375.0 1.0 copy-done.12
  376.0 0.8 collective-permute-done
  376.8 2.2 add_convert_fusion.4
  379.0 3.0 collective-permute-start.3
  382.0 2.3 collective-permute-start.2
  384.4 36.5 %attend_back.1 = (bf16[1,1024,512]{2,1,0:T(8,128)(2,1)}, bf16[1,1024,512]{2,1,0:T(8,128)(2,1)}, bf16[1,1024,512]{2,1,0:T(8,128)(2,1)}, f32[1,8,5,512]{3,2,1,0:T(8,128)}) custom-call(s32[4]{0:T(128)} %get-tuple-element.119.first_ref, s32[4]{0:T(128)} %broadcast_add_fusion.last_ref, bf16[1,1024,512]{2,1,0:T(8,128)(2,1)} %fusion.17.q_ref, ...), custom_call_target="tpu_custom_call" | custom-call | flops 35000000512 | bytes 1000000 | tf_op jit(solution)/shard_map/attend_back/pallas_call | solution.py:295
  420.9 6.2 convolution_convert_fusion.4.refs_3_
  427.1 0.6 dynamic-slice.6
  427.8 6.7 %bitcast_convert_fusion = f32[1024,2048]{1,0:T(8,128)} fusion(bf16[1,1024,2048]{2,1,0:T(8,128)(2,1)} %param.13), kind=kLoop, calls=%fused_computation.83 | loop fusion | flops 2097152 | bytes 12582912 | tf_op jit(solution)/shard_map/convert_element_type | solution.py:1195
  434.5 0.2 fusion.25
  434.8 0.1 reshape.328
  434.9 4.2 add_convert_fusion.2
  439.1 3.2 collective-permute-start.5
  442.3 3.5 collective-permute-start.4
  445.8 2.4 fusion.36
  448.3 5.8 fusion.34
  454.0 7.7 %multiply_reduce_fusion = (f32[2048]{0:T(1024)S(1)}, bf16[1024,2048]{1,0:T(8,128)(2,1)}) fusion(f32[1024]{0:T(1024)S(1)} %copy-done.19, bf16[1,1024,2048]{2,1,0:T(8,128)(2,1)S(1)} %copy-done.3, bf16[2048,512]{1,0:T(8,128)(2,1)} %param.18, bf16[1,1024,512]{2,1,0:T(8,128)(2,1)S(1)} %copy-done.11, f32[1024,2048]{1,0:T(8,128)S(1)} %fusion.36, ...), kind=kOutput, calls=%fused_computation.1 | convolution fusion | flops 2162161664 | bytes 28323840 | tf_op jit(solution)/shard_map/dot_general | solution.py:47
  461.8 0.7 select_maximum_fusion.refs_1_
  462.4 10.7 %convolution_convert_fusion.1.refs_2_ = bf16[2048,1536]{1,0:T(8,128)(2,1)} fusion(bf16[1024,512]{1,0:T(8,128)(2,1)S(1)} %bitcast.84, bf16[1024,512]{1,0:T(8,128)(2,1)} %bitcast.103, bf16[1024,512]{1,0:T(8,128)(2,1)} %bitcast.102, f32[2048]{0:T(1024)S(1)} %copy-done.17, f32[1024]{0:T(1024)S(1)} %copy-done.19, bf16[1,1024,2048]{2,1,0:T(8,128)(2,1)S(1)} %copy-done.3), kind=kOutput, calls=%fused_computation.6 | convolution fusion | flops 6463422464 | bytes 13643776 | tf_op jit(solution)/shard_map/dot_general | solution.py:1159
  473.1 123.3 %tail_sums.1 = (f32[256,2048]{1,0:T(8,128)}, f32[8,2048]{1,0:T(8,128)}, f32[8,2048]{1,0:T(8,128)}, bf16[2048,512]{1,0:T(8,128)(2,1)}, bf16[2048,512]{1,0:T(8,128...) custom-call(bf16[1024,2048]{1,0:T(8,128)(2,1)} %get-tuple-element.126.refs_0_, ...), custom_call_target="tpu_custom_call" | custom-call | flops 109999996928 | bytes 1000000 | tf_op jit(solution)/shard_map/tail_sums/pallas_call | solution.py:1078
  596.5 4.3 convert_bitcast_fusion
  600.8 0.9 slice_reduce_fusion
  601.7 1.4 slice.20
  603.1 2.6 convert_element_type.270
  605.7 2.6 convert_element_type.271
  608.3 2.6 convert_element_type.272
  611.0 5.5 copy.45
  616.4 1.4 slice.19
  618.0 0.7 copy.46
  618.6 2.1 multiply_reduce_fusion.2
  620.8 0.1 copy-done.6
  620.9 3.3 fusion.21
  624.1 4.4 fusion.22
  628.6 8.0 %convert_element_type.274 = f32[1280,2048]{1,0:T(8,128)} convert(bf16[1280,2048]{1,0:T(8,128)(2,1)} %all-gather.5.cloned.1.call-done) | non-fusion elementwise | flops 2621440 | bytes 15728640 | tf_op jit(solution)/shard_map/convert_element_type | solution.py:1231
  636.6 13.3 %fusion.39 = (f32[2048,1280]{1,0:T(8,128)}, f32[2048,1280]{1,0:T(8,128)}) fusion(bf16[2048,2560]{1,0:T(8,128)(2,1)} %all-gather.3.cloned.1.call-done), kind=kLoop, calls=%fused_computation.84 | loop fusion | bytes 41943040 | tf_op jit(solution)/shard_map/split | solution.py:1241
  (101 shorter events, 0.8 us)
Async XLA Ops:
  7.2 19.6 %copy-start = (f32[32,8]{0,1:T(8,128)S(1)}, f32[32,8]{0,1:T(8,128)}, u32[]{:S(2)}) copy-start(f32[32,8]{0,1:T(8,128)} %param.25) | copy-start | bytes 3076
  7.2 6.6 copy-start.16
  7.2 344.5 %reduce-scatter.5.cloned.1.call-start = ((), (), s32[]{:S(2)}) async-start(), calls=%async_computation.4 | async-start | bytes 5898240 | tf_op jit(solution)/shard_map/reduce_scatter | solution.py:1229
  9.4 4.4 copy-start.2
  13.8 8.5 %copy-start.18 = (f32[1024]{0:T(1024)}, f32[1024]{0:T(1024)S(1)}, u32[]{:S(2)}) copy-start(f32[1024]{0:T(1024)S(1)} %add_rsqrt_fusion) | copy-start | bytes 12292
  13.8 5.1 copy-start.27
  18.9 3.4 copy-start.10
  22.3 3.4 copy-start.20
  26.8 0.9 copy-start.14
  27.7 26.3 %copy-start.25 = (bf16[512,2048]{1,0:T(8,128)(2,1)S(1)}, bf16[512,2048]{1,0:T(8,128)(2,1)}, u32[]{:S(2)}) copy-start(bf16[512,2048]{1,0:T(8,128)(2,1)} %param.19) | copy-start | bytes 6291460
  168.6 9.1 %copy-start.23 = (bf16[2048,1280]{1,0:T(8,128)(2,1)S(1)}, bf16[2048,1280]{1,0:T(8,128)(2,1)}, u32[]{:S(2)}) copy-start(bf16[2048,1280]{1,0:T(8,128)(2,1)} %param.21) | copy-start | bytes 15728644
  168.6 9.1 %copy-start.32 = (bf16[1024,2048]{1,0:T(8,128)(2,1)S(1)}, bf16[1024,2048]{1,0:T(8,128)(2,1)}, u32[]{:S(2)}) copy-start(bf16[1024,2048]{1,0:T(8,128)(2,1)} %get-tuple-element.50) | copy-start | bytes 12582916
  168.6 20.7 %slice-start = ((s8[5242880]{0:T(1024)(128)(4,1)}), s8[4194304]{0:T(1024)(128)(4,1)S(1)}, s32[]{:S(2)}) async-start(s8[5242880]{0:T(1024)(128)(4,1)} %bitcast.96), calls=%async_computation.6 | async-start | bytes 8388608
  177.7 11.6 %slice-start.1 = ((s8[5242880]{0:T(1024)(128)(4,1)}), s8[1048576]{0:T(1024)(128)(4,1)S(1)}, s32[]{:S(2)}) async-start(s8[5242880]{0:T(1024)(128)(4,1)} %bitcast.96), calls=%async_computation.7 | async-start | bytes 2097152
  189.3 36.2 %copy-start.31 = (bf16[1024,1280]{1,0:T(8,128)(2,1)}, bf16[1024,1280]{1,0:T(8,128)(2,1)S(1)}, u32[]{:S(2)}) copy-start(bf16[1024,1280]{1,0:T(8,128)(2,1)S(1)} %get-tuple-element.122.hidden_hbm) | copy-start | bytes 7864324
  189.3 10.6 %copy-start.33 = (bf16[1024,1280]{1,0:T(8,128)(2,1)S(1)}, bf16[1024,1280]{1,0:T(8,128)(2,1)}, u32[]{:S(2)}) copy-start(bf16[1024,1280]{1,0:T(8,128)(2,1)} %get-tuple-element.124) | copy-start | bytes 7864324
  189.3 10.6 %copy-start.34 = (bf16[1024,1280]{1,0:T(8,128)(2,1)S(1)}, bf16[1024,1280]{1,0:T(8,128)(2,1)}, u32[]{:S(2)}) copy-start(bf16[1024,1280]{1,0:T(8,128)(2,1)} %get-tuple-element.123) | copy-start | bytes 7864324
  213.7 11.9 %copy-start.24 = (bf16[1,1024,2048]{2,1,0:T(8,128)(2,1)S(1)}, bf16[1,1024,2048]{2,1,0:T(8,128)(2,1)}, u32[]{:S(2)}) copy-start(bf16[1,1024,2048]{2,1,0:T(8,128)(2,1)} %param.15) | copy-start | bytes 12582916
  233.0 187.9 %reduce-scatter.3.cloned.1.call-start = ((), (), s32[]{:S(2)}) async-start(), calls=%async_computation.2 | async-start | bytes 11796480 | tf_op jit(solution)/shard_map/reduce_scatter | solution.py:1228
  233.8 394.8 %all-gather.5.cloned.1.call-start = ((), (), s32[]{:S(2)}) async-start(), calls=%async_computation.5 | async-start | bytes 5898240 | tf_op jit(solution)/shard_map/all_gather | solution.py:1231
  351.8 284.8 %all-gather.3.cloned.1.call-start = ((), (), s32[]{:S(2)}) async-start(), calls=%async_computation.3 | async-start | bytes 11796480 | tf_op jit(solution)/shard_map/all_gather | solution.py:1240
  353.5 21.5 %collective-permute-start.1 = (bf16[256,2048]{1,0:T(8,128)(2,1)S(1)}, bf16[256,2048]{1,0:T(8,128)(2,1)S(1)}, u32[]{:S(2)}, u32[]{:S(2)}) collective-permute-start(bf16[256,2048]{1,0:T(8,128)(2,1)S(1)} %get-tuple-element.54), channel_id=1, source_target_pairs={{1,0},{2,1},{3,2},{5,4},{6,5},{7,6},{9,8},{10,9},{11,10},{13,12},{... | collective-permute-start | bytes 3145736 | tf_op jit(solution)/shard_map/ppermute | solution.py:1136
  355.4 21.3 %collective-permute-start = (bf16[256,2048]{1,0:T(8,128)(2,1)S(1)}, bf16[256,2048]{1,0:T(8,128)(2,1)}, u32[]{:S(2)}, u32[]{:S(2)}) collective-permute-start(bf16[256,2048]{1,0:T(8,128)(2,1)S(1)} %get-tuple-element.53), channel_id=1, source_target_pairs={{0,1},{1,2},{2,3},{4,5},{5,6},{6,7},{8,9},{9,10},{10,11},{12,13},{... | collective-permute-start | bytes 3145736 | tf_op jit(solution)/shard_map/ppermute | solution.py:1136
  360.3 16.5 %copy-start.4 = (bf16[1024,2048]{1,0:T(8,128)(2,1)S(1)}, bf16[1024,2048]{1,0:T(8,128)(2,1)}, u32[]{:S(2)}) copy-start(bf16[1024,2048]{1,0:T(8,128)(2,1)} %get-tuple-element.52) | copy-start | bytes 12582916
  375.0 1.0 copy-start.12
  379.0 55.9 %collective-permute-start.3 = (bf16[256,2048]{1,0:T(8,128)(2,1)S(1)}, bf16[256,2048]{1,0:T(8,128)(2,1)S(1)}, u32[]{:S(2)}, u32[]{:S(2)}) collective-permute-start(bf16[256,2048]{1,0:T(8,128)(2,1)S(1)} %get-tuple-element.57), channel_id=1, source_target_pairs={{1,0},{2,1},{3,2},{5,4},{6,5},{7,6},{9,8},{10,9},{11,10},{13,12},{... | collective-permute-start | bytes 3145736 | tf_op jit(solution)/shard_map/ppermute | solution.py:1136
  382.0 52.9 %collective-permute-start.2 = (bf16[256,2048]{1,0:T(8,128)(2,1)S(1)}, bf16[256,2048]{1,0:T(8,128)(2,1)}, u32[]{:S(2)}, u32[]{:S(2)}) collective-permute-start(bf16[256,2048]{1,0:T(8,128)(2,1)S(1)} %get-tuple-element.56), channel_id=1, source_target_pairs={{0,1},{1,2},{2,3},{4,5},{5,6},{6,7},{8,9},{9,10},{10,11},{12,13},{... | collective-permute-start | bytes 3145736 | tf_op jit(solution)/shard_map/ppermute | solution.py:1136
  420.9 6.2 copy-start.19
  427.8 6.7 %copy-start.13 = (f32[1,8,5,512]{3,2,1,0:T(8,128)S(1)}, f32[1,8,5,512]{3,2,1,0:T(8,128)}, u32[]{:S(2)}) copy-start(f32[1,8,5,512]{3,2,1,0:T(8,128)} %get-tuple-element.70) | copy-start | bytes 245764
  427.8 6.8 %copy-start.15 = (s32[2560]{0:T(1024)S(1)}, s32[2560]{0:T(1024)}, u32[]{:S(2)}) copy-start(s32[2560]{0:T(1024)} %copy-done.14) | copy-start | bytes 30724
  434.9 10.9 %copy-start.26 = (bf16[2048,512]{1,0:T(8,128)(2,1)S(1)}, bf16[2048,512]{1,0:T(8,128)(2,1)}, u32[]{:S(2)}) copy-start(bf16[2048,512]{1,0:T(8,128)(2,1)} %param.16) | copy-start | bytes 6291460
  434.9 10.9 %copy-start.29 = (bf16[1,1024,512]{2,1,0:T(8,128)(2,1)S(1)}, bf16[1,1024,512]{2,1,0:T(8,128)(2,1)}, u32[]{:S(2)}) copy-start(bf16[1,1024,512]{2,1,0:T(8,128)(2,1)} %get-tuple-element.66) | copy-start | bytes 3145732
  439.1 9.1 %copy-start.28 = (bf16[2048,512]{1,0:T(8,128)(2,1)S(1)}, bf16[2048,512]{1,0:T(8,128)(2,1)}, u32[]{:S(2)}) copy-start(bf16[2048,512]{1,0:T(8,128)(2,1)} %param.17) | copy-start | bytes 6291460
  439.1 9.1 %copy-start.30 = (bf16[1,1024,512]{2,1,0:T(8,128)(2,1)S(1)}, bf16[1,1024,512]{2,1,0:T(8,128)(2,1)}, u32[]{:S(2)}) copy-start(bf16[1,1024,512]{2,1,0:T(8,128)(2,1)} %get-tuple-element.67) | copy-start | bytes 3145732
  439.1 185.0 %collective-permute-start.5 = (bf16[256,2048]{1,0:T(8,128)(2,1)}, bf16[256,2048]{1,0:T(8,128)(2,1)}, u32[]{:S(2)}, u32[]{:S(2)}) collective-permute-start(bf16[256,2048]{1,0:T(8,128)(2,1)} %get-tuple-element.64), channel_id=1, source_target_pairs={{1,0},{2,1},{3,2},{5,4},{6,5},{7,6},{9,8},{10,9},{11,10},{13,12},{... | collective-permute-start | bytes 3145736 | tf_op jit(solution)/shard_map/ppermute | solution.py:1136
  442.3 181.8 %collective-permute-start.4 = (bf16[256,2048]{1,0:T(8,128)(2,1)}, bf16[256,2048]{1,0:T(8,128)(2,1)}, u32[]{:S(2)}, u32[]{:S(2)}) collective-permute-start(bf16[256,2048]{1,0:T(8,128)(2,1)} %get-tuple-element.63), channel_id=1, source_target_pairs={{0,1},{1,2},{2,3},{4,5},{5,6},{6,7},{8,9},{9,10},{10,11},{12,13},{... | collective-permute-start | bytes 3145736 | tf_op jit(solution)/shard_map/ppermute | solution.py:1136
  448.2 5.8 copy-start.3
  448.2 5.8 copy-start.11
  454.0 7.7 %copy-start.21 = (f32[1,2048]{1,0:T(1,128)S(1)}, f32[1,2048]{1,0:T(1,128)}, u32[]{:S(2)}) copy-start(f32[1,2048]{1,0:T(1,128)} %get-tuple-element.69) | copy-start | bytes 24580
  454.0 8.4 %copy-start.17 = (f32[2048]{0:T(1024)S(1)}, f32[2048]{0:T(1024)}, u32[]{:S(2)}) copy-start(f32[2048]{0:T(1024)} %param.23) | copy-start | bytes 24580
  596.4 6.7 %copy-start.9 = (bf16[2048,512]{1,0:T(8,128)(2,1)S(1)}, bf16[2048,512]{1,0:T(8,128)(2,1)}, u32[]{:S(2)}) copy-start(bf16[2048,512]{1,0:T(8,128)(2,1)} %get-tuple-element.72) | copy-start | bytes 6291460
  600.8 4.9 copy-start.8
  605.7 2.6 copy-start.7
  611.0 7.7 %copy-start.5 = (f32[256,2048]{1,0:T(8,128)S(1)}, f32[256,2048]{1,0:T(8,128)}, u32[]{:S(2)}) copy-start(f32[256,2048]{1,0:T(8,128)} %get-tuple-element.71) | copy-start | bytes 6291460
  616.4 4.3 copy-start.22
  618.6 2.2 copy-start.6
  636.6 13.3 %copy-start.1 = (f32[32,8]{0,1:T(8,128)S(1)}, f32[32,8]{0,1:T(8,128)}, u32[]{:S(2)}) copy-start(f32[32,8]{0,1:T(8,128)} %param.25) | copy-start | bytes 3076
Sparse Core Ops, SparseCore 0:
  233.1 65.7 reduce-scatter.4
  303.4 81.5 reduce-scatter.2
  387.1 42.4 all-gather.4
  431.5 68.0 all-gather.2

commit v5 on v4

--- a/solution.py
+++ b/solution.py
@@ -12,10 +12,12 @@
 tile = 256
 kinds = 5
 group_pairs = 1
-line_chunks = 8
+line_chunks = 16
 tail_columns = 256
-tail_subs = 4
-tail_lag = 2
+tail_subs = 8
+tail_lag = 3
+line_lag = 3
+sum_lag = 2
 lanes = 128
 bf16 = jnp.bfloat16
 f32 = jnp.float32
@@ -357,21 +359,22 @@
 
 
 class LineScatter:
-    def __init__(self, axis, count, subs, part_ref, share_ref, land_ref, send_sem, recv_sem):
-        self.axis, self.count, self.subs = axis, count, subs
-        self.part_ref, self.share_ref, self.land_ref = part_ref, share_ref, land_ref
+    def __init__(self, axis, count, subs, first, part_ref, land_ref, send_sem, recv_sem, arrive):
+        self.axis, self.count, self.subs, self.first = axis, count, subs, first
+        self.part_ref, self.land_ref, self.arrive = part_ref, land_ref, arrive
         self.send_sem, self.recv_sem = send_sem, recv_sem
         self.me = lax.axis_index(axis)
         self.share = part_ref.shape[0] // count
         self.size = self.share // subs
         self.length = (count - 1) * subs
-        self.steps = self.length + count - 1
+        self.steps = first + self.length + (count - 1) * line_lag
 
     @staticmethod
     def scratch(count, subs, shape):
         items = (2, (count - 1) * subs)
         return [
-            pltpu.VMEM((2,) + shape, bf16),
+            pltpu.VMEM(shape, bf16),
+            pltpu.VMEM((shape[0] + shape[0] // count, shape[1]), bf16),
             pltpu.SemaphoreType.DMA(items),
             pltpu.SemaphoreType.DMA(items),
         ]
@@ -382,16 +385,23 @@
     def owner(self, flow, item):
         return self.count - 1 - item // self.subs
 
-    def rows(self, flow, item):
+    def start(self, flow, item):
         along = self.owner(flow, item)
         owner = along if flow == 0 else self.count - 1 - along
-        start = owner * self.share + item % self.subs * self.size
+        return owner * self.share + item % self.subs * self.size
+
+    def rows(self, start):
         return pl.ds(pl.multiple_of(start, self.size), self.size)
 
-    def copy(self, flow, item, source):
-        here = self.rows(flow, item)
+    def landing(self, flow, start):
+        return self.rows(start + self.share if flow == 0 else start)
+
+    def copy(self, flow, item, landed):
+        start = self.start(flow, item)
+        landing = self.landing(flow, start)
+        source = self.land_ref.at[landing] if landed else self.part_ref.at[self.rows(start)]
         return pltpu.make_async_remote_copy(
-            src_ref=source.at[here], dst_ref=self.land_ref.at[flow, here],
+            src_ref=source, dst_ref=self.land_ref.at[landing],
             send_sem=self.send_sem.at[flow, item], recv_sem=self.recv_sem.at[flow, item],
             device_id={self.axis: self.me + 1 if flow == 0 else self.me - 1},
             device_id_type=mesh_ids,
@@ -400,49 +410,39 @@
     def step(self, time):
         for flow in range(2):
             place = self.place(flow)
-            item = time - place
+            item = time - self.first - place * line_lag
             safe = jnp.clip(item, 0, self.length - 1)
             along = self.owner(flow, safe)
             valid = (item >= 0) & (item < self.length) & (along >= place)
-            here = self.rows(flow, safe)
+            start = self.start(flow, safe)
+            here = self.rows(start)
+            landing = self.landing(flow, start)
 
             @pl.when(valid & (place == 0))
             def _():
-                self.copy(flow, safe, self.part_ref).start()
+                self.copy(flow, safe, False).start()
 
             @pl.when(valid & (place > 0))
             def _():
-                self.copy(flow, safe, self.part_ref).wait_recv()
+                self.copy(flow, safe, False).wait_recv()
 
             @pl.when(valid & (place > 0) & (along > place))
             def _():
-                self.land_ref[flow, here, :] = add_low(
-                    self.land_ref[flow, here, :], self.part_ref[here, :]
+                self.land_ref[landing, :] = add_low(
+                    self.land_ref[landing, :], self.part_ref[here, :]
                 )
-                self.copy(flow, safe, self.land_ref.at[flow]).start()
+                self.copy(flow, safe, True).start()
 
     def finish(self):
         def total(sub, carry):
-            size = self.size
-            start = pl.multiple_of(self.me * self.share + sub * size, size)
-            here = pl.ds(start, size)
-            mine = pl.ds(pl.multiple_of(sub * size, size), size)
-            value = self.part_ref[here, :].astype(f32)
-
-            @pl.when(self.me == 0)
-            def _():
-                self.share_ref[mine, :] = value + self.land_ref[1, here, :].astype(f32)
-
-            @pl.when(self.me == self.count - 1)
-            def _():
-                self.share_ref[mine, :] = value + self.land_ref[0, here, :].astype(f32)
-
-            @pl.when((self.me > 0) & (self.me < self.count - 1))
-            def _():
-                self.share_ref[mine, :] = (
-                    value + self.land_ref[0, here, :].astype(f32)
-                    + self.land_ref[1, here, :].astype(f32)
-                )
+            start = self.me * self.share + sub * self.size
+            value = self.part_ref[self.rows(start), :].astype(f32)
+            last = self.count - 1
+            from_left = self.land_ref[self.landing(0, start), :].astype(f32)
+            from_right = self.land_ref[self.landing(1, start), :].astype(f32)
+            value = value + jnp.where(self.me > 0, from_left, 0.0)
+            value = value + jnp.where(self.me < last, from_right, 0.0)
+            self.arrive(sub * self.size, self.rows(start), value)
             return carry
 
         lax.fori_loop(0, self.subs, total, 0)
@@ -451,7 +451,7 @@
             for flow in range(2):
                 @pl.when(self.owner(flow, item) > self.place(flow))
                 def _():
-                    self.copy(flow, item, self.part_ref).wait_send()
+                    self.copy(flow, item, False).wait_send()
             return carry
 
         lax.fori_loop(0, self.length, drain, 0)
@@ -588,16 +588,16 @@
 
 
 class SmallSum:
-    def __init__(self, cube_axis, bits, line_axis, count, gap, own_ref, cube_ref, all_ref, work_ref, land_ref,
+    def __init__(self, cube_axis, bits, line_axis, count, first, gap, own_ref, cube_ref, all_ref, work_ref, land_ref,
                  line_ref, send_sem, recv_sem, line_send_sem, line_recv_sem):
         self.cube_axis, self.bits, self.line_axis, self.count = cube_axis, bits, line_axis, count
-        self.gap = gap
+        self.first, self.gap = first, gap
         self.own_ref, self.cube_ref, self.all_ref = own_ref, cube_ref, all_ref
         self.work_ref, self.land_ref, self.line_ref = work_ref, land_ref, line_ref
         self.sems = (send_sem, recv_sem, line_send_sem, line_recv_sem)
         self.me = lax.axis_index(cube_axis)
         self.line_me = lax.axis_index(line_axis)
-        self.steps = (bits + 1) * gap + 1
+        self.steps = first + (bits + 1) * gap + 1
 
     @staticmethod
     def scratch(bits, count, shape):
@@ -628,7 +628,7 @@
 
     def step(self, time):
         for turn in range(self.bits + 2):
-            pl.when(time == turn * self.gap)(functools.partial(self.turn, turn))
+            pl.when(time == self.first + turn * self.gap)(functools.partial(self.turn, turn))
 
     def turn(self, turn):
         bits = self.bits
@@ -672,7 +672,7 @@
         self.sems = (send_sem, recv_sem, back_send_sem, back_recv_sem)
         self.me = lax.axis_index(axis)
         self.size = part_ref.shape[0] // (2 * chunks)
-        self.steps = chunks + 2 * (count - 1)
+        self.steps = chunks + 2 * (count - 1) * sum_lag
 
     @staticmethod
     def scratch(chunks, shape):
@@ -706,7 +706,7 @@
         last = self.count - 1
         for flow in range(2):
             place = self.place(flow)
-            chunk = time - place
+            chunk = time - place * sum_lag
             valid = (chunk >= 0) & (chunk < self.chunks)
             here = pl.ds(self.start(flow, chunk), self.size)
 
@@ -729,7 +729,7 @@
                 self.back_copy(flow, chunk).start()
         for flow in range(2):
             place = self.place(flow)
-            chunk = time - 2 * last + place
+            chunk = time - (2 * last - place) * sum_lag
             valid = (chunk >= 0) & (chunk < self.chunks)
 
             @pl.when(valid & (place < last))
@@ -806,6 +806,44 @@
             self.store(block, block % 2).wait()
 
 
+class FfnGrads:
+    def __init__(self, normed_ref, gate_ref, up_ref, out_ref, stage_ref, sem, first):
+        self.normed_ref, self.gate_ref, self.up_ref = normed_ref, gate_ref, up_ref
+        self.out_ref, self.stage_ref, self.sem, self.first = out_ref, stage_ref, sem, first
+        self.rows = stage_ref.shape[1]
+        self.blocks = out_ref.shape[0] // self.rows
+        self.steps = first + self.blocks
+
+    def store(self, block, slot):
+        there = pl.ds(pl.multiple_of(block * self.rows, self.rows), self.rows)
+        return pltpu.make_async_copy(
+            self.stage_ref.at[slot], self.out_ref.at[there], self.sem.at[slot]
+        )
+
+    def step(self, time):
+        block = time - self.first
+        slot = block % 2
+
+        @pl.when((block >= 2) & (block < self.blocks))
+        def _():
+            self.store(block - 2, slot).wait()
+
+        @pl.when((block >= 0) & (block < self.blocks))
+        def _():
+            width = self.gate_ref.shape[1]
+            there = pl.ds(pl.multiple_of(block * self.rows, self.rows), self.rows)
+            normed_t = jnp.transpose(self.normed_ref[:, there].astype(f32)).astype(bf16)
+            for index, right_ref in enumerate((self.gate_ref, self.up_ref)):
+                self.stage_ref[slot, :, index * width : (index + 1) * width] = dot_nn(
+                    normed_t, right_ref[...]
+                ).astype(bf16)
+            self.store(block, slot).start()
+
+    def finish(self):
+        for block in range(max(self.blocks - 2, 0), self.blocks):
+            self.store(block, block % 2).wait()
+
+
 def run_parts(parts):
     def step(time, carry):
         for part in parts:
@@ -843,13 +881,18 @@
 
 
 def enter_kernel(
-    axis, count, chunks, part_hbm, x_hbm, grad_hbm, w_hbm, gain_ref, total_hbm, normed_hbm, hidden_hbm,
-    x_ref, normed_ref, grad_ref, w_ref, stage_ref, load_sem, stage_sem, store_sem, *line_scratch,
+    axis, count, chunks, part_hbm, x_hbm, grad_hbm, w_hbm, first_hbm, mixed_hbm, gain_ref,
+    total_hbm, normed_hbm, hidden_hbm, first_t_hbm, mixed_t_hbm,
+    x_ref, normed_ref, grad_ref, w_ref, first_ref, mixed_ref, stage_ref, turn_ref, load_sem, stage_sem,
+    turn_sem, store_sem, *line_scratch,
 ):
     loads = [
         pltpu.make_async_copy(source, target, load_sem.at[index])
         for index, (source, target) in enumerate(
-            ((part_hbm, line_scratch[0]), (x_hbm, x_ref), (grad_hbm, grad_ref), (w_hbm, w_ref))
+            (
+                (part_hbm, line_scratch[0]), (x_hbm, x_ref), (grad_hbm, grad_ref), (w_hbm, w_ref),
+                (first_hbm, first_ref), (mixed_hbm, mixed_ref),
+            )
         )
     ]
     for load in loads:
@@ -870,19 +913,21 @@
     )
 
     def before():
-        loads[1].wait()
-        loads[2].wait()
-        loads[3].wait()
+        for load in loads[1:]:
+            load.wait()
 
     product = BlockedProduct(
         grad_ref, w_ref, True, hidden_hbm, stage_ref, stage_sem, 1, before
     )
+    transposes = Transposes(
+        [(first_ref, first_t_hbm), (mixed_ref, mixed_t_hbm)], turn_ref, turn_sem, 2, 2, lambda: None
+    )
     loads[0].wait()
-    run_parts([line, product])
+    run_parts([line, product, transposes])
     stores.finish()
 
 
-def enter_ffn(part, x, grad, w_down, gain, axis, chunks, cid):
+def enter_ffn(part, x, grad, w_down, first_normed, mixed, gain, axis, chunks, cid):
     count = lax.axis_size(axis)
     tokens, width = part.shape
     hbm = pl.BlockSpec(memory_space=pl.ANY)
@@ -893,13 +938,17 @@
             jax.ShapeDtypeStruct((tokens, width), bf16),
             jax.ShapeDtypeStruct((tokens, width), bf16),
             jax.ShapeDtypeStruct((tokens, w_down.shape[0]), f32),
+            jax.ShapeDtypeStruct((width, tokens), bf16),
+            jax.ShapeDtypeStruct((mixed.shape[1], tokens), bf16),
         ),
-        in_specs=[hbm] * 4 + [pl.BlockSpec(memory_space=pltpu.VMEM)],
-        out_specs=[hbm] * 3,
+        in_specs=[hbm] * 6 + [pl.BlockSpec(memory_space=pltpu.VMEM)],
+        out_specs=[hbm] * 5,
         scratch_shapes=[
-            whole, whole, whole, pltpu.VMEM(w_down.shape, bf16),
+            whole, whole, whole, pltpu.VMEM(w_down.shape, bf16), whole, pltpu.VMEM(mixed.shape, bf16),
             pltpu.VMEM((2, tokens, lanes), f32),
-            pltpu.SemaphoreType.DMA((4,)),
+            pltpu.VMEM((2, lanes, tokens), bf16),
+            pltpu.SemaphoreType.DMA((6,)),
+            pltpu.SemaphoreType.DMA((2,)),
             pltpu.SemaphoreType.DMA((2,)),
             pltpu.SemaphoreType.DMA((2, 2, chunks)),
             *LineSum.scratch(chunks, part.shape),
@@ -909,14 +958,14 @@
         ),
         cost_estimate=cost(110),
         name="enter_ffn",
-    )(part, x, grad, w_down, gain[None])
+    )(part, x, grad, w_down, first_normed, mixed, gain[None])
 
 
 def leave_kernel(
-    axis, count, chunks, part_hbm, x_hbm, attn_hbm, grad_hbm, hidden_hbm, w_hbm, gain_ref,
-    branch_hbm, ffn_hbm, share_ref, sum_ref,
-    x_ref, attn_ref, grad_ref, hidden_ref, w_ref, branch_ref, stage_ref, load_sem, stage_sem, store_sem,
-    *line_scratch,
+    axis, count, chunks, part_hbm, x_hbm, attn_hbm, grad_hbm, hidden_hbm, w_hbm, normed_hbm, gate_hbm,
+    up_hbm, gain_ref, branch_hbm, ffn_hbm, grads_hbm, share_ref, sum_ref,
+    x_ref, attn_ref, grad_ref, hidden_ref, w_ref, normed_ref, gate_ref, up_ref, branch_ref, stage_ref,
+    grads_stage_ref, load_sem, stage_sem, grads_sem, store_sem, *line_scratch,
 ):
     loads = [
         pltpu.make_async_copy(source, target, load_sem.at[index])
@@ -924,6 +973,7 @@
             (
                 (part_hbm, line_scratch[0]), (hidden_hbm, hidden_ref), (w_hbm, w_ref),
                 (x_hbm, x_ref), (attn_hbm, attn_ref), (grad_hbm, grad_ref),
+                (normed_hbm, normed_ref), (gate_hbm, gate_ref), (up_hbm, up_ref),
             )
         )
     ]
@@ -964,12 +1014,17 @@
     product = BlockedProduct(
         hidden_ref, w_ref, False, ffn_hbm, stage_ref, stage_sem, 0, before
     )
+    grads = FfnGrads(
+        normed_ref, gate_ref, up_ref, grads_hbm, grads_stage_ref, grads_sem, product.steps
+    )
     loads[0].wait()
-    run_parts([line, product])
+    run_parts([line, product, grads])
     stores.finish()
 
 
-def leave_ffn(part, x, attn_total, grad, hidden, w_down, gain, axis, chunks, cid):
+def leave_ffn(
+    part, x, attn_total, grad, hidden, w_down, normed, grad_gate, grad_up, gain, axis, chunks, cid
+):
     count = lax.axis_size(axis)
     tokens, width = part.shape
     hbm = pl.BlockSpec(memory_space=pl.ANY)
@@ -980,16 +1035,19 @@
         out_shape=(
             jax.ShapeDtypeStruct((tokens, width), bf16),
             jax.ShapeDtypeStruct((tokens, width), bf16),
+            jax.ShapeDtypeStruct((width, 2 * hidden.shape[1]), bf16),
             jax.ShapeDtypeStruct((tokens // count, width), f32),
             jax.ShapeDtypeStruct((1, width), f32),
         ),
-        in_specs=[hbm] * 6 + [vmem],
-        out_specs=[hbm, hbm, vmem, vmem],
+        in_specs=[hbm] * 9 + [vmem],
+        out_specs=[hbm, hbm, hbm, vmem, vmem],
         scratch_shapes=[
             whole, whole, whole, pltpu.VMEM(hidden.shape, bf16), pltpu.VMEM(w_down.shape, bf16),
-            whole,
+            whole, pltpu.VMEM(hidden.shape, bf16), pltpu.VMEM(hidden.shape, bf16), whole,
             pltpu.VMEM((2, tokens, tile), bf16),
-            pltpu.SemaphoreType.DMA((6,)),
+            pltpu.VMEM((2, lanes, 2 * hidden.shape[1]), bf16),
+            pltpu.SemaphoreType.DMA((9,)),
+            pltpu.SemaphoreType.DMA((2,)),
             pltpu.SemaphoreType.DMA((2,)),
             pltpu.SemaphoreType.DMA((2, chunks)),
             *LineSum.scratch(chunks, part.shape),
@@ -999,152 +1057,398 @@
         ),
         cost_estimate=cost(110),
         name="leave_ffn",
-    )(part, x, attn_total, grad, hidden, w_down, gain[None])
-
-
-def tail_kernel(line_axis, count, subs, cube_axis, bits, lag, widths, out_width, *refs):
-    part_ref, small_ref, *grad_refs = refs[: 2 + len(widths)]
-    refs = refs[2 + len(widths) :]
-    share_ref, small_cube_ref, small_all_ref = refs[:3]
-    out_count = sum(widths) // out_width
-    sum_refs = refs[3 : 3 + out_count]
-    scratch = list(refs[3 + out_count :])
-    data_ref, total_ref, load_sem, store_sem = scratch[:4]
-    line_scratch, scratch = scratch[4:7], scratch[7:]
+    )(part, x, attn_total, grad, hidden, w_down, normed, grad_gate, grad_up, gain[None])
+
+
+class RowProducts:
+    def __init__(self, count, grads_ref, weights_ref, x_hbm, x_ref, x_sem, part_ref, sum_ref):
+        self.grads_ref, self.weights_ref = grads_ref, weights_ref
+        self.x_hbm, self.x_ref, self.x_sem = x_hbm, x_ref, x_sem
+        self.part_ref, self.sum_ref = part_ref, sum_ref
+        self.share = part_ref.shape[0] // count
+        self.order = []
+        for index in range(count):
+            self.order.append(count - 1 - index // 2 if index % 2 == 0 else index // 2)
+        self.steps = count
+
+    def rows(self, index):
+        owner = self.order[index]
+        return slice(owner * self.share, (owner + 1) * self.share)
+
+    def load(self, index):
+        slot = index % 2
+        return pltpu.make_async_copy(
+            self.x_hbm.at[self.rows(index)], self.x_ref.at[slot], self.x_sem.at[slot]
+        )
+
+    def block(self, index):
+        rows, slot = self.rows(index), index % 2
+        self.load(index).wait()
+        x = self.x_ref[slot].astype(f32)
+        scale = lax.rsqrt(jnp.mean(x * x, axis=-1, keepdims=True) + 1e-06)
+
+        def columns(place, carry):
+            there = pl.ds(pl.multiple_of(place * tile, tile), tile)
+            value = dot_nt(self.grads_ref[0, rows, :], self.weights_ref[0, there, :])
+            value = value + dot_nt(self.grads_ref[1, rows, :], self.weights_ref[1, there, :])
+            value = value + dot_nt(self.grads_ref[2, rows, :], self.weights_ref[2, there, :])
+            self.part_ref[rows, there] = value.astype(bf16)
+            hat = self.x_ref[slot, :, there].astype(f32) * scale
+            self.sum_ref[:, there] = self.sum_ref[:, there] + jnp.sum(
+                value * hat, axis=0, keepdims=True
+            )
+            return carry
+
+        lax.fori_loop(0, self.part_ref.shape[1] // tile, columns, 0)
+        if index + 2 < len(self.order):
+            self.load(index + 2).start()
+
+    def step(self, time):
+        for index in range(len(self.order)):
+            pl.when(time == index)(functools.partial(self.block, index))
+
+    def finish(self):
+        pass
+
+
+def tail_kernel(
+    line_axis, count, subs, cube_axis, bits, lag, dq_hbm, dk_hbm, dv_hbm, wq_hbm, wk_hbm, wv_hbm,
+    x_hbm, normed_hbm, mixed_hbm, branch_hbm, ffn_hbm, middle_ref, gain_ref, small_ref,
+    input_out, ffn_out, small_cube_ref, small_all_ref, q_out, k_out, v_out, o_out, *scratch,
+):
+    (grads_ref, weights_ref, x_ref, mine_ref, normed_ref, mixed_ref, branch_ref, own_ref, data_ref,
+     total_ref, load_sem, x_sem, branch_sem, store_sem, out_sem) = scratch[:15]
+    line_scratch, ffn_scratch, scratch = scratch[15:19], scratch[19:23], scratch[23:]
     cube_scratch, small_scratch = scratch[: bits + 4], scratch[bits + 4 :]
-    chunks, _, columns = data_ref.shape
-
-    def load(chunk, source):
-        return pltpu.make_async_copy(source, data_ref.at[chunk], load_sem.at[chunk])
-
-    per_out = out_width // columns
+    chunks, depth, columns = data_ref.shape
+    tokens, width = dq_hbm.shape
+    per_weight = width // columns
+    per_chunk = depth // width
+    pieces = depth // columns
+    part_ref, ffn_ref = line_scratch[0], ffn_scratch[0]
+    me = lax.axis_index(line_axis)
+    share = tokens // count
+    my_rows = pl.ds(pl.multiple_of(me * share, share), share)
+    pairs = [(ffn_hbm, ffn_ref)]
+    pairs += [(hbm, grads_ref.at[index]) for index, hbm in enumerate((dq_hbm, dk_hbm, dv_hbm))]
+    pairs += [(hbm, weights_ref.at[index]) for index, hbm in enumerate((wq_hbm, wk_hbm, wv_hbm))]
+    pairs += [(mixed_hbm, mixed_ref), (normed_hbm, normed_ref), (x_hbm.at[my_rows], mine_ref)]
+    loads = [
+        pltpu.make_async_copy(source, target, load_sem.at[index])
+        for index, (source, target) in enumerate(pairs)
+    ]
+
+    def branch_load(piece, slot):
+        there = pl.ds(pl.multiple_of(piece * columns, columns), columns)
+        return pltpu.make_async_copy(
+            branch_hbm.at[:, there], branch_ref.at[slot], branch_sem.at[slot]
+        )
+
+    products = RowProducts(
+        count, grads_ref, weights_ref, x_hbm, x_ref, x_sem, part_ref, own_ref.at[0:1]
+    )
+    for load in loads[:7]:
+        load.start()
+    for index in range(min(2, count)):
+        products.load(index).start()
+    for load in loads[7:]:
+        load.start()
+    branch_load(0, 0).start()
+    greet(line_axis, count, cube_axis, bits)
+    own_ref[...] = small_ref[...]
 
     def store(chunk, index=0):
-        there = pl.ds(pl.multiple_of(chunk % per_out * columns, columns), columns)
+        there = pl.ds(pl.multiple_of(chunk % per_weight * columns, columns), columns)
         return pltpu.make_async_copy(
-            total_ref.at[chunk], sum_refs[index].at[:, there], store_sem.at[chunk]
+            total_ref.at[chunk], (q_out, k_out, v_out)[index].at[:, there], store_sem.at[chunk]
         )
 
-    def store_any(chunk):
-        for index in range(out_count):
-            @pl.when(chunk // per_out == index)
+    def store_out(chunk, piece):
+        first = pl.multiple_of((chunk * per_chunk + piece) * columns, columns)
+        return pltpu.make_async_copy(
+            total_ref.at[3 * per_weight + chunk, pl.ds(piece * width, width)],
+            o_out.at[:, pl.ds(first, columns)], store_sem.at[3 * per_weight + chunk],
+        )
+
+    def done(chunk):
+        for index in range(3):
+            @pl.when(chunk // per_weight == index)
             def _():
                 store(chunk, index).start()
 
-    chunk = 0
-    for grad_ref, width in zip(grad_refs, widths):
-        for start in range(0, width, columns):
-            load(chunk, grad_ref.at[:, start : start + columns]).start()
-            chunk += 1
-    greet(line_axis, count, cube_axis, bits)
-    parts = [
-        LineScatter(line_axis, count, subs, part_ref, share_ref, *line_scratch),
-        CubeSum(
-            cube_axis, bits, data_ref, total_ref, cube_scratch[:bits], *cube_scratch[bits:], lag,
-            lambda chunk: load(chunk, grad_refs[0].at[:, :columns]).wait(),
-            store_any,
-        ),
-        SmallSum(
-            cube_axis, bits, line_axis, count, 2, small_ref, small_cube_ref, small_all_ref,
-            *small_scratch,
-        ),
-    ]
+        @pl.when(chunk >= 3 * per_weight)
+        def _():
+            for piece in range(per_chunk):
+                store_out(chunk - 3 * per_weight, piece).start()
+
+    def ready(chunk):
+        @pl.when(chunk == 0)
+        def _():
+            for load in loads[1:4] + loads[7:9]:
+                load.wait()
+
+        @pl.when(chunk < 3 * per_weight)
+        def _():
+            there = pl.ds(pl.multiple_of(chunk % per_weight * columns, columns), columns)
+            right = grads_ref[chunk // per_weight, :, there]
+
+            def rows(index, carry):
+                here = pl.ds(pl.multiple_of(index * tile, tile), tile)
+                data_ref[chunk, here, :] = dot_nn(normed_ref[here, :], right).astype(bf16)
+                return carry
+
+            lax.fori_loop(0, depth // tile, rows, 0)
+
+        @pl.when(chunk >= 3 * per_weight)
+        def _():
+            def piece(index, carry):
+                number = (chunk - 3 * per_weight) * per_chunk + index
+                slot = number % 2
+
+                @pl.when(number + 1 < pieces)
+                def _():
+                    branch_load(number + 1, 1 - slot).start()
+
+                branch_load(number, slot).wait()
+                here = pl.ds(pl.multiple_of(index * width, width), width)
+                data_ref[chunk, here, :] = dot_nn(mixed_ref[...], branch_ref[slot]).astype(bf16)
+                return carry
+
+            lax.fori_loop(0, per_chunk, piece, 0)
+
+    def arrive(start, rows, grad_normed):
+        here = pl.ds(pl.multiple_of(start, grad_normed.shape[0]), grad_normed.shape[0])
+        x = mine_ref[here, :].astype(f32)
+        scale = lax.rsqrt(jnp.mean(x * x, axis=-1, keepdims=True) + 1e-06)
+        hat = x * scale
+        grad_hat = grad_normed * gain_ref[...]
+        inner = jnp.mean(grad_hat * hat, axis=-1, keepdims=True)
+        value = middle_ref[here, :] + scale * (grad_hat - hat * inner)
+        part_ref[rows, :] = value.astype(bf16)
+
+    def arrive_ffn(start, rows, value):
+        ffn_ref[rows, :] = value.astype(bf16)
+
+    line_ffn = LineScatter(line_axis, count, subs, 0, *ffn_scratch, arrive_ffn)
+    line = LineScatter(line_axis, count, subs, 2, *line_scratch, arrive)
+    cube = CubeSum(
+        cube_axis, bits, data_ref, total_ref, cube_scratch[:bits], *cube_scratch[bits:], lag, ready, done
+    )
+    small = SmallSum(
+        cube_axis, bits, line_axis, count, count + 1, 2, own_ref, small_cube_ref, small_all_ref,
+        *small_scratch,
+    )
+    loads[0].wait()
 
     def step(time, carry):
-        for part in parts:
-            part.step(time)
+        line_ffn.step(time)
+        cube.step(time)
+
+        @pl.when(time == 0)
+        def _():
+            for load in loads[4:7]:
+                load.wait()
+
+        products.step(time)
+        line.step(time)
+        small.step(time)
         return carry
 
+    parts = [line_ffn, line, cube, products, small]
     lax.fori_loop(0, max(part.steps for part in parts), step, 0)
+    loads[9].wait()
     for part in parts:
         part.finish()
+    outs = [
+        pltpu.make_async_copy(part_ref.at[my_rows], input_out, out_sem.at[0]),
+        pltpu.make_async_copy(ffn_ref.at[my_rows], ffn_out, out_sem.at[1]),
+    ]
+    for out in outs:
+        out.start()
 
     def stored(chunk, carry):
         store(chunk).wait()
         return carry
 
-    lax.fori_loop(0, chunks, stored, 0)
-
-
-def tail_sums(part, small, grads, line_axis, cube_axis, out_width, columns, subs, lag, cid):
+    lax.fori_loop(0, 3 * per_weight, stored, 0)
+    for chunk in range(chunks - 3 * per_weight):
+        for piece in range(per_chunk):
+            store_out(chunk, piece).wait()
+    for out in outs:
+        out.wait()
+
+
+def tail_sums(
+    grads, weights, x, normed_t, mixed_t, branch, ffn_part, grad_middle_share, gain, small, line_axis,
+    cube_axis, columns, subs, lag, cid,
+):
     count = lax.axis_size(line_axis)
     bits = lax.axis_size(cube_axis).bit_length() - 1
-    rows = grads[0].shape[0]
-    widths = tuple(grad.shape[1] for grad in grads)
-    chunks = sum(widths) // columns
+    tokens, depth = x.shape
+    width = grads[0].shape[1]
+    chunks = 4 * width // columns
     vmem = pl.BlockSpec(memory_space=pltpu.VMEM)
     hbm = pl.BlockSpec(memory_space=pl.ANY)
     small_shape = jax.ShapeDtypeStruct(small.shape, f32)
+    weight_shape = jax.ShapeDtypeStruct((depth, width), bf16)
+    share_shape = jax.ShapeDtypeStruct((tokens // count, depth), bf16)
     return pl.pallas_call(
-        functools.partial(
-            tail_kernel, line_axis, count, subs, cube_axis, bits, lag, widths, out_width
-        ),
+        functools.partial(tail_kernel, line_axis, count, subs, cube_axis, bits, lag),
         out_shape=(
-            jax.ShapeDtypeStruct((part.shape[0] // count, part.shape[1]), f32),
+            share_shape,
+            share_shape,
             small_shape,
             small_shape,
-            *[jax.ShapeDtypeStruct((rows, out_width), bf16)] * (sum(widths) // out_width),
+            weight_shape, weight_shape, weight_shape,
+            jax.ShapeDtypeStruct((width, depth), bf16),
         ),
-        in_specs=[vmem, vmem] + [hbm] * len(grads),
-        out_specs=[vmem, vmem, vmem] + [hbm] * (sum(widths) // out_width),
+        in_specs=[hbm] * 11 + [vmem] * 3,
+        out_specs=[hbm] * 2 + [vmem] * 2 + [hbm] * 4,
         scratch_shapes=[
-            pltpu.VMEM((chunks, rows, columns), bf16),
-            pltpu.VMEM((chunks, rows, columns), bf16),
+            pltpu.VMEM((3, tokens, width), bf16),
+            pltpu.VMEM((3, depth, width), bf16),
+            pltpu.VMEM((2, tokens // count, depth), bf16),
+            pltpu.VMEM((tokens // count, depth), bf16),
+            pltpu.VMEM((depth, tokens), bf16),
+            pltpu.VMEM((width, tokens), bf16),
+            pltpu.VMEM((2, tokens, columns), bf16),
+            pltpu.VMEM(small.shape, f32),
+            pltpu.VMEM((chunks, depth, columns), bf16),
+            pltpu.VMEM((chunks, depth, columns), bf16),
+            pltpu.SemaphoreType.DMA((10,)),
+            pltpu.SemaphoreType.DMA((2,)),
+            pltpu.SemaphoreType.DMA((2,)),
             pltpu.SemaphoreType.DMA((chunks,)),
-            pltpu.SemaphoreType.DMA((chunks,)),
-            *LineScatter.scratch(count, subs, part.shape),
-            *CubeSum.scratch(bits, chunks, rows, columns),
+            pltpu.SemaphoreType.DMA((2,)),
+            *LineScatter.scratch(count, subs, x.shape),
+            *LineScatter.scratch(count, subs, x.shape),
+            *CubeSum.scratch(bits, chunks, depth, columns),
             *SmallSum.scratch(bits, count, small.shape),
         ],
         compiler_params=pltpu.CompilerParams(
             collective_id=cid, has_side_effects=True, vmem_limit_bytes=63 * 2**20
         ),
-        cost_estimate=cost(110),
+        cost_estimate=cost(20),
         name="tail_sums",
-    )(part, small, *grads)
-
-
-def after(value, other):
-    return lax.optimization_barrier((value, other))[0]
-
-
-class PermutedScatter:
-    def __init__(self, part, axis):
-        self.part, self.axis = part, axis
-        self.count = lax.axis_size(axis)
-        self.me = lax.axis_index(axis)
-        self.share = part.shape[0] // self.count
-        self.time = 0
-        self.arrived = None
-
-    def block(self, owner):
-        owner = jnp.clip(owner, 0, self.count - 1)
-        return lax.dynamic_slice_in_dim(self.part, owner * self.share, self.share, 0)
-
-    def hop(self, *others):
-        if self.time >= self.count - 1:
-            return others
-        to_right = self.block(self.count - 1 - self.time + self.me)
-        to_left = self.block(self.time - (self.count - 1) + self.me)
-        if self.arrived is not None:
-            to_right = add_low(to_right, self.arrived[0])
-            to_left = add_low(to_left, self.arrived[1])
-        to_right, to_left, *others = lax.optimization_barrier((to_right, to_left, *others))
-        right = [(index, index + 1) for index in range(self.count - 1)]
-        left = [(index + 1, index) for index in range(self.count - 1)]
-        self.arrived = (
-            lax.ppermute(to_right, self.axis, right), lax.ppermute(to_left, self.axis, left)
+    )(
+        *grads, *weights, x, normed_t, mixed_t, branch, ffn_part, grad_middle_share, gain[None], small
+    )
+
+
+class Transposes:
+    def __init__(self, pairs, stage_ref, sem, first, per_step, before):
+        self.pairs, self.stage_ref, self.sem = pairs, stage_ref, sem
+        self.first, self.per_step, self.before = first, per_step, before
+        self.tasks = []
+        for index, (source_ref, _) in enumerate(pairs):
+            self.tasks += [(index, block) for block in range(source_ref.shape[1] // lanes)]
+        self.steps = first + -(-len(self.tasks) // per_step)
+
+    def store(self, index, block, slot):
+        there = pl.ds(pl.multiple_of(block * lanes, lanes), lanes)
+        return pltpu.make_async_copy(
+            self.stage_ref.at[slot], self.pairs[index][1].at[there], self.sem.at[slot]
         )
-        self.time += 1
-        return others
-
-    def total(self):
-        while self.time < self.count - 1:
-            self.hop()
-        return (
-            self.block(self.me).astype(f32)
-            + self.arrived[0].astype(f32) + self.arrived[1].astype(f32)
-        )
+
+    def step(self, time):
+        pl.when(time == self.first)(self.before)
+        offset = 0
+        for index, (source_ref, _) in enumerate(self.pairs):
+            blocks = source_ref.shape[1] // lanes
+            for turn in range(self.per_step):
+                task = (time - self.first) * self.per_step + turn
+                slot = task % 2
+                block = task - offset
+
+                @pl.when((block >= 0) & (block < blocks))
+                def _():
+                    @pl.when(task >= 2)
+                    def _():
+                        self.store(index, 0, slot).wait()
+
+                    there = pl.ds(pl.multiple_of(block * lanes, lanes), lanes)
+
+                    def rows(place, carry):
+                        here = pl.ds(pl.multiple_of(place * tile, tile), tile)
+                        value = jnp.transpose(source_ref[here, there].astype(f32))
+                        self.stage_ref[slot, :, here] = value.astype(bf16)
+                        return carry
+
+                    lax.fori_loop(0, source_ref.shape[0] // tile, rows, 0)
+                    self.store(index, block, slot).start()
+            offset += blocks
+
+    def finish(self):
+        for task in range(len(self.tasks) - 2, len(self.tasks)):
+            self.store(self.tasks[task][0], self.tasks[task][1], task % 2).wait()
+
+
+def widen_kernel(
+    ffn_ref, down_ref, q_ref, k_ref, v_ref, o_ref, x_ref, attn_ref, share_ref, input_ref, all_ref,
+    cube_ref, gate_out, up_out, down_out, q_out, k_out, v_out, o_out, output_out, input_out,
+    gain_attn_out, gain_ffn_out,
+):
+    width = gate_out.shape[1]
+    gate_out[...] = ffn_ref[:, :width].astype(f32)
+    up_out[...] = ffn_ref[:, width:].astype(f32)
+    down_out[...] = down_ref[...].astype(f32)
+    q_out[...] = q_ref[...].astype(f32)
+    k_out[...] = k_ref[...].astype(f32)
+    v_out[...] = v_ref[...].astype(f32)
+    o_out[...] = o_ref[...].astype(f32)
+    middle = x_ref[...].astype(f32) + attn_ref[...].astype(f32)
+    output_out[...] = (middle + share_ref[...].astype(f32)).astype(bf16)
+    input_out[...] = input_ref[...]
+    gain_attn_out[...] = all_ref[0:1]
+    gain_ffn_out[...] = cube_ref[1:2]
+
+
+def widen(ffn, down, query, key, value, out, x, attn_total, ffn_share, input_grad, small_all, small_cube, axis):
+    width, depth = down.shape
+    local = query.shape[1]
+    steps = depth // lanes
+    share = ffn_share.shape[0]
+    piece = share // steps
+    base = (lax.axis_index(axis) * steps).astype(jnp.int32).reshape(1)
+
+    def rows(columns):
+        return pl.BlockSpec((lanes, columns), lambda i, base: (i, 0))
+
+    out_rows = pl.BlockSpec((local // steps, depth), lambda i, base: (i, 0))
+    down_rows = pl.BlockSpec((width // steps, depth), lambda i, base: (i, 0))
+    share_rows = pl.BlockSpec((piece, depth), lambda i, base: (i, 0))
+    mine = pl.BlockSpec((piece, depth), lambda i, base: (base[0] + i, 0))
+    small = pl.BlockSpec(small_all.shape, lambda i, base: (0, 0))
+    line = pl.BlockSpec((1, depth), lambda i, base: (0, 0))
+    share_shape = jax.ShapeDtypeStruct((share, depth), bf16)
+    return pl.pallas_call(
+        lambda base, *refs: widen_kernel(*refs),
+        out_shape=(
+            jax.ShapeDtypeStruct((depth, width), f32),
+            jax.ShapeDtypeStruct((depth, width), f32),
+            jax.ShapeDtypeStruct((width, depth), f32),
+            *[jax.ShapeDtypeStruct((depth, local), f32)] * 3,
+            jax.ShapeDtypeStruct((local, depth), f32),
+            share_shape,
+            share_shape,
+            jax.ShapeDtypeStruct((1, depth), f32),
+            jax.ShapeDtypeStruct((1, depth), f32),
+        ),
+        grid_spec=pltpu.PrefetchScalarGridSpec(
+            num_scalar_prefetch=1,
+            grid=(steps,),
+            in_specs=[
+                rows(2 * width), down_rows, rows(local), rows(local), rows(local), out_rows,
+                mine, mine, share_rows, share_rows, small, small,
+            ],
+            out_specs=[
+                rows(width), rows(width), down_rows,
+                rows(local), rows(local), rows(local), out_rows, share_rows, share_rows, line, line,
+            ],
+        ),
+        cost_estimate=cost(26),
+        name="widen",
+    )(base, ffn, down, query, key, value, out, x, attn_total, ffn_share, input_grad, small_all, small_cube)
 
 
 def project(left_side, right_side):
@@ -1153,12 +1457,6 @@
 
 def project_back(left_side, right_side):
     return dot_nt(left_side, right_side)
-
-
-def weight_term(left_side, right_side):
-    return lax.dot_general(
-        left_side, right_side, (((0,), (0,)), ((), ())), preferred_element_type=f32
-    ).astype(bf16)
 
 
 def norm_scale(signal):
@@ -1186,13 +1484,8 @@
     heads_shape = (row_count, length, local_width)
     share_shape = (row_count, share_rows, model_width)
 
-    def take_share(signal):
-        part = lax.dynamic_slice_in_dim(
-            signal.reshape(row_count, length, -1), first_row, share_rows, 1
-        )
-        return part.reshape(row_count * share_rows, -1)
-
-    flat_inputs = inputs.reshape(token_count, model_width).astype(f32)
+    low_inputs = inputs.reshape(token_count, model_width)
+    flat_inputs = low_inputs.astype(f32)
     grad_out = cotangent.reshape(token_count, model_width)
     scale_attn = norm_scale(flat_inputs)
     normed = (flat_inputs * scale_attn * gain_attn).astype(bf16)
@@ -1205,8 +1498,8 @@
     mixed, totals = attend(queries, keys, values, segments, lines)
     mixed_flat = mixed.reshape(token_count, local_width)
     attn_part = project(mixed_flat, w_out)
-    attn_total, normed_ffn, grad_hidden = enter_ffn(
-        attn_part.astype(bf16), inputs.reshape(token_count, model_width), grad_out, w_down,
+    attn_total, normed_ffn, grad_hidden, normed_t, mixed_t = enter_ffn(
+        attn_part.astype(bf16), low_inputs, grad_out, w_down, normed, mixed_flat,
         gain_ffn, "tensor", line_chunks, 0,
     )
     gate_pre = project(normed_ffn, w_gate)
@@ -1215,63 +1508,45 @@
     hidden = (act_value * up_pre).astype(bf16)
     grad_gate = act_pull(grad_hidden * up_pre)[0].astype(bf16)
     grad_up = (grad_hidden * act_value).astype(bf16)
+    down = lax.dot_general(
+        hidden, grad_out, (((0,), (0,)), ((), ())), preferred_element_type=f32
+    ).astype(bf16)
+    grad_gate, grad_up, down = lax.optimization_barrier((grad_gate, grad_up, down))
+    down = lax.psum(down, "dp")
     norm_ffn_part = project_back(grad_gate, w_gate) + project_back(grad_up, w_up)
-    gate_up_grad = weight_term(normed_ffn, jnp.concatenate([grad_gate, grad_up], axis=1))
-    down_grad = weight_term(hidden, grad_out)
-    norm_ffn_low, gate_up_grad, down_grad = lax.optimization_barrier(
-        (norm_ffn_part.astype(bf16), gate_up_grad, down_grad)
-    )
-    grad_branch, ffn_part, grad_middle_share, gain_ffn_part = leave_ffn(
-        norm_ffn_low, inputs.reshape(token_count, model_width), attn_total, grad_out, hidden, w_down,
-        gain_ffn, "tensor", line_chunks, 1,
-    )
-    gate_up_piece = lax.psum_scatter(gate_up_grad, "dp", scatter_dimension=0, tiled=True)
-    down_piece = lax.psum_scatter(down_grad, "dp", scatter_dimension=1, tiled=True)
-    down_piece = after(down_piece, grad_branch)
-    down_grad = lax.all_gather(down_piece, "dp", axis=1, tiled=True).astype(f32)
-    scatter = PermutedScatter(ffn_part, "tensor")
-    scatter.hop()
+    grad_branch, ffn_part, ffn_grad, grad_middle_share, gain_ffn_part = leave_ffn(
+        norm_ffn_part.astype(bf16), low_inputs, attn_total, grad_out, hidden, w_down, normed_ffn,
+        grad_gate, grad_up, gain_ffn, "tensor", line_chunks, 1,
+    )
+    ffn_grad, down, grad_branch = lax.optimization_barrier((ffn_grad, down, grad_branch))
+    ffn_grad = lax.psum(ffn_grad, "dp")
     grad_mixed = project_back(grad_branch, w_out).astype(bf16).reshape(heads_shape)
-    (grad_mixed,) = scatter.hop(grad_mixed)
     grad_query, grad_key, grad_value, sums = attend_back(
         queries, keys, values, grad_mixed, mixed, totals, segments, lines
     )
-    gate_up_piece = after(gate_up_piece, grad_query)
-    gate_up_grad = lax.all_gather(gate_up_piece, "dp", axis=0, tiled=True)
-    gate_grad, up_grad = jnp.split(gate_up_grad.astype(f32), 2, axis=1)
-    grad_query, grad_key, grad_value = scatter.hop(grad_query, grad_key, grad_value)
     grad_query = grad_query.reshape(token_count, local_width)
     grad_key = grad_key.reshape(token_count, local_width)
     grad_value = grad_value.reshape(token_count, local_width)
     sums = jnp.sum(sums, axis=0).reshape(head_count, -1)
     table_grad = lax.dot_general(onehot, sums, (((1,), (1,)), ((), ())), precision=highest)
-    norm_attn_part = (
-        project_back(grad_query, w_query)
-        + project_back(grad_key, w_key)
-        + project_back(grad_value, w_value)
-    )
-    gain_attn_part = jnp.sum(norm_attn_part * (flat_inputs * scale_attn), axis=0)
-    qkv_grad = weight_term(normed, jnp.concatenate([grad_query, grad_key, grad_value], axis=1))
-    out_grad = weight_term(grad_branch, mixed_flat)
     table_line = jnp.pad(table_grad.reshape(-1), (0, model_width - bucket_count * head_count))
-    small = jnp.stack([gain_attn_part, gain_ffn_part[0], table_line])
+    small = jnp.stack([jnp.zeros_like(table_line), gain_ffn_part[0], table_line])
     small = jnp.pad(small, ((0, 8 - small.shape[0]), (0, 0)))
-    ffn_share = scatter.total()
-    middle_share = take_share(inputs).astype(f32) + take_share(attn_total).astype(f32)
-    output = (middle_share + ffn_share).reshape(share_shape).astype(bf16)
-    grad_normed_attn, small_cube, small_all, *attn_sums = tail_sums(
-        norm_attn_part.astype(bf16), small, [qkv_grad, out_grad], "tensor", "dp",
-        local_width, tail_columns, tail_subs, tail_lag, 2,
-    )
-    query_grad, key_grad, value_grad, out_grad = [grad.astype(f32) for grad in attn_sums]
-    out_grad = jnp.transpose(out_grad)
-    gain_attn_grad, gain_ffn_grad = small_all[0], small_cube[1]
+    input_grad, ffn_share, small_cube, small_all, *attn_grads = tail_sums(
+        (grad_query, grad_key, grad_value), (w_query, w_key, w_value), low_inputs, normed_t, mixed_t,
+        grad_branch, ffn_part, grad_middle_share, gain_attn, small, "tensor", "dp",
+        tail_columns, tail_subs, tail_lag, 2,
+    )
+    (
+        gate_grad, up_grad, down_grad, query_grad, key_grad, value_grad, out_grad, output, input_grad,
+        gain_attn_grad, gain_ffn_grad,
+    ) = widen(
+        ffn_grad, down, *attn_grads, low_inputs, attn_total, ffn_share, input_grad, small_all,
+        small_cube, "tensor",
+    )
+    gain_attn_grad, gain_ffn_grad = gain_attn_grad[0], gain_ffn_grad[0]
     table_grad = small_cube[2, : bucket_count * head_count].reshape(bucket_count, head_count)
-    inputs_share = take_share(flat_inputs)
-    grad_input = grad_middle_share + norm_back(
-        inputs_share, take_share(scale_attn), gain_attn, grad_normed_attn
-    )
-    input_grad = grad_input.reshape(share_shape).astype(bf16)
+    output, input_grad = output.reshape(share_shape), input_grad.reshape(share_shape)
     return (
         output, input_grad, query_grad, key_grad, value_grad, out_grad, gate_grad, up_grad,
         down_grad, gain_attn_grad, gain_ffn_grad, table_grad,

time: 663 us -> 602 us (0.908)
  Pallas kernels: 413 us -> 491 us
  matrix products: 121 us -> 71.9 us
  other arithmetic: 49.5 us -> 6.3 us
  local copies, waits for them, and re-layouts: 29.5 us -> 8.58 us
  starting transfers between devices: 19 us -> 0.08 us
  waiting for transfers between devices: 9.84 us -> 0.06 us
    pallas_call x1, Pallas kernels: 123 us -> 170 us  [tail_sums(): pl.pallas_call(functools.partial(tail_kernel, line_axis, count, subs, cub...]
    convert_element_type x9 -> x1, other arithmetic: 36.6 us -> 1.03 us  [shards(): normed = (flat_inputs * scale_attn * gain_attn).astype(bf16)]
    dot_general x4 -> x1, matrix products: 38.1 us -> 7.33 us  [shards(): lax.dot_general(hidden, grad_out, (((0,), (0,)), ((), ())), preferred_ele...]
    pallas_call x0 -> x1, Pallas kernels: none -> 28.1 us  [widen(): pl.pallas_call(lambda base, *refs: widen_kernel(*refs), out_shape=(jax.Sh...]
    dot_general x6 -> x3, matrix products: 44.7 us -> 25.4 us  [dot_nt(): lax.dot_general(left_side, right_side, (((1,), (1,)), ((), ())), preferre...]
    ppermute x6 -> x0, starting transfers between devices: 18.8 us -> none  [the longest x3 10.7 us: hop(): lax.ppermute(to_right, self.axis, right)]
    split x1 -> x0, local copies, waits for them, and re-layouts: 13.3 us -> none  [shards(): gate_grad, up_grad = jnp.split(gate_up_grad.astype(f32), 2, axis=1)]
    ppermute x6 -> x0, waiting for transfers between devices: 9.05 us -> none  [the longest x3 8.24 us: hop(): lax.ppermute(to_left, self.axis, left)]
  transfers between devices with their start and end apart: 10 -> 2, of which waited for: 2 -> 0; matrix products, arithmetic and copies ran while one was open for 15% -> 4% of each run, Pallas kernels for 42% -> 55%
where the time goes in v5:
time: 602 us; the launch traced here: 593 us
  Pallas kernels  491 us (82%)
  matrix products  71.9 us (12%)
  between operations  14.6 us (2%)
  local copies, waits for them, and re-layouts  8.58 us (1%)
  other arithmetic  6.3 us (1%)
    pallas_call x1, Pallas kernels, tail_sums(): pl.pallas_call(functools.partial(tail_kernel, line_axis, count, subs, cub...  170 us
    pallas_call x1, Pallas kernels, leave_ffn(): pl.pallas_call(functools.partial(leave_kernel, axis, count, chunks), out_...  118 us
    pallas_call x1, Pallas kernels, enter_ffn(): pl.pallas_call(functools.partial(enter_kernel, axis, count, chunks), out_...  112 us
    dot_general x6, matrix products, project(): return jnp.dot(left_side, right_side, preferred_element_type=f32)  38.8 us
    pallas_call x1, Pallas kernels, attend_back(): pl.pallas_call(functools.partial(backward_kernel, block_count), out_shape...  36.3 us
    pallas_call x1, Pallas kernels, widen(): pl.pallas_call(lambda base, *refs: widen_kernel(*refs), out_shape=(jax.Sh...  28.1 us
    pallas_call x1, Pallas kernels, attend(): pl.pallas_call(functools.partial(forward_kernel, block_count), out_shape=...  26.3 us
    dot_general x3, matrix products, dot_nt(): lax.dot_general(left_side, right_side, (((1,), (1,)), ((), ())), preferre...  25.4 us
  transfers between devices with their start and end apart: 2, of which 0 were waited for; matrix products, arithmetic and copies ran while one was open for 4% of the time, Pallas kernels for 55%

profile of v5, /device:TPU:17, one launch (start us, length us, event | category | flops | bytes accessed | tf_op | source)
XLA Modules:
  0.0 592.7 jit_solution(18012611946285895825)
XLA Ops:
  7.2 0.0 copy-start
  7.2 0.0 copy-start.7
  7.2 0.0 all-reduce.5.cloned.1.call-start
  7.3 0.0 copy-start.2
  7.3 3.2 fusion
  10.5 0.0 copy-done.7
  10.5 0.2 copy-done.2
  10.7 1.0 fusion.2.first_hbm
  11.7 0.6 copy-done.12
  12.3 3.3 fusion.10.q_ref
  15.6 0.0 copy-done.13
  15.6 3.3 fusion.11.k_ref
  18.9 0.0 copy-done.3
  18.9 0.0 copy-done.14
  18.9 3.3 fusion.12.v_ref
  22.2 0.1 subtract_abs_fusion
  22.3 0.0 copy-start.4
  22.3 0.6 copy-done.4
  22.9 0.0 copy-done
  22.9 0.2 fusion.15
  23.1 0.7 copy.39.line_ref
  23.8 0.5 broadcast.252
  24.3 0.0 copy-done.6
  24.3 0.7 reduce.9
  25.0 0.1 fusion.22
  25.1 0.1 copy.45
  25.2 0.1 copy.46
  25.3 0.7 convert_reduce_fusion
  26.0 0.5 broadcast_add_fusion.last_ref
  26.5 1.0 copy.38.seg_col_ref
  27.5 26.3 %attend.1 = (bf16[1,1024,512]{2,1,0:T(8,128)(2,1)}, f32[1,4,2,1024]{3,2,1,0:T(2,128)}) custom-call(s32[4]{0:T(128)} %get-tuple-element.131.first_ref, s32[4]{0:T(128)} %broadcast_add_fusion.last_ref, bf16[1,1024,512]{2,1,0:T(8,128)(2,1)} %fusion.10.q_ref, bf16[1,1024,512]{2,1,0:T(8,128)(2,1)} %fusion.11.k_ref, bf16[1,1024,512]{2,1,0:T(8,128)(2,1)} %fusion.12.v_ref, ...), custom_call_target="tpu_custom_call" | custom-call | flops 24999999488 | bytes 1000000 | tf_op jit(solution)/shard_map/attend/pallas_call | solution.py:269
  53.8 0.0 copy-done.11
  53.8 5.6 convolution_convert_fusion.1.part_hbm
  59.4 111.8 %enter_ffn.1 = (bf16[1024,2048]{1,0:T(8,128)(2,1)}, bf16[1024,2048]{1,0:T(8,128)(2,1)}, f32[1024,1280]{1,0:T(8,128)}, bf16[2048,1024]{1,0:T(8,128)(2,1)}, bf16[512,1024]{1,0:T(8,128)(2,1)}) custom-call(bf16[1024,2048]{1,0:T(8,128)(2,1)} %convolution_convert_fusion.1.part_hbm, bf16[1024,2048]{1,0:T(8,128)(2,1)} %bitcast.59, bf16[1024,2048]{1,0:T(8,128)(2,1)} %bitcast.72, ...), custom_call_target="tpu_custom_call" | custom-call | flops 109999996928 | bytes 1000000 | tf_op jit(solution)/shard_map/enter_ffn/pallas_call | solution.py:935
  171.2 0.0 copy-start.9
  171.2 9.0 %fusion.23 = f32[1024,1280]{1,0:T(8,128)S(1)} fusion(bf16[1024,2048]{1,0:T(8,128)(2,1)} %get-tuple-element.55.normed_hbm, bf16[2048,1280]{1,0:T(8,128)(2,1)} %param.20), kind=kOutput, calls=%fused_computation.49 | convolution fusion | flops 5368709120 | bytes 14680064 | tf_op jit(solution)/shard_map/dot_general | solution.py:1455
  180.3 0.0 copy-done.9
  180.3 0.0 copy-start.10
  180.3 14.2 %multiply_convert_fusion = (bf16[1024,1280]{1,0:T(8,128)(2,1)S(1)}, bf16[1024,1280]{1,0:T(8,128)(2,1)}, bf16[1024,1280]{1,0:T(8,128)(2,1)S(1)}) fusion(f32[1024,1280]{1,0:T(8,128)S(1)} %fusion.23, f32[1024,1280]{1,0:T(8,128)} %get-tuple-element.54, bf16[1024,2048]{1,0:T(8,128)(2,1)} %get-tuple-element.55.normed_hbm, bf16[2048,1280]{1,0:T(8,128)(2,1)S(1)} %copy-done.9), kind=kOutput, calls=%fused_computation.16 | convolution fusion | flops 5402787840 | bytes 27787264 | tf_op jit(solution)/shard_map/dot_general | solution.py:1455
  194.5 1.5 copy-done.15
  196.0 0.0 copy-done.10
  196.0 7.3 %convolution_convert_fusion = bf16[1280,2048]{1,0:T(8,128)(2,1)} fusion(bf16[1024,1280]{1,0:T(8,128)(2,1)S(1)} %get-tuple-element.132.hidden_hbm, bf16[1,1024,2048]{2,1,0:T(8,128)(2,1)S(1)} %copy-done.10), kind=kOutput, calls=%fused_computation.6 | convolution fusion | flops 5371330560 | bytes 12058624 | tf_op jit(solution)/shard_map/dot_general | solution.py:1511
  203.4 0.0 all-reduce.5.cloned.1.call-update
  203.4 0.0 all-reduce.7.cloned.1.call-start
  203.4 8.4 %fusion.24 = f32[1024,2048]{1,0:T(8,128)S(1)} fusion(bf16[1024,1280]{1,0:T(8,128)(2,1)} %get-tuple-element.56.gate_hbm, bf16[2048,1280]{1,0:T(8,128)(2,1)} %param.20), kind=kOutput, calls=%fused_computation.50 | convolution fusion | flops 5368709120 | bytes 16252928 | tf_op jit(solution)/shard_map/dot_general | solution.py:49
  211.8 0.0 copy-done.16
  211.8 10.8 %add_convert_fusion.part_hbm = bf16[1024,2048]{1,0:T(8,128)(2,1)} fusion(f32[1024,2048]{1,0:T(8,128)S(1)} %fusion.24, bf16[1024,1280]{1,0:T(8,128)(2,1)S(1)} %get-tuple-element.57.up_hbm, bf16[2048,1280]{1,0:T(8,128)(2,1)} %param.21), kind=kOutput, calls=%fused_computation.5 | convolution fusion | flops 5372903424 | bytes 20447232 | tf_op jit(solution)/shard_map/dot_general | solution.py:49
  222.6 118.4 %leave_ffn.1 = (bf16[1024,2048]{1,0:T(8,128)(2,1)}, bf16[1024,2048]{1,0:T(8,128)(2,1)}, bf16[2048,2560]{1,0:T(8,128)(2,1)}, f32[256,2048]{1,0:T(8,128)}, f32[1,2048]{1,0:T(1,128)}) custom-call(bf16[1024,2048]{1,0:T(8,128)(2,1)} %add_convert_fusion.part_hbm, bf16[1024,2048]{1,0:T(8,128)(2,1)} %bitcast.60, ...), custom_call_target="tpu_custom_call" | custom-call | flops 109999996928 | bytes 1000000 | tf_op jit(solution)/shard_map/leave_ffn/pallas_call | solution.py:1033
  341.1 0.0 all-reduce.5.cloned.1.call-done.refs_1_
  341.1 6.2 %fusion.13.grad_ref = bf16[1,1024,512]{2,1,0:T(8,128)(2,1)} fusion(bf16[1024,2048]{1,0:T(8,128)(2,1)} %get-tuple-element.64.branch_hbm, bf16[512,2048]{1,0:T(8,128)(2,1)} %param.19), kind=kOutput, calls=%fused_computation.27 | convolution fusion | flops 2148007936 | bytes 7340032 | tf_op jit(solution)/shard_map/dot_general | solution.py:49
  347.3 0.0 all-reduce.7.cloned.1.call-update
  347.3 0.0 copy-start.5
  347.3 36.3 %attend_back.1 = (bf16[1,1024,512]{2,1,0:T(8,128)(2,1)}, bf16[1,1024,512]{2,1,0:T(8,128)(2,1)}, bf16[1,1024,512]{2,1,0:T(8,128)(2,1)}, f32[1,8,5,512]{3,2,1,0:T(8,128)}) custom-call(s32[4]{0:T(128)} %get-tuple-element.131.first_ref, s32[4]{0:T(128)} %broadcast_add_fusion.last_ref, bf16[1,1024,512]{2,1,0:T(8,128)(2,1)} %fusion.10.q_ref, ...), custom_call_target="tpu_custom_call" | custom-call | flops 35000000512 | bytes 1000000 | tf_op jit(solution)/shard_map/attend_back/pallas_call | solution.py:297
  383.7 1.0 copy.47
  384.6 0.2 fusion.14
  384.9 0.1 reshape.293
  385.0 0.1 pad_maximum_fusion
  385.1 0.6 pad.9.small_ref
  385.7 170.3 %tail_sums.1 = (bf16[256,2048]{1,0:T(8,128)(2,1)}, bf16[256,2048]{1,0:T(8,128)(2,1)}, f32[8,2048]{1,0:T(8,128)}, f32[8,2048]{1,0:T(8,128)}, bf16[2048,512]{1,0:T...) custom-call(bf16[1024,512]{1,0:T(8,128)(2,1)} %bitcast.77, ...), custom_call_target="tpu_custom_call" | custom-call | flops 20000000000 | bytes 1000000 | tf_op jit(solution)/shard_map/tail_sums/pallas_call | solution.py:1295
  556.0 0.7 slice_reduce_fusion
  556.8 0.1 reshape_squeeze.3
  556.8 0.7 copy.43
  557.5 28.1 %widen.1 = (f32[2048,1280]{1,0:T(8,128)}, f32[2048,1280]{1,0:T(8,128)}, f32[1280,2048]{1,0:T(8,128)}, f32[2048,512]{1,0:T(8,128)}, f32[2048,512]{1,0:T(8,128)}, ...) custom-call(s32[1]{0:T(128)} %bitcast.base, ...), custom_call_target="tpu_custom_call" | custom-call | flops 25999998976 | bytes 1000000 | tf_op jit(solution)/shard_map/widen/pallas_call | solution.py:1424
  585.6 0.0 copy-done.1
  (22 shorter events, 0.1 us)
Async XLA Ops:
  7.2 15.7 %copy-start = (f32[32,8]{0,1:T(8,128)S(1)}, f32[32,8]{0,1:T(8,128)}, u32[]{:S(2)}) copy-start(f32[32,8]{0,1:T(8,128)} %param.25) | copy-start | bytes 3076
  7.2 3.3 copy-start.7
  7.2 333.9 %all-reduce.5.cloned.1.call-start = ((), (), s32[]{:S(2)}) async-start(), calls=%async_computation | async-start | bytes 10485760 | tf_op jit(solution)/shard_map/psum | solution.py:1515
  7.3 3.5 copy-start.2
  10.7 1.6 copy-start.12
  12.3 6.6 %copy-start.3 = (bf16[1024,2048]{1,0:T(8,128)(2,1)}, bf16[1024,2048]{1,0:T(8,128)(2,1)S(1)}, u32[]{:S(2)}) copy-start(bf16[1024,2048]{1,0:T(8,128)(2,1)S(1)} %fusion.2.first_hbm) | copy-start | bytes 12582916
  12.3 3.3 copy-start.13
  15.6 3.3 copy-start.14
  18.9 5.4 copy-start.6
  22.3 0.6 copy-start.4
  27.5 26.3 %copy-start.11 = (bf16[512,2048]{1,0:T(8,128)(2,1)S(1)}, bf16[512,2048]{1,0:T(8,128)(2,1)}, u32[]{:S(2)}) copy-start(bf16[512,2048]{1,0:T(8,128)(2,1)} %param.19) | copy-start | bytes 6291460
  171.2 9.1 %copy-start.9 = (bf16[2048,1280]{1,0:T(8,128)(2,1)S(1)}, bf16[2048,1280]{1,0:T(8,128)(2,1)}, u32[]{:S(2)}) copy-start(bf16[2048,1280]{1,0:T(8,128)(2,1)} %param.21) | copy-start | bytes 15728644
  180.3 15.7 %copy-start.10 = (bf16[1,1024,2048]{2,1,0:T(8,128)(2,1)S(1)}, bf16[1,1024,2048]{2,1,0:T(8,128)(2,1)}, u32[]{:S(2)}) copy-start(bf16[1,1024,2048]{2,1,0:T(8,128)(2,1)} %param.15) | copy-start | bytes 12582916
  194.5 1.5 copy-start.15
  194.5 17.3 %copy-start.16 = (bf16[1024,1280]{1,0:T(8,128)(2,1)}, bf16[1024,1280]{1,0:T(8,128)(2,1)S(1)}, u32[]{:S(2)}) copy-start(bf16[1024,1280]{1,0:T(8,128)(2,1)S(1)} %get-tuple-element.57.up_hbm) | copy-start | bytes 7864324
  203.4 354.1 %all-reduce.7.cloned.1.call-start = ((), (), s32[]{:S(2)}) async-start(), calls=%async_computation.1 | async-start | bytes 20971520 | tf_op jit(solution)/shard_map/psum | solution.py:1522
  347.3 37.3 %copy-start.5 = (s32[2560]{0:T(1024)S(1)}, s32[2560]{0:T(1024)}, u32[]{:S(2)}) copy-start(s32[2560]{0:T(1024)} %copy-done.4) | copy-start | bytes 30724
  347.3 37.7 %copy-start.8 = (f32[1,2048]{1,0:T(1,128)S(1)}, f32[1,2048]{1,0:T(1,128)}, u32[]{:S(2)}) copy-start(f32[1,2048]{1,0:T(1,128)} %get-tuple-element.73) | copy-start | bytes 24580
  557.5 28.1 %copy-start.1 = (f32[32,8]{0,1:T(8,128)S(1)}, f32[32,8]{0,1:T(8,128)}, u32[]{:S(2)}) copy-start(f32[32,8]{0,1:T(8,128)} %param.25) | copy-start | bytes 3076
Sparse Core Ops, SparseCore 0:
  203.5 96.2 all-reduce.4
  347.4 202.7 all-reduce.6

commit v6 on v5

--- a/solution.py
+++ b/solution.py
@@ -14,10 +14,12 @@
 group_pairs = 1
 line_chunks = 16
 tail_columns = 256
-tail_subs = 8
-tail_lag = 3
-line_lag = 3
+tail_subs = 4
+tail_lag = 2
+line_lag = 2
 sum_lag = 2
+gelu_scale = 0.7978845608028654
+gelu_cubic = 0.044715
 lanes = 128
 bf16 = jnp.bfloat16
 f32 = jnp.float32
@@ -105,9 +107,18 @@
     return slice(pair * lanes, (pair + 1) * lanes)
 
 
+def code_keys(group, k_ref, k_code_ref, coded_ref):
+    for pair in range(group):
+        keys = k_ref[0, :, pair_columns(pair)]
+        for half in range(2):
+            coded_ref[2 * pair + half] = jnp.where(
+                half_mask(keys.shape, half), keys, k_code_ref[0]
+            )
+
+
 def forward_kernel(
-    block_count, first_ref, last_ref, q_ref, k_ref, v_ref, seg_row_ref, seg_col_ref, line_ref,
-    out_ref, lse_ref, bias_ref, vt_ref,
+    block_count, seg_ref, q_ref, k_ref, v_ref, q_code_ref, k_code_ref, line_ref,
+    out_ref, lse_ref, bias_ref, vt_ref, coded_ref,
 ):
     row = pl.program_id(0)
     mid = lanes // 2
@@ -119,27 +130,26 @@
         ones = jnp.ones_like(values_t)
         vt_ref[2 * pair] = jnp.where(place < mid, values_t, ones)
         vt_ref[2 * pair + 1] = jnp.where(place < mid, ones, values_t)
+    code_keys(group, k_ref, k_code_ref, coded_ref)
 
     @pl.loop(0, block_count)
     def _(block):
-        first = first_ref[row * block_count + block]
-        last = last_ref[row * block_count + block]
+        first, last = block_range(seg_ref, row, block, block_count)
         here = pl.ds(pl.multiple_of(block * tile, tile), tile)
 
         def run(number):
             rows = pl.ds(pl.multiple_of(first * tile, tile), number * tile)
             shift = first - block + block_count - 1
             bias_rows = pl.ds(pl.multiple_of(shift * tile, tile), number * tile)
-            same = seg_col_ref[0, rows, :] == seg_row_ref[0, :, here]
+            q_code = q_code_ref[0, here, :]
             for pair in range(group):
-                keys = k_ref[0, rows, pair_columns(pair)]
                 q_pair = q_ref[0, here, pair_columns(pair)]
                 sums = []
                 tops = []
                 for half in range(2):
                     head = 2 * pair + half
-                    scores = dot_nt(keys, keep_half(q_pair, half)) + bias_ref[head, bias_rows, :]
-                    scores = jnp.where(same, scores, -1000000000.0)
+                    q_coded = jnp.where(half_mask(q_pair.shape, half), q_pair, q_code)
+                    scores = dot_nt(coded_ref[head, rows, :], q_coded) + bias_ref[head, bias_rows, :]
                     top = jnp.max(scores, axis=0, keepdims=True)
                     weights = jnp.exp(scores - top).astype(bf16)
                     sums.append(dot_nn(vt_ref[head, :, rows], weights))
@@ -158,9 +168,9 @@
 
 
 def backward_kernel(
-    block_count, first_ref, last_ref, q_ref, k_ref, v_ref, grad_ref, out_ref, lse_ref, seg_row_ref,
-    seg_col_ref, line_ref, dq_ref, dk_ref, dv_ref, sums_ref,
-    bias_ref, gbias_ref, kt_ref, dk_acc, dv_acc,
+    block_count, seg_ref, q_ref, k_ref, v_ref, grad_ref, out_ref, lse_ref, q_code_ref, k_code_ref,
+    line_ref, dq_ref, dk_ref, dv_ref, sums_ref,
+    bias_ref, gbias_ref, kt_ref, dk_acc, dv_acc, coded_ref,
 ):
     row = pl.program_id(0)
     mid = lanes // 2
@@ -173,24 +183,23 @@
         zeros = jnp.zeros_like(keys_t)
         kt_ref[2 * pair] = jnp.where(place < mid, keys_t, zeros)
         kt_ref[2 * pair + 1] = jnp.where(place < mid, zeros, keys_t)
+    code_keys(group, k_ref, k_code_ref, coded_ref)
     gbias_ref[...] = jnp.zeros_like(gbias_ref)
     dk_acc[...] = jnp.zeros_like(dk_acc)
     dv_acc[...] = jnp.zeros_like(dv_acc)
 
     @pl.loop(0, block_count)
     def _(block):
-        first = first_ref[row * block_count + block]
-        last = last_ref[row * block_count + block]
+        first, last = block_range(seg_ref, row, block, block_count)
         here = pl.ds(pl.multiple_of(block * tile, tile), tile)
 
         def run(number):
             rows = pl.ds(pl.multiple_of(first * tile, tile), number * tile)
             shift = first - block + block_count - 1
             bias_rows = pl.ds(pl.multiple_of(shift * tile, tile), number * tile)
-            same = seg_col_ref[0, rows, :] == seg_row_ref[0, :, here]
+            q_code = q_code_ref[0, here, :]
             for pair in range(group):
                 columns = pair_columns(pair)
-                keys = k_ref[0, rows, columns]
                 values = v_ref[0, rows, columns]
                 q_pair = q_ref[0, here, columns]
                 grad_pair = grad_ref[0, here, columns]
@@ -202,8 +211,8 @@
                     grad_half = keep_half(grad_pair, half)
                     picker = half_mask((8, lanes), half).astype(f32)
                     delta = dot_nt(picker, product, precision=highest)[0:1]
-                    scores = dot_nt(keys, q_half) + bias_ref[head, bias_rows, :]
-                    scores = jnp.where(same, scores, -1000000000.0)
+                    q_coded = jnp.where(half_mask(q_pair.shape, half), q_pair, q_code)
+                    scores = dot_nt(coded_ref[head, rows, :], q_coded) + bias_ref[head, bias_rows, :]
                     weights = jnp.exp(scores - lse_ref[0, pair, half : half + 1, here])
                     grad_scores = weights * (dot_nt(values, grad_half) - delta)
                     gbias_ref[head, bias_rows, :] = gbias_ref[head, bias_rows, :] + grad_scores
@@ -238,34 +247,39 @@
             sums_ref[0, head, 4 * side] = wide[0]
 
 
-def block_range(segments, block_count):
-    rows = segments.shape[0]
-    blocks = segments.reshape(rows, block_count, tile)
-    first_seg = blocks[:, :, 0]
-    last_seg = blocks[:, :, tile - 1]
-    first = jnp.sum((last_seg[:, None, :] < first_seg[:, :, None]).astype(jnp.int32), axis=-1)
-    last = jnp.sum((first_seg[:, None, :] <= last_seg[:, :, None]).astype(jnp.int32), axis=-1) - 1
-    return first.reshape(-1), last.reshape(-1)
+def block_range(seg_ref, row, block, block_count):
+    head, tail = block * tile, block * tile + tile - 1
+    first = last = 0
+    for other in range(block_count):
+        ends_before = seg_ref[row, other * tile + tile - 1] < seg_ref[row, head]
+        starts_by = seg_ref[row, other * tile] <= seg_ref[row, tail]
+        first = first + ends_before.astype(jnp.int32)
+        last = last + starts_by.astype(jnp.int32)
+    return first, last - 1
+
+
+def doc_codes(segments):
+    lane = jnp.arange(lanes, dtype=jnp.int32) % (lanes // 2)
+    same = lane == segments[:, :, None]
+    return same.astype(bf16), jnp.where(same, 0.0, -1000000000.0).astype(bf16)
 
 
 def grouping(width, length):
     pairs = width // lanes
     group = group_pairs if pairs % group_pairs == 0 else 1
     whole = pl.BlockSpec((1, length, group * lanes), lambda r, h, *_: (r, 0, h))
-    seg_row = pl.BlockSpec((1, 1, length), lambda r, h, *_: (r, 0, 0))
-    seg_col = pl.BlockSpec((1, length, 1), lambda r, h, *_: (r, 0, 0))
+    code = pl.BlockSpec((1, length, lanes), lambda r, h, *_: (r, 0, 0))
     line = pl.BlockSpec((2 * group, kinds, 2 * tile), lambda r, h, *_: (h, 0, 0))
     total = pl.BlockSpec((1, group, 2, length), lambda r, h, *_: (r, h, 0, 0))
     sums = pl.BlockSpec((1, 2 * group, kinds, 2 * tile), lambda r, h, *_: (r, h, 0, 0))
-    return pairs, group, whole, seg_row, seg_col, line, total, sums
-
-
-def attend(queries, keys, values, segments, lines):
+    return pairs, group, whole, code, line, total, sums
+
+
+def attend(queries, keys, values, segments, codes, lines):
     rows, length, width = queries.shape
     block_count = length // tile
     spans = 2 * block_count - 1
-    first, last = block_range(segments, block_count)
-    pairs, group, whole, seg_row, seg_col, line, total, _ = grouping(width, length)
+    pairs, group, whole, code, line, total, _ = grouping(width, length)
     return pl.pallas_call(
         functools.partial(forward_kernel, block_count),
         out_shape=(
@@ -273,26 +287,26 @@
             jax.ShapeDtypeStruct((rows, pairs, 2, length), f32),
         ),
         grid_spec=pltpu.PrefetchScalarGridSpec(
-            num_scalar_prefetch=2,
+            num_scalar_prefetch=1,
             grid=(rows, pairs // group),
-            in_specs=[whole, whole, whole, seg_row, seg_col, line],
+            in_specs=[whole, whole, whole, code, code, line],
             out_specs=[whole, total],
             scratch_shapes=[
                 pltpu.VMEM((2 * group, spans * tile, tile), f32),
                 pltpu.VMEM((2 * group, lanes, length), bf16),
+                pltpu.VMEM((2 * group, length, lanes), bf16),
             ],
         ),
         cost_estimate=cost(25),
         name="attend",
-    )(first, last, queries, keys, values, segments[:, None, :], segments[:, :, None], lines)
-
-
-def attend_back(queries, keys, values, grad_mixed, mixed, totals, segments, lines):
+    )(segments, queries, keys, values, *codes, lines)
+
+
+def attend_back(queries, keys, values, grad_mixed, mixed, totals, segments, codes, lines):
     rows, length, width = queries.shape
     block_count = length // tile
     spans = 2 * block_count - 1
-    first, last = block_range(segments, block_count)
-    pairs, group, whole, seg_row, seg_col, line, total, sums = grouping(width, length)
+    pairs, group, whole, code, line, total, sums = grouping(width, length)
     shape = jax.ShapeDtypeStruct((rows, length, width), bf16)
     return pl.pallas_call(
         functools.partial(backward_kernel, block_count),
@@ -301,9 +315,9 @@
             jax.ShapeDtypeStruct((rows, 2 * pairs, kinds, 2 * tile), f32),
         ),
         grid_spec=pltpu.PrefetchScalarGridSpec(
-            num_scalar_prefetch=2,
+            num_scalar_prefetch=1,
             grid=(rows, pairs // group),
-            in_specs=[whole, whole, whole, whole, whole, total, seg_row, seg_col, line],
+            in_specs=[whole, whole, whole, whole, whole, total, code, code, line],
             out_specs=[whole, whole, whole, sums],
             scratch_shapes=[
                 pltpu.VMEM((2 * group, spans * tile, tile), f32),
@@ -311,13 +325,13 @@
                 pltpu.VMEM((2 * group, lanes, length), bf16),
                 pltpu.VMEM((length, group * lanes), f32),
                 pltpu.VMEM((length, group * lanes), f32),
+                pltpu.VMEM((2 * group, length, lanes), bf16),
             ],
         ),
         cost_estimate=cost(35),
         name="attend_back",
     )(
-        first, last, queries, keys, values, grad_mixed, mixed, totals,
-        segments[:, None, :], segments[:, :, None], lines,
+        segments, queries, keys, values, grad_mixed, mixed, totals, *codes, lines,
     )
 
 
@@ -1326,7 +1340,7 @@
             *SmallSum.scratch(bits, count, small.shape),
         ],
         compiler_params=pltpu.CompilerParams(
-            collective_id=cid, has_side_effects=True, vmem_limit_bytes=63 * 2**20
+            collective_id=cid, has_side_effects=True, vmem_limit_bytes=67_043_328
         ),
         cost_estimate=cost(20),
         name="tail_sums",
@@ -1451,6 +1465,66 @@
     )(base, ffn, down, query, key, value, out, x, attn_total, ffn_share, input_grad, small_all, small_cube)
 
 
+def hidden_kernel(normed_ref, w_gate_ref, w_up_ref, grad_ref, hidden_out, gate_out, up_out):
+    def rows(index, carry):
+        here = pl.ds(pl.multiple_of(index * 2 * tile, 2 * tile), 2 * tile)
+        left = normed_ref[here, :]
+        gate = dot_nn(left, w_gate_ref[...])
+        up = dot_nn(left, w_up_ref[...])
+        grad_hidden = grad_ref[here, :]
+        square = gate * gate
+        bend = jnp.tanh(gelu_scale * gate * (1.0 + gelu_cubic * square))
+        half = 0.5 * (1.0 + bend)
+        act = gate * half
+        slope = half + 0.5 * gate * (1.0 - bend * bend) * gelu_scale * (
+            1.0 + 3.0 * gelu_cubic * square
+        )
+        hidden_out[here, :] = (act * up).astype(bf16)
+        gate_out[here, :] = (grad_hidden * up * slope).astype(bf16)
+        up_out[here, :] = (grad_hidden * act).astype(bf16)
+        return carry
+
+    lax.fori_loop(0, normed_ref.shape[0] // (2 * tile), rows, 0)
+
+
+def ffn_hidden(normed, w_gate, w_up, grad_hidden):
+    tokens, depth = normed.shape
+    width = w_gate.shape[1]
+    columns = tile if width % tile == 0 else lanes
+    block = pl.BlockSpec((tokens, columns), lambda j: (0, j))
+    weight = pl.BlockSpec((depth, columns), lambda j: (0, j))
+    return pl.pallas_call(
+        hidden_kernel,
+        out_shape=[jax.ShapeDtypeStruct((tokens, width), bf16)] * 3,
+        grid=(width // columns,),
+        in_specs=[pl.BlockSpec((tokens, depth), lambda j: (0, 0)), weight, weight, block],
+        out_specs=[block] * 3,
+        cost_estimate=cost(20),
+        name="ffn_hidden",
+    )(normed, w_gate, w_up, grad_hidden)
+
+
+def ffn_back_kernel(gate_ref, up_ref, w_gate_ref, w_up_ref, out_ref):
+    value = dot_nt(gate_ref[...], w_gate_ref[...]) + dot_nt(up_ref[...], w_up_ref[...])
+    out_ref[...] = value.astype(bf16)
+
+
+def ffn_back(grad_gate, grad_up, w_gate, w_up):
+    tokens, width = grad_gate.shape
+    depth = w_gate.shape[0]
+    whole = pl.BlockSpec((tokens, width), lambda i: (0, 0))
+    weight = pl.BlockSpec((tile, width), lambda i: (i, 0))
+    return pl.pallas_call(
+        ffn_back_kernel,
+        out_shape=jax.ShapeDtypeStruct((tokens, depth), bf16),
+        grid=(depth // tile,),
+        in_specs=[whole, whole, weight, weight],
+        out_specs=pl.BlockSpec((tokens, tile), lambda i: (0, i)),
+        cost_estimate=cost(16),
+        name="ffn_back",
+    )(grad_gate, grad_up, w_gate, w_up)
+
+
 def project(left_side, right_side):
     return jnp.dot(left_side, right_side, preferred_element_type=f32)
 
@@ -1495,34 +1569,30 @@
     onehot = offset_onehot(bucket_count)
     lines = jnp.dot(jnp.transpose(bias_table), onehot, precision=highest)
     lines = lines.reshape(head_count, kinds, 2 * tile)
-    mixed, totals = attend(queries, keys, values, segments, lines)
+    codes = doc_codes(segments)
+    mixed, totals = attend(queries, keys, values, segments, codes, lines)
     mixed_flat = mixed.reshape(token_count, local_width)
     attn_part = project(mixed_flat, w_out)
     attn_total, normed_ffn, grad_hidden, normed_t, mixed_t = enter_ffn(
         attn_part.astype(bf16), low_inputs, grad_out, w_down, normed, mixed_flat,
         gain_ffn, "tensor", line_chunks, 0,
     )
-    gate_pre = project(normed_ffn, w_gate)
-    up_pre = project(normed_ffn, w_up)
-    act_value, act_pull = jax.vjp(lambda signal: jax.nn.gelu(signal, approximate=True), gate_pre)
-    hidden = (act_value * up_pre).astype(bf16)
-    grad_gate = act_pull(grad_hidden * up_pre)[0].astype(bf16)
-    grad_up = (grad_hidden * act_value).astype(bf16)
+    hidden, grad_gate, grad_up = ffn_hidden(normed_ffn, w_gate, w_up, grad_hidden)
     down = lax.dot_general(
         hidden, grad_out, (((0,), (0,)), ((), ())), preferred_element_type=f32
     ).astype(bf16)
     grad_gate, grad_up, down = lax.optimization_barrier((grad_gate, grad_up, down))
     down = lax.psum(down, "dp")
-    norm_ffn_part = project_back(grad_gate, w_gate) + project_back(grad_up, w_up)
+    norm_ffn_part = ffn_back(grad_gate, grad_up, w_gate, w_up)
     grad_branch, ffn_part, ffn_grad, grad_middle_share, gain_ffn_part = leave_ffn(
-        norm_ffn_part.astype(bf16), low_inputs, attn_total, grad_out, hidden, w_down, normed_ffn,
+        norm_ffn_part, low_inputs, attn_total, grad_out, hidden, w_down, normed_ffn,
         grad_gate, grad_up, gain_ffn, "tensor", line_chunks, 1,
     )
     ffn_grad, down, grad_branch = lax.optimization_barrier((ffn_grad, down, grad_branch))
     ffn_grad = lax.psum(ffn_grad, "dp")
     grad_mixed = project_back(grad_branch, w_out).astype(bf16).reshape(heads_shape)
     grad_query, grad_key, grad_value, sums = attend_back(
-        queries, keys, values, grad_mixed, mixed, totals, segments, lines
+        queries, keys, values, grad_mixed, mixed, totals, segments, codes, lines
     )
     grad_query = grad_query.reshape(token_count, local_width)
     grad_key = grad_key.reshape(token_count, local_width)

time: 602 us -> 592 us (0.983)
  matrix products: 71.9 us -> 32.1 us
  Pallas kernels: 491 us -> 526 us
    pallas_call x0 -> x2, Pallas kernels: none -> 36.5 us  [the longest x1 20.1 us: ffn_hidden(): pl.pallas_call(hidden_kernel, out_shape=[jax.ShapeDtypeStruct((tokens, wi...]
    dot_general x6 -> x4, matrix products: 38.8 us -> 15.5 us  [project(): return jnp.dot(left_side, right_side, preferred_element_type=f32)]
    dot_general x3 -> x1, matrix products: 25.4 us -> 6.2 us  [dot_nt(): lax.dot_general(left_side, right_side, (((1,), (1,)), ((), ())), preferre...]
  transfers between devices with their start and end apart: 2 -> 2, of which waited for: 0 -> 0; matrix products, arithmetic and copies ran while one was open for 4% -> 1% of each run, Pallas kernels for 55% -> 58%
where the time goes in v6:
time: 592 us; the launch traced here: 585 us
  Pallas kernels  526 us (89%)
  matrix products  32.1 us (5%)
  between operations  14.5 us (2%)
  other arithmetic  7.64 us (1%)
    pallas_call x1, Pallas kernels, tail_sums(): pl.pallas_call(functools.partial(tail_kernel, line_axis, count, subs, cub...  168 us
    pallas_call x1, Pallas kernels, leave_ffn(): pl.pallas_call(functools.partial(leave_kernel, axis, count, chunks), out_...  119 us
    pallas_call x1, Pallas kernels, enter_ffn(): pl.pallas_call(functools.partial(enter_kernel, axis, count, chunks), out_...  112 us
    pallas_call x1, Pallas kernels, attend_back(): pl.pallas_call(functools.partial(backward_kernel, block_count), out_shape...  35.3 us
    pallas_call x1, Pallas kernels, widen(): pl.pallas_call(lambda base, *refs: widen_kernel(*refs), out_shape=(jax.Sh...  28.1 us
    pallas_call x1, Pallas kernels, attend(): pl.pallas_call(functools.partial(forward_kernel, block_count), out_shape=...  26.6 us
    pallas_call x1, Pallas kernels, ffn_hidden(): pl.pallas_call(hidden_kernel, out_shape=[jax.ShapeDtypeStruct((tokens, wi...  20.1 us
    pallas_call x1, Pallas kernels, ffn_back(): pl.pallas_call(ffn_back_kernel, out_shape=jax.ShapeDtypeStruct((tokens, d...  16.4 us
  transfers between devices with their start and end apart: 2, of which 0 were waited for; matrix products, arithmetic and copies ran while one was open for 1% of the time, Pallas kernels for 58%

profile of v6, /device:TPU:17, one launch (start us, length us, event | category | flops | bytes accessed | tf_op | source)
XLA Modules:
  0.0 585.3 jit_solution(364203596755649519)
XLA Ops:
  7.2 0.0 copy-start.4
  7.2 0.0 all-reduce.5.cloned.1.call-start
  7.2 0.0 copy-start
  7.3 1.7 compare_convert_fusion.q_code_ref
  9.0 1.6 fusion.7.k_code_ref
  10.6 3.1 fusion
  13.7 0.0 copy-done.4
  13.7 0.0 copy-done
  13.7 0.0 copy-start.8
  13.7 1.0 fusion.2.first_hbm
  14.8 0.5 copy-done.8
  15.3 0.0 copy-start.1
  15.3 0.0 copy-start.9
  15.3 3.3 fusion.3.q_ref
  18.6 0.0 copy-done.9
  18.6 0.0 copy-start.10
  18.6 3.3 fusion.4.k_ref
  21.9 0.0 copy-done.1
  21.9 0.0 copy-done.10
  21.9 0.0 copy-start.6
  21.9 3.3 fusion.5.v_ref
  25.2 0.1 subtract_abs_fusion
  25.3 0.0 copy-start.2
  25.4 0.6 copy-done.2
  25.9 0.0 copy-done.6
  25.9 0.2 fusion.9
  26.2 0.7 copy.26.line_ref
  26.9 0.0 copy-start.7
  26.9 26.6 %attend.1 = (bf16[1,1024,512]{2,1,0:T(8,128)(2,1)}, f32[1,4,2,1024]{3,2,1,0:T(2,128)}) custom-call(s32[1,1024]{1,0:T(1,128)} %seg_ref.3, bf16[1,1024,512]{2,1,0:T(8,128)(2,1)} %fusion.3.q_ref, bf16[1,1024,512]{2,1,0:T(8,128)(2,1)} %fusion.4.k_ref, bf16[1,1024,512]{2,1,0:T(8,128)(2,1)} %fusion.5.v_ref, bf16[1,1024,128]{2,1,0:T(8,128)(2,1)} %compare_convert_fusion.q_code_ref, ...), custom_call_target="tpu_custom_call" | custom-call | flops 24999999488 | bytes 1000000 | tf_op jit(solution)/shard_map/attend/pallas_call | solution.py:283
  53.5 0.0 copy-done.7
  53.5 5.6 convolution_convert_fusion.1.part_hbm
  59.1 111.7 %enter_ffn.1 = (bf16[1024,2048]{1,0:T(8,128)(2,1)}, bf16[1024,2048]{1,0:T(8,128)(2,1)}, f32[1024,1280]{1,0:T(8,128)}, bf16[2048,1024]{1,0:T(8,128)(2,1)}, bf16[512,1024]{1,0:T(8,128)(2,1)}) custom-call(bf16[1024,2048]{1,0:T(8,128)(2,1)} %convolution_convert_fusion.1.part_hbm, bf16[1024,2048]{1,0:T(8,128)(2,1)} %bitcast.48, bf16[1024,2048]{1,0:T(8,128)(2,1)} %bitcast.58, ...), custom_call_target="tpu_custom_call" | custom-call | flops 109999996928 | bytes 1000000 | tf_op jit(solution)/shard_map/enter_ffn/pallas_call | solution.py:949
  170.8 20.1 %ffn_hidden.1 = (bf16[1024,1280]{1,0:T(8,128)(2,1)}, bf16[1024,1280]{1,0:T(8,128)(2,1)}, bf16[1024,1280]{1,0:T(8,128)(2,1)}) custom-call(bf16[1024,2048]{1,0:T(8,128)(2,1)} %get-tuple-element.57.normed_ref.normed_hbm, bf16[2048,1280]{1,0:T(8,128)(2,1)} %w_gate_ref.3, bf16[2048,1280]{1,0:T(8,128)(2,1)} %w_up_ref.3, f32[1024,1280]{1,0:T(8,128)} %get-tuple-element.58.grad_ref), custom_call_target="tpu_custom_call" | custom-call | flops 20000000000 | bytes 1000000 | tf_op jit(solution)/shard_map/ffn_hidden/pallas_call | solution.py:1496
  190.9 9.9 %convolution_convert_fusion = bf16[1280,2048]{1,0:T(8,128)(2,1)} fusion(bf16[1024,1280]{1,0:T(8,128)(2,1)} %get-tuple-element.61.hidden_hbm, bf16[1,1024,2048]{2,1,0:T(8,128)(2,1)} %param.15), kind=kOutput, calls=%fused_computation.5 | convolution fusion | flops 5371330560 | bytes 12058624 | tf_op jit(solution)/shard_map/dot_general | solution.py:1581
  200.8 0.0 all-reduce.5.cloned.1.call-update
  200.8 0.0 all-reduce.7.cloned.1.call-start
  200.9 16.4 %ffn_back.1.part_hbm = bf16[1024,2048]{1,0:T(8,128)(2,1)} custom-call(bf16[1024,1280]{1,0:T(8,128)(2,1)} %get-tuple-element.62.gate_ref.gate_hbm, bf16[1024,1280]{1,0:T(8,128)(2,1)} %get-tuple-element.63.up_ref.up_hbm, bf16[2048,1280]{1,0:T(8,128)(2,1)} %w_gate_ref.3, bf16[2048,1280]{1,0:T(8,128)(2,1)} %w_up_ref.3), custom_call_target="tpu_custom_call" | custom-call | flops 16000000000 | bytes 1000000 | tf_op jit(solution)/shard_map/ffn_back/pallas_call | solution.py:1517
  217.3 119.4 %leave_ffn.1 = (bf16[1024,2048]{1,0:T(8,128)(2,1)}, bf16[1024,2048]{1,0:T(8,128)(2,1)}, bf16[2048,2560]{1,0:T(8,128)(2,1)}, f32[256,2048]{1,0:T(8,128)}, f32[1,2048]{1,0:T(1,128)}) custom-call(bf16[1024,2048]{1,0:T(8,128)(2,1)} %ffn_back.1.part_hbm, bf16[1024,2048]{1,0:T(8,128)(2,1)} %bitcast.49, bf16[1024,2048]{1,0:T(8,128)(2,1)} %get-tuple-element.64.attn_hbm.refs_7_, ...), custom_call_target="tpu_custom_call" | custom-call | flops 109999996928 | bytes 1000000 | tf_op jit(solution)/shard_map/leave_ffn/pallas_call | solution.py:1047
  336.7 0.0 all-reduce.5.cloned.1.call-done.refs_1_
  336.8 6.2 %fusion.6.grad_ref = bf16[1,1024,512]{2,1,0:T(8,128)(2,1)} fusion(bf16[1024,2048]{1,0:T(8,128)(2,1)} %get-tuple-element.70.branch_hbm, bf16[512,2048]{1,0:T(8,128)(2,1)} %param.19), kind=kOutput, calls=%fused_computation.14 | convolution fusion | flops 2148007936 | bytes 7340032 | tf_op jit(solution)/shard_map/dot_general | solution.py:51
  343.0 0.0 all-reduce.7.cloned.1.call-update
  343.0 0.0 copy-start.3
  343.0 0.0 copy-start.5
  343.0 35.3 %attend_back.1 = (bf16[1,1024,512]{2,1,0:T(8,128)(2,1)}, bf16[1,1024,512]{2,1,0:T(8,128)(2,1)}, bf16[1,1024,512]{2,1,0:T(8,128)(2,1)}, f32[1,8,5,512]{3,2,1,0:T(8,128)}) custom-call(s32[1,1024]{1,0:T(1,128)} %seg_ref.3, bf16[1,1024,512]{2,1,0:T(8,128)(2,1)} %fusion.3.q_ref, bf16[1,1024,512]{2,1,0:T(8,128)(2,1)} %fusion.4.k_ref, ...), custom_call_target="tpu_custom_call" | custom-call | flops 35000000512 | bytes 1000000 | tf_op jit(solution)/shard_map/attend_back/pallas_call | solution.py:311
  378.3 1.0 copy.31
  379.3 0.0 copy-done.3
  379.3 0.2 fusion.8
  379.5 0.1 reshape.267
  379.6 0.0 copy-done.5
  379.7 0.1 pad_maximum_fusion
  379.7 0.6 pad.9.small_ref
  380.4 168.2 %tail_sums.1 = (bf16[256,2048]{1,0:T(8,128)(2,1)}, bf16[256,2048]{1,0:T(8,128)(2,1)}, f32[8,2048]{1,0:T(8,128)}, f32[8,2048]{1,0:T(8,128)}, bf16[2048,512]{1,0:T...) custom-call(bf16[1024,512]{1,0:T(8,128)(2,1)} %bitcast.63, ...), custom_call_target="tpu_custom_call" | custom-call | flops 20000000000 | bytes 1000000 | tf_op jit(solution)/shard_map/tail_sums/pallas_call | solution.py:1309
  548.6 0.7 slice_reduce_fusion
  549.3 0.1 reshape_squeeze.3
  549.4 0.7 copy.29
  550.1 0.0 all-reduce.7.cloned.1.call-done.refs_0_
  550.1 28.1 %widen.1 = (f32[2048,1280]{1,0:T(8,128)}, f32[2048,1280]{1,0:T(8,128)}, f32[1280,2048]{1,0:T(8,128)}, f32[2048,512]{1,0:T(8,128)}, f32[2048,512]{1,0:T(8,128)}, ...) custom-call(s32[1]{0:T(128)} %bitcast.base, ...), custom_call_target="tpu_custom_call" | custom-call | flops 25999998976 | bytes 1000000 | tf_op jit(solution)/shard_map/widen/pallas_call | solution.py:1438
  (9 shorter events, 0.1 us)
Async XLA Ops:
  7.2 6.5 %copy-start.4 = (f32[2048]{0:T(1024)S(1)}, f32[2048]{0:T(1024)}, u32[]{:S(2)}) copy-start(f32[2048]{0:T(1024)} %param.23) | copy-start | bytes 24580
  7.2 329.6 %all-reduce.5.cloned.1.call-start = ((), (), s32[]{:S(2)}) async-start(), calls=%async_computation | async-start | bytes 10485760 | tf_op jit(solution)/shard_map/psum | solution.py:1585
  7.2 6.5 %copy-start = (bf16[1,1024,2048]{2,1,0:T(8,128)(2,1)S(1)}, bf16[1,1024,2048]{2,1,0:T(8,128)(2,1)}, u32[]{:S(2)}) copy-start(bf16[1,1024,2048]{2,1,0:T(8,128)(2,1)} %param.13) | copy-start | bytes 12582916
  13.7 1.6 copy-start.8
  15.3 6.6 %copy-start.1 = (bf16[1024,2048]{1,0:T(8,128)(2,1)}, bf16[1024,2048]{1,0:T(8,128)(2,1)S(1)}, u32[]{:S(2)}) copy-start(bf16[1024,2048]{1,0:T(8,128)(2,1)S(1)} %fusion.2.first_hbm) | copy-start | bytes 12582916
  15.3 3.3 copy-start.9
  18.6 3.3 copy-start.10
  21.9 4.0 copy-start.6
  25.3 0.6 copy-start.2
  26.9 26.6 %copy-start.7 = (bf16[512,2048]{1,0:T(8,128)(2,1)S(1)}, bf16[512,2048]{1,0:T(8,128)(2,1)}, u32[]{:S(2)}) copy-start(bf16[512,2048]{1,0:T(8,128)(2,1)} %param.19) | copy-start | bytes 6291460
  200.8 349.3 %all-reduce.7.cloned.1.call-start = ((), (), s32[]{:S(2)}) async-start(), calls=%async_computation.1 | async-start | bytes 20971520 | tf_op jit(solution)/shard_map/psum | solution.py:1592
  343.0 36.3 %copy-start.3 = (s32[2560]{0:T(1024)S(1)}, s32[2560]{0:T(1024)}, u32[]{:S(2)}) copy-start(s32[2560]{0:T(1024)} %copy-done.2) | copy-start | bytes 30724
  343.0 36.6 %copy-start.5 = (f32[1,2048]{1,0:T(1,128)S(1)}, f32[1,2048]{1,0:T(1,128)}, u32[]{:S(2)}) copy-start(f32[1,2048]{1,0:T(1,128)} %get-tuple-element.79) | copy-start | bytes 24580
Sparse Core Ops, SparseCore 0:
  201.0 95.3 all-reduce.4
  343.1 206.9 all-reduce.6

commit v7 on v6

--- a/solution.py
+++ b/solution.py
@@ -89,6 +89,30 @@
     return line
 
 
+def unskew_corner(part, near):
+    group, rows = 8, 96
+    top = 0 if near > 0 else tile - rows
+    left = lanes if near > 0 else 0
+    corner = part[top : top + rows, left : left + lanes]
+    other = part[rows:] if near > 0 else part[: tile - rows]
+    beside = part[top : top + rows, lanes - left : tile - left]
+    rest = jnp.sum(other, axis=0, keepdims=True)
+    rest = rest[:, :lanes] + rest[:, lanes:] + jnp.sum(beside, axis=0, keepdims=True)
+    gathered = jnp.zeros((group, tile), f32)
+    for start in range(0, rows, group):
+        piece = corner[start : start + group]
+        wide = jnp.concatenate([piece, jnp.zeros_like(piece)], axis=1)
+        gathered = gathered + pltpu.roll(wide, (left if near > 0 else rows) - start, 1)
+    line = gathered[0:1]
+    for shift in range(1, group):
+        line = line + pltpu.roll(gathered[shift : shift + 1], tile - shift, 1)
+    place = lax.broadcasted_iota(jnp.int32, line.shape, 1)
+    edge = 0 if near > 0 else tile - 1
+    line = line + jnp.where(place == edge, jnp.sum(rest, axis=1, keepdims=True), 0.0)
+    blank = jnp.zeros_like(line)
+    return jnp.concatenate([blank, line] if near > 0 else [line, blank], axis=1)
+
+
 def half_mask(shape, half):
     lane = lax.broadcasted_iota(jnp.int32, shape, len(shape) - 1)
     return (lane < lanes // 2) if half == 0 else (lane >= lanes // 2)
@@ -107,17 +131,16 @@
     return slice(pair * lanes, (pair + 1) * lanes)
 
 
-def code_keys(group, k_ref, k_code_ref, coded_ref):
+def code_keys(group, k_ref, code_ref, coded_ref):
+    k_code = ((code_ref[0].astype(f32) - 1.0) * 1000000000.0).astype(bf16)
     for pair in range(group):
         keys = k_ref[0, :, pair_columns(pair)]
         for half in range(2):
-            coded_ref[2 * pair + half] = jnp.where(
-                half_mask(keys.shape, half), keys, k_code_ref[0]
-            )
+            coded_ref[2 * pair + half] = jnp.where(half_mask(keys.shape, half), keys, k_code)
 
 
 def forward_kernel(
-    block_count, seg_ref, q_ref, k_ref, v_ref, q_code_ref, k_code_ref, line_ref,
+    block_count, seg_ref, q_ref, k_ref, v_ref, q_code_ref, line_ref,
     out_ref, lse_ref, bias_ref, vt_ref, coded_ref,
 ):
     row = pl.program_id(0)
@@ -130,7 +153,7 @@
         ones = jnp.ones_like(values_t)
         vt_ref[2 * pair] = jnp.where(place < mid, values_t, ones)
         vt_ref[2 * pair + 1] = jnp.where(place < mid, ones, values_t)
-    code_keys(group, k_ref, k_code_ref, coded_ref)
+    code_keys(group, k_ref, q_code_ref, coded_ref)
 
     @pl.loop(0, block_count)
     def _(block):
@@ -168,7 +191,7 @@
 
 
 def backward_kernel(
-    block_count, seg_ref, q_ref, k_ref, v_ref, grad_ref, out_ref, lse_ref, q_code_ref, k_code_ref,
+    block_count, seg_ref, q_ref, k_ref, v_ref, grad_ref, out_ref, lse_ref, q_code_ref,
     line_ref, dq_ref, dk_ref, dv_ref, sums_ref,
     bias_ref, gbias_ref, kt_ref, dk_acc, dv_acc, coded_ref,
 ):
@@ -183,7 +206,7 @@
         zeros = jnp.zeros_like(keys_t)
         kt_ref[2 * pair] = jnp.where(place < mid, keys_t, zeros)
         kt_ref[2 * pair + 1] = jnp.where(place < mid, zeros, keys_t)
-    code_keys(group, k_ref, k_code_ref, coded_ref)
+    code_keys(group, k_ref, q_code_ref, coded_ref)
     gbias_ref[...] = jnp.zeros_like(gbias_ref)
     dk_acc[...] = jnp.zeros_like(dk_acc)
     dv_acc[...] = jnp.zeros_like(dv_acc)
@@ -240,7 +263,8 @@
                 side = 0 if near < 0 else 1
                 far[side] = part if far[side] is None else far[side] + part
             else:
-                sums_ref[0, head, near + 2] = unskew(part)[0]
+                line = unskew(part) if near == 0 else unskew_corner(part, near)
+                sums_ref[0, head, near + 2] = line[0]
         for side in range(2):
             wide = jnp.sum(far[side], axis=0, keepdims=True)
             wide = jnp.concatenate([wide, jnp.zeros_like(wide)], axis=1)
@@ -261,7 +285,7 @@
 def doc_codes(segments):
     lane = jnp.arange(lanes, dtype=jnp.int32) % (lanes // 2)
     same = lane == segments[:, :, None]
-    return same.astype(bf16), jnp.where(same, 0.0, -1000000000.0).astype(bf16)
+    return same.astype(bf16)
 
 
 def grouping(width, length):
@@ -289,7 +313,7 @@
         grid_spec=pltpu.PrefetchScalarGridSpec(
             num_scalar_prefetch=1,
             grid=(rows, pairs // group),
-            in_specs=[whole, whole, whole, code, code, line],
+            in_specs=[whole, whole, whole, code, line],
             out_specs=[whole, total],
             scratch_shapes=[
                 pltpu.VMEM((2 * group, spans * tile, tile), f32),
@@ -299,7 +323,7 @@
         ),
         cost_estimate=cost(25),
         name="attend",
-    )(segments, queries, keys, values, *codes, lines)
+    )(segments, queries, keys, values, codes, lines)
 
 
 def attend_back(queries, keys, values, grad_mixed, mixed, totals, segments, codes, lines):
@@ -317,7 +341,7 @@
         grid_spec=pltpu.PrefetchScalarGridSpec(
             num_scalar_prefetch=1,
             grid=(rows, pairs // group),
-            in_specs=[whole, whole, whole, whole, whole, total, code, code, line],
+            in_specs=[whole, whole, whole, whole, whole, total, code, line],
             out_specs=[whole, whole, whole, sums],
             scratch_shapes=[
                 pltpu.VMEM((2 * group, spans * tile, tile), f32),
@@ -331,7 +355,7 @@
         cost_estimate=cost(35),
         name="attend_back",
     )(
-        segments, queries, keys, values, grad_mixed, mixed, totals, *codes, lines,
+        segments, queries, keys, values, grad_mixed, mixed, totals, codes, lines,
     )
 
 
@@ -1420,13 +1444,13 @@
 def widen(ffn, down, query, key, value, out, x, attn_total, ffn_share, input_grad, small_all, small_cube, axis):
     width, depth = down.shape
     local = query.shape[1]
-    steps = depth // lanes
+    steps = depth // tile
     share = ffn_share.shape[0]
     piece = share // steps
     base = (lax.axis_index(axis) * steps).astype(jnp.int32).reshape(1)
 
     def rows(columns):
-        return pl.BlockSpec((lanes, columns), lambda i, base: (i, 0))
+        return pl.BlockSpec((tile, columns), lambda i, base: (i, 0))
 
     out_rows = pl.BlockSpec((local // steps, depth), lambda i, base: (i, 0))
     down_rows = pl.BlockSpec((width // steps, depth), lambda i, base: (i, 0))

time: 592 us -> 588 us (level)
    pallas_call x1, Pallas kernels: 168 us -> 177 us  [tail_sums(): pl.pallas_call(functools.partial(tail_kernel, line_axis, count, subs, cub...]
  transfers between devices with their start and end apart: 2 -> 2, of which waited for: 0 -> 1; matrix products, arithmetic and copies ran while one was open for 1% -> 1% of each run, Pallas kernels for 58% -> 59%
where the time goes in v7:
time: 588 us; the launch traced here: 581 us
  Pallas kernels  524 us (89%)
  matrix products  32.1 us (5%)
  between operations  14.5 us (2%)
    pallas_call x1, Pallas kernels, tail_sums(): pl.pallas_call(functools.partial(tail_kernel, line_axis, count, subs, cub...  177 us
    pallas_call x1, Pallas kernels, leave_ffn(): pl.pallas_call(functools.partial(leave_kernel, axis, count, chunks), out_...  119 us
    pallas_call x1, Pallas kernels, enter_ffn(): pl.pallas_call(functools.partial(enter_kernel, axis, count, chunks), out_...  112 us
    pallas_call x1, Pallas kernels, attend_back(): pl.pallas_call(functools.partial(backward_kernel, block_count), out_shape...  29.9 us
    pallas_call x1, Pallas kernels, widen(): pl.pallas_call(lambda base, *refs: widen_kernel(*refs), out_shape=(jax.Sh...  27.2 us
    pallas_call x1, Pallas kernels, attend(): pl.pallas_call(functools.partial(forward_kernel, block_count), out_shape=...  22.9 us
    pallas_call x1, Pallas kernels, ffn_hidden(): pl.pallas_call(hidden_kernel, out_shape=[jax.ShapeDtypeStruct((tokens, wi...  20.1 us
    pallas_call x1, Pallas kernels, ffn_back(): pl.pallas_call(ffn_back_kernel, out_shape=jax.ShapeDtypeStruct((tokens, d...  16.6 us
  transfers between devices with their start and end apart: 2, of which 1 were waited for; matrix products, arithmetic and copies ran while one was open for 1% of the time, Pallas kernels for 59%

profile of v7, /device:TPU:17, one launch (start us, length us, event | category | flops | bytes accessed | tf_op | source)
XLA Modules:
  0.0 581.3 jit_solution(18444887262371616229)
XLA Ops:
  7.2 0.0 copy-start.4
  7.2 0.0 all-reduce.5.cloned.1.call-start
  7.2 0.0 copy-start
  7.3 3.2 fusion
  10.5 0.0 copy-done.4
  10.5 0.2 copy-done
  10.7 0.0 copy-start.9
  10.7 1.0 fusion.2.first_hbm
  11.7 0.6 copy-done.9
  12.3 0.0 copy-start.1
  12.3 0.0 copy-start.10
  12.3 3.3 fusion.3.q_ref
  15.6 0.0 copy-done.10
  15.6 0.0 copy-start.11
  15.6 3.3 fusion.4.k_ref
  18.9 0.0 copy-done.1
  18.9 0.0 copy-done.11
  18.9 0.0 copy-start.7
  18.9 0.0 copy-start.6
  18.9 3.3 fusion.5.v_ref
  22.2 0.1 subtract_abs_fusion
  22.3 0.0 copy-done.7
  22.3 0.0 copy-start.2
  22.3 0.2 fusion.8
  22.6 0.7 copy.26.line_ref
  23.3 0.0 copy-done.2
  23.3 0.0 copy-done.6
  23.3 0.9 compare_convert_fusion.q_code_ref
  24.2 0.0 copy-start.8
  24.2 22.9 %attend.1 = (bf16[1,1024,512]{2,1,0:T(8,128)(2,1)}, f32[1,4,2,1024]{3,2,1,0:T(2,128)}) custom-call(s32[1,1024]{1,0:T(1,128)} %seg_ref.3, bf16[1,1024,512]{2,1,0:T(8,128)(2,1)} %fusion.3.q_ref, bf16[1,1024,512]{2,1,0:T(8,128)(2,1)} %fusion.4.k_ref, bf16[1,1024,512]{2,1,0:T(8,128)(2,1)} %fusion.5.v_ref, bf16[1,1024,128]{2,1,0:T(8,128)(2,1)} %compare_convert_fusion.q_code_ref, ...), custom_call_target="tpu_custom_call" | custom-call | flops 24999999488 | bytes 1000000 | tf_op jit(solution)/shard_map/attend/pallas_call | solution.py:307
  47.1 0.0 copy-done.8
  47.1 5.6 convolution_convert_fusion.1.part_hbm
  52.7 111.7 %enter_ffn.1 = (bf16[1024,2048]{1,0:T(8,128)(2,1)}, bf16[1024,2048]{1,0:T(8,128)(2,1)}, f32[1024,1280]{1,0:T(8,128)}, bf16[2048,1024]{1,0:T(8,128)(2,1)}, bf16[512,1024]{1,0:T(8,128)(2,1)}) custom-call(bf16[1024,2048]{1,0:T(8,128)(2,1)} %convolution_convert_fusion.1.part_hbm, bf16[1024,2048]{1,0:T(8,128)(2,1)} %bitcast.48, bf16[1024,2048]{1,0:T(8,128)(2,1)} %bitcast.57, ...), custom_call_target="tpu_custom_call" | custom-call | flops 109999996928 | bytes 1000000 | tf_op jit(solution)/shard_map/enter_ffn/pallas_call | solution.py:973
  164.4 20.1 %ffn_hidden.1 = (bf16[1024,1280]{1,0:T(8,128)(2,1)}, bf16[1024,1280]{1,0:T(8,128)(2,1)}, bf16[1024,1280]{1,0:T(8,128)(2,1)}) custom-call(bf16[1024,2048]{1,0:T(8,128)(2,1)} %get-tuple-element.57.normed_ref.normed_hbm, bf16[2048,1280]{1,0:T(8,128)(2,1)} %w_gate_ref.3, bf16[2048,1280]{1,0:T(8,128)(2,1)} %w_up_ref.3, f32[1024,1280]{1,0:T(8,128)} %get-tuple-element.58.grad_ref), custom_call_target="tpu_custom_call" | custom-call | flops 20000000000 | bytes 1000000 | tf_op jit(solution)/shard_map/ffn_hidden/pallas_call | solution.py:1520
  184.5 9.9 %convolution_convert_fusion = bf16[1280,2048]{1,0:T(8,128)(2,1)} fusion(bf16[1024,1280]{1,0:T(8,128)(2,1)} %get-tuple-element.61.hidden_hbm, bf16[1,1024,2048]{2,1,0:T(8,128)(2,1)} %param.15), kind=kOutput, calls=%fused_computation.5 | convolution fusion | flops 5371330560 | bytes 12058624 | tf_op jit(solution)/shard_map/dot_general | solution.py:1605
  194.4 0.0 all-reduce.5.cloned.1.call-update
  194.5 0.0 all-reduce.7.cloned.1.call-start
  194.5 16.6 %ffn_back.1.part_hbm = bf16[1024,2048]{1,0:T(8,128)(2,1)} custom-call(bf16[1024,1280]{1,0:T(8,128)(2,1)} %get-tuple-element.62.gate_ref.gate_hbm, bf16[1024,1280]{1,0:T(8,128)(2,1)} %get-tuple-element.63.up_ref.up_hbm, bf16[2048,1280]{1,0:T(8,128)(2,1)} %w_gate_ref.3, bf16[2048,1280]{1,0:T(8,128)(2,1)} %w_up_ref.3), custom_call_target="tpu_custom_call" | custom-call | flops 16000000000 | bytes 1000000 | tf_op jit(solution)/shard_map/ffn_back/pallas_call | solution.py:1541
  211.1 119.4 %leave_ffn.1 = (bf16[1024,2048]{1,0:T(8,128)(2,1)}, bf16[1024,2048]{1,0:T(8,128)(2,1)}, bf16[2048,2560]{1,0:T(8,128)(2,1)}, f32[256,2048]{1,0:T(8,128)}, f32[1,2048]{1,0:T(1,128)}) custom-call(bf16[1024,2048]{1,0:T(8,128)(2,1)} %ffn_back.1.part_hbm, bf16[1024,2048]{1,0:T(8,128)(2,1)} %bitcast.49, bf16[1024,2048]{1,0:T(8,128)(2,1)} %get-tuple-element.64.attn_hbm.refs_7_, ...), custom_call_target="tpu_custom_call" | custom-call | flops 109999996928 | bytes 1000000 | tf_op jit(solution)/shard_map/leave_ffn/pallas_call | solution.py:1071
  330.5 0.0 all-reduce.5.cloned.1.call-done.refs_1_
  330.5 6.2 %fusion.6.grad_ref = bf16[1,1024,512]{2,1,0:T(8,128)(2,1)} fusion(bf16[1024,2048]{1,0:T(8,128)(2,1)} %get-tuple-element.70.branch_hbm, bf16[512,2048]{1,0:T(8,128)(2,1)} %param.19), kind=kOutput, calls=%fused_computation.14 | convolution fusion | flops 2148007936 | bytes 7340032 | tf_op jit(solution)/shard_map/dot_general | solution.py:51
  336.7 0.0 all-reduce.7.cloned.1.call-update
  336.8 0.0 copy-start.3
  336.8 0.0 copy-start.5
  336.8 29.9 %attend_back.1 = (bf16[1,1024,512]{2,1,0:T(8,128)(2,1)}, bf16[1,1024,512]{2,1,0:T(8,128)(2,1)}, bf16[1,1024,512]{2,1,0:T(8,128)(2,1)}, f32[1,8,5,512]{3,2,1,0:T(8,128)}) custom-call(s32[1,1024]{1,0:T(1,128)} %seg_ref.3, bf16[1,1024,512]{2,1,0:T(8,128)(2,1)} %fusion.3.q_ref, bf16[1,1024,512]{2,1,0:T(8,128)(2,1)} %fusion.4.k_ref, ...), custom_call_target="tpu_custom_call" | custom-call | flops 35000000512 | bytes 1000000 | tf_op jit(solution)/shard_map/attend_back/pallas_call | solution.py:335
  366.7 1.0 copy.31
  367.6 0.0 copy-done.3
  367.7 0.2 fusion.7
  367.9 0.1 reshape.214
  368.0 0.0 copy-done.5
  368.0 0.1 pad_maximum_fusion
  368.1 0.6 pad.9.small_ref
  368.8 176.5 %tail_sums.1 = (bf16[256,2048]{1,0:T(8,128)(2,1)}, bf16[256,2048]{1,0:T(8,128)(2,1)}, f32[8,2048]{1,0:T(8,128)}, f32[8,2048]{1,0:T(8,128)}, bf16[2048,512]{1,0:T...) custom-call(bf16[1024,512]{1,0:T(8,128)(2,1)} %bitcast.62, ...), custom_call_target="tpu_custom_call" | custom-call | flops 20000000000 | bytes 1000000 | tf_op jit(solution)/shard_map/tail_sums/pallas_call | solution.py:1333
  545.3 0.7 slice_reduce_fusion
  546.0 0.1 reshape_squeeze.3
  546.1 0.7 copy.29
  546.8 0.2 all-reduce.7.cloned.1.call-done.refs_0_
  547.0 27.2 %widen.1 = (f32[2048,1280]{1,0:T(8,128)}, f32[2048,1280]{1,0:T(8,128)}, f32[1280,2048]{1,0:T(8,128)}, f32[2048,512]{1,0:T(8,128)}, f32[2048,512]{1,0:T(8,128)}, ...) custom-call(s32[1]{0:T(128)} %bitcast.base, ...), custom_call_target="tpu_custom_call" | custom-call | flops 25999998976 | bytes 1000000 | tf_op jit(solution)/shard_map/widen/pallas_call | solution.py:1462
  (9 shorter events, 0.1 us)
Async XLA Ops:
  7.2 3.3 copy-start.4
  7.2 323.3 %all-reduce.5.cloned.1.call-start = ((), (), s32[]{:S(2)}) async-start(), calls=%async_computation | async-start | bytes 10485760 | tf_op jit(solution)/shard_map/psum | solution.py:1609
  7.2 3.5 copy-start
  10.7 1.6 copy-start.9
  12.3 6.6 %copy-start.1 = (bf16[1024,2048]{1,0:T(8,128)(2,1)}, bf16[1024,2048]{1,0:T(8,128)(2,1)S(1)}, u32[]{:S(2)}) copy-start(bf16[1024,2048]{1,0:T(8,128)(2,1)S(1)} %fusion.2.first_hbm) | copy-start | bytes 12582916
  12.3 3.3 copy-start.10
  15.6 3.3 copy-start.11
  18.9 3.4 copy-start.7
  18.9 4.4 copy-start.6
  22.3 0.9 copy-start.2
  24.2 22.9 %copy-start.8 = (bf16[512,2048]{1,0:T(8,128)(2,1)S(1)}, bf16[512,2048]{1,0:T(8,128)(2,1)}, u32[]{:S(2)}) copy-start(bf16[512,2048]{1,0:T(8,128)(2,1)} %param.19) | copy-start | bytes 6291460
  194.5 352.5 %all-reduce.7.cloned.1.call-start = ((), (), s32[]{:S(2)}) async-start(), calls=%async_computation.1 | async-start | bytes 20971520 | tf_op jit(solution)/shard_map/psum | solution.py:1616
  336.8 30.9 %copy-start.3 = (s32[2560]{0:T(1024)S(1)}, s32[2560]{0:T(1024)}, u32[]{:S(2)}) copy-start(s32[2560]{0:T(1024)} %copy-done.2) | copy-start | bytes 30724
  336.8 31.3 %copy-start.5 = (f32[1,2048]{1,0:T(1,128)S(1)}, f32[1,2048]{1,0:T(1,128)}, u32[]{:S(2)}) copy-start(f32[1,2048]{1,0:T(1,128)} %get-tuple-element.79) | copy-start | bytes 24580
Sparse Core Ops, SparseCore 0:
  194.6 99.3 all-reduce.4
  336.9 210.0 all-reduce.6

commit v8 on v7

--- a/solution.py
+++ b/solution.py
@@ -15,7 +15,7 @@
 line_chunks = 16
 tail_columns = 256
 tail_subs = 4
-tail_lag = 2
+tail_lag = 3
 line_lag = 2
 sum_lag = 2
 gelu_scale = 0.7978845608028654

time: 588 us -> 611 us (1.039)
  Pallas kernels: 524 us -> 546 us
    pallas_call x1, Pallas kernels: 177 us -> 198 us  [tail_sums(): pl.pallas_call(functools.partial(tail_kernel, line_axis, count, subs, cub...]
  transfers between devices with their start and end apart: 2 -> 2, of which waited for: 1 -> 0; matrix products, arithmetic and copies ran while one was open for 1% -> 1% of each run, Pallas kernels for 59% -> 60%
where the time goes in v8:
time: 611 us; the launch traced here: 602 us
  Pallas kernels  546 us (89%)
  matrix products  32.1 us (5%)
  between operations  14.5 us (2%)
    pallas_call x1, Pallas kernels, tail_sums(): pl.pallas_call(functools.partial(tail_kernel, line_axis, count, subs, cub...  198 us
    pallas_call x1, Pallas kernels, leave_ffn(): pl.pallas_call(functools.partial(leave_kernel, axis, count, chunks), out_...  119 us
    pallas_call x1, Pallas kernels, enter_ffn(): pl.pallas_call(functools.partial(enter_kernel, axis, count, chunks), out_...  112 us
    pallas_call x1, Pallas kernels, attend_back(): pl.pallas_call(functools.partial(backward_kernel, block_count), out_shape...  29.9 us
    pallas_call x1, Pallas kernels, widen(): pl.pallas_call(lambda base, *refs: widen_kernel(*refs), out_shape=(jax.Sh...  27.2 us
    pallas_call x1, Pallas kernels, attend(): pl.pallas_call(functools.partial(forward_kernel, block_count), out_shape=...  22.9 us
    pallas_call x1, Pallas kernels, ffn_hidden(): pl.pallas_call(hidden_kernel, out_shape=[jax.ShapeDtypeStruct((tokens, wi...  20.1 us
    pallas_call x1, Pallas kernels, ffn_back(): pl.pallas_call(ffn_back_kernel, out_shape=jax.ShapeDtypeStruct((tokens, d...  16.4 us
  transfers between devices with their start and end apart: 2, of which 0 were waited for; matrix products, arithmetic and copies ran while one was open for 1% of the time, Pallas kernels for 60%

profile of v8, /device:TPU:17, one launch (start us, length us, event | category | flops | bytes accessed | tf_op | source)
XLA Modules:
  0.0 602.5 jit_solution(16637114949039328379)
XLA Ops:
  7.2 0.0 copy-start.4
  7.2 0.0 all-reduce.5.cloned.1.call-start
  7.2 0.0 copy-start
  7.3 3.2 fusion
  10.5 0.0 copy-done.4
  10.5 0.2 copy-done
  10.7 0.0 copy-start.9
  10.7 1.0 fusion.2.first_hbm
  11.7 0.6 copy-done.9
  12.3 0.0 copy-start.1
  12.3 0.0 copy-start.10
  12.3 3.3 fusion.3.q_ref
  15.6 0.0 copy-done.10
  15.6 0.0 copy-start.11
  15.6 3.3 fusion.4.k_ref
  18.9 0.0 copy-done.1
  18.9 0.0 copy-done.11
  18.9 0.0 copy-start.7
  18.9 0.0 copy-start.6
  18.9 3.3 fusion.5.v_ref
  22.2 0.1 subtract_abs_fusion
  22.3 0.0 copy-done.7
  22.3 0.0 copy-start.2
  22.3 0.2 fusion.8
  22.6 0.7 copy.26.line_ref
  23.3 0.0 copy-done.2
  23.3 0.0 copy-done.6
  23.3 0.9 compare_convert_fusion.q_code_ref
  24.2 0.0 copy-start.8
  24.2 22.9 %attend.1 = (bf16[1,1024,512]{2,1,0:T(8,128)(2,1)}, f32[1,4,2,1024]{3,2,1,0:T(2,128)}) custom-call(s32[1,1024]{1,0:T(1,128)} %seg_ref.3, bf16[1,1024,512]{2,1,0:T(8,128)(2,1)} %fusion.3.q_ref, bf16[1,1024,512]{2,1,0:T(8,128)(2,1)} %fusion.4.k_ref, bf16[1,1024,512]{2,1,0:T(8,128)(2,1)} %fusion.5.v_ref, bf16[1,1024,128]{2,1,0:T(8,128)(2,1)} %compare_convert_fusion.q_code_ref, ...), custom_call_target="tpu_custom_call" | custom-call | flops 24999999488 | bytes 1000000 | tf_op jit(solution)/shard_map/attend/pallas_call | solution.py:307
  47.1 0.0 copy-done.8
  47.1 5.6 convolution_convert_fusion.1.part_hbm
  52.7 111.7 %enter_ffn.1 = (bf16[1024,2048]{1,0:T(8,128)(2,1)}, bf16[1024,2048]{1,0:T(8,128)(2,1)}, f32[1024,1280]{1,0:T(8,128)}, bf16[2048,1024]{1,0:T(8,128)(2,1)}, bf16[512,1024]{1,0:T(8,128)(2,1)}) custom-call(bf16[1024,2048]{1,0:T(8,128)(2,1)} %convolution_convert_fusion.1.part_hbm, bf16[1024,2048]{1,0:T(8,128)(2,1)} %bitcast.48, bf16[1024,2048]{1,0:T(8,128)(2,1)} %bitcast.57, ...), custom_call_target="tpu_custom_call" | custom-call | flops 109999996928 | bytes 1000000 | tf_op jit(solution)/shard_map/enter_ffn/pallas_call | solution.py:973
  164.4 20.1 %ffn_hidden.1 = (bf16[1024,1280]{1,0:T(8,128)(2,1)}, bf16[1024,1280]{1,0:T(8,128)(2,1)}, bf16[1024,1280]{1,0:T(8,128)(2,1)}) custom-call(bf16[1024,2048]{1,0:T(8,128)(2,1)} %get-tuple-element.57.normed_ref.normed_hbm, bf16[2048,1280]{1,0:T(8,128)(2,1)} %w_gate_ref.3, bf16[2048,1280]{1,0:T(8,128)(2,1)} %w_up_ref.3, f32[1024,1280]{1,0:T(8,128)} %get-tuple-element.58.grad_ref), custom_call_target="tpu_custom_call" | custom-call | flops 20000000000 | bytes 1000000 | tf_op jit(solution)/shard_map/ffn_hidden/pallas_call | solution.py:1520
  184.5 9.9 %convolution_convert_fusion = bf16[1280,2048]{1,0:T(8,128)(2,1)} fusion(bf16[1024,1280]{1,0:T(8,128)(2,1)} %get-tuple-element.61.hidden_hbm, bf16[1,1024,2048]{2,1,0:T(8,128)(2,1)} %param.15), kind=kOutput, calls=%fused_computation.5 | convolution fusion | flops 5371330560 | bytes 12058624 | tf_op jit(solution)/shard_map/dot_general | solution.py:1605
  194.4 0.0 all-reduce.5.cloned.1.call-update
  194.5 0.0 all-reduce.7.cloned.1.call-start
  194.5 16.4 %ffn_back.1.part_hbm = bf16[1024,2048]{1,0:T(8,128)(2,1)} custom-call(bf16[1024,1280]{1,0:T(8,128)(2,1)} %get-tuple-element.62.gate_ref.gate_hbm, bf16[1024,1280]{1,0:T(8,128)(2,1)} %get-tuple-element.63.up_ref.up_hbm, bf16[2048,1280]{1,0:T(8,128)(2,1)} %w_gate_ref.3, bf16[2048,1280]{1,0:T(8,128)(2,1)} %w_up_ref.3), custom_call_target="tpu_custom_call" | custom-call | flops 16000000000 | bytes 1000000 | tf_op jit(solution)/shard_map/ffn_back/pallas_call | solution.py:1541
  210.9 119.5 %leave_ffn.1 = (bf16[1024,2048]{1,0:T(8,128)(2,1)}, bf16[1024,2048]{1,0:T(8,128)(2,1)}, bf16[2048,2560]{1,0:T(8,128)(2,1)}, f32[256,2048]{1,0:T(8,128)}, f32[1,2048]{1,0:T(1,128)}) custom-call(bf16[1024,2048]{1,0:T(8,128)(2,1)} %ffn_back.1.part_hbm, bf16[1024,2048]{1,0:T(8,128)(2,1)} %bitcast.49, bf16[1024,2048]{1,0:T(8,128)(2,1)} %get-tuple-element.64.attn_hbm.refs_7_, ...), custom_call_target="tpu_custom_call" | custom-call | flops 109999996928 | bytes 1000000 | tf_op jit(solution)/shard_map/leave_ffn/pallas_call | solution.py:1071
  330.4 0.0 all-reduce.5.cloned.1.call-done.refs_1_
  330.4 6.2 %fusion.6.grad_ref = bf16[1,1024,512]{2,1,0:T(8,128)(2,1)} fusion(bf16[1024,2048]{1,0:T(8,128)(2,1)} %get-tuple-element.70.branch_hbm, bf16[512,2048]{1,0:T(8,128)(2,1)} %param.19), kind=kOutput, calls=%fused_computation.14 | convolution fusion | flops 2148007936 | bytes 7340032 | tf_op jit(solution)/shard_map/dot_general | solution.py:51
  336.6 0.0 all-reduce.7.cloned.1.call-update
  336.6 0.0 copy-start.3
  336.6 0.0 copy-start.5
  336.6 29.9 %attend_back.1 = (bf16[1,1024,512]{2,1,0:T(8,128)(2,1)}, bf16[1,1024,512]{2,1,0:T(8,128)(2,1)}, bf16[1,1024,512]{2,1,0:T(8,128)(2,1)}, f32[1,8,5,512]{3,2,1,0:T(8,128)}) custom-call(s32[1,1024]{1,0:T(1,128)} %seg_ref.3, bf16[1,1024,512]{2,1,0:T(8,128)(2,1)} %fusion.3.q_ref, bf16[1,1024,512]{2,1,0:T(8,128)(2,1)} %fusion.4.k_ref, ...), custom_call_target="tpu_custom_call" | custom-call | flops 35000000512 | bytes 1000000 | tf_op jit(solution)/shard_map/attend_back/pallas_call | solution.py:335
  366.5 1.0 copy.31
  367.5 0.0 copy-done.3
  367.5 0.2 fusion.7
  367.8 0.1 reshape.214
  367.9 0.0 copy-done.5
  367.9 0.1 pad_maximum_fusion
  368.0 0.6 pad.9.small_ref
  368.6 198.1 %tail_sums.1 = (bf16[256,2048]{1,0:T(8,128)(2,1)}, bf16[256,2048]{1,0:T(8,128)(2,1)}, f32[8,2048]{1,0:T(8,128)}, f32[8,2048]{1,0:T(8,128)}, bf16[2048,512]{1,0:T...) custom-call(bf16[1024,512]{1,0:T(8,128)(2,1)} %bitcast.62, ...), custom_call_target="tpu_custom_call" | custom-call | flops 20000000000 | bytes 1000000 | tf_op jit(solution)/shard_map/tail_sums/pallas_call | solution.py:1333
  566.7 0.7 slice_reduce_fusion
  567.4 0.1 reshape_squeeze.3
  567.5 0.7 copy.29
  568.2 0.0 all-reduce.7.cloned.1.call-done.refs_0_
  568.2 27.2 %widen.1 = (f32[2048,1280]{1,0:T(8,128)}, f32[2048,1280]{1,0:T(8,128)}, f32[1280,2048]{1,0:T(8,128)}, f32[2048,512]{1,0:T(8,128)}, f32[2048,512]{1,0:T(8,128)}, ...) custom-call(s32[1]{0:T(128)} %bitcast.base, ...), custom_call_target="tpu_custom_call" | custom-call | flops 25999998976 | bytes 1000000 | tf_op jit(solution)/shard_map/widen/pallas_call | solution.py:1462
  (9 shorter events, 0.1 us)
Async XLA Ops:
  7.2 3.3 copy-start.4
  7.2 323.2 %all-reduce.5.cloned.1.call-start = ((), (), s32[]{:S(2)}) async-start(), calls=%async_computation | async-start | bytes 10485760 | tf_op jit(solution)/shard_map/psum | solution.py:1609
  7.2 3.5 copy-start
  10.7 1.6 copy-start.9
  12.3 6.6 %copy-start.1 = (bf16[1024,2048]{1,0:T(8,128)(2,1)}, bf16[1024,2048]{1,0:T(8,128)(2,1)S(1)}, u32[]{:S(2)}) copy-start(bf16[1024,2048]{1,0:T(8,128)(2,1)S(1)} %fusion.2.first_hbm) | copy-start | bytes 12582916
  12.3 3.3 copy-start.10
  15.6 3.3 copy-start.11
  18.9 3.4 copy-start.7
  18.9 4.4 copy-start.6
  22.3 0.9 copy-start.2
  24.2 22.9 %copy-start.8 = (bf16[512,2048]{1,0:T(8,128)(2,1)S(1)}, bf16[512,2048]{1,0:T(8,128)(2,1)}, u32[]{:S(2)}) copy-start(bf16[512,2048]{1,0:T(8,128)(2,1)} %param.19) | copy-start | bytes 6291460
  194.5 373.7 %all-reduce.7.cloned.1.call-start = ((), (), s32[]{:S(2)}) async-start(), calls=%async_computation.1 | async-start | bytes 20971520 | tf_op jit(solution)/shard_map/psum | solution.py:1616
  336.6 30.9 %copy-start.3 = (s32[2560]{0:T(1024)S(1)}, s32[2560]{0:T(1024)}, u32[]{:S(2)}) copy-start(s32[2560]{0:T(1024)} %copy-done.2) | copy-start | bytes 30724
  336.6 31.3 %copy-start.5 = (f32[1,2048]{1,0:T(1,128)S(1)}, f32[1,2048]{1,0:T(1,128)}, u32[]{:S(2)}) copy-start(f32[1,2048]{1,0:T(1,128)} %get-tuple-element.79) | copy-start | bytes 24580
Sparse Core Ops, SparseCore 0:
  194.6 100.2 all-reduce.4
  336.7 213.9 all-reduce.6
